TPU v7x, 128 devices: a whole 4x4x4 slice. The times are simulated.
128 devices in a mesh: pairs: 32 (over y, z, core), coup: 4 (over x).
Axes of the slice: x: 4, y: 4, z: 4, core: 2. Of those that a mesh axis runs over, the one named last changes fastest.
Arguments:
- coupling_list: int32 [3, 2048], P(None, 'pairs'), may hold values from 0 to 511, as said below
- pair_slot: int32 [128], replicated, may hold values from 0 to 127, as said below
- coupling_weight: float32 [2048], P('pairs'), may hold values from -1 to 1
- integrals: bfloat16 [128, 448, 448], P(('pairs', 'coup')), may hold values from -6 to 6
- orbital_energy: float32 [128, 448], P(('pairs', 'coup')), may hold values from 0.5 to 3
- pair_energy: float32 [128], P(('pairs', 'coup')), may hold values from 0.3 to 3
- intersections: bfloat16 [512, 448, 448], P(('pairs', 'coup')), may hold values from -0.25 to 0.25
Outputs:
- amplitudes: float32 [128, 448, 448], P(('pairs', 'coup'))
Inputs may be any that keep to these rules, and one draw needn't show every extreme that they name: `coupling_list`: row 0 and row 1 hold pair numbers, row 2 an intersection index. Positions g * 64 to (g + 1) * 64 - 1 form block g: its pairs i have rows (pair_slot) in g * 4 to (g + 1) * 4 - 1 and its intersection indices lie in g * 16 to (g + 1) * 16 - 1; for every h, exactly two couplings of block g have pair j with its row in h * 4 to (h + 1) * 4 - 1, and both name the same pair j. In each block at most 32 couplings have pair i with its row in the same 1 row of one device, and exactly 32 do for one such device. Likewise in each block at most 32 couplings have an intersection index among the same 4 indices of one device, and exactly 32 do for one such device. `pair_slot`: A permutation of the pairs.
All inputs are finite; a program needn't handle non-finite values.
Results may differ from a plain program's by a relative error of at most 0.0024.
Values may be sent and summed in bfloat16 or wider, within the bound.
No kernel may reach another device: no remote copies, remote signals or barrier semaphores. Data moves between devices by JAX's collectives and lax.ppermute only.
A program may use at most 128 MiB of HBM per device.

v0:
```python
import math

import jax
import jax.numpy as jnp
from jax import lax
from jax.sharding import Mesh
from jax.sharding import PartitionSpec as P

ITERS = 2
PAIRS = ("pairs_0", "pairs_1", "pairs_2")
PAIRS_COUP = ("pairs_0", "pairs_1", "pairs_2", "coup")


def in_blocks(x, dim, peers):
    before, after = (x.shape[:dim], x.shape[dim + 1 :])
    return jnp.moveaxis(x.reshape(*before, peers, -1, *after), dim, 0)


def in_order(tiles, dim):
    tiles = jnp.moveaxis(tiles, 0, dim)
    dims = tiles.shape
    return tiles.reshape(*dims[:dim], dims[dim] * dims[dim + 1], *dims[dim + 2 :])


def exchange_in_order(tiles, axes, order):
    dims = [lax.axis_size(a) for a in axes]
    tiles = tiles.reshape(*dims, *tiles.shape[1:])
    for k in order:
        tiles = lax.all_to_all(tiles, axes[k], split_axis=k, concat_axis=k, tiled=True)
    return tiles.reshape(-1, *tiles.shape[len(axes) :])


def two_step_exchange(x, groups, order, split_dim, concat_dim):
    peers = lax.axis_size(groups[0]) * lax.axis_size(groups[1])
    tiles = in_blocks(x, split_dim, peers)
    return in_order(exchange_in_order(tiles, groups, order), concat_dim)


def sum_at_owner(x, axis, dim):
    peers = lax.axis_size(axis)
    tiles = lax.all_to_all(in_blocks(x, dim, peers), axis, 0, 0, tiled=True)
    return jnp.sum(tiles, axis=0)


def lookup(lookup_table, queries):
    columns = lax.broadcasted_iota(jnp.int32, (queries.shape[0], lookup_table.shape[0]), 1)
    return jnp.sum(jnp.where(queries[:, None] == columns, lookup_table[None, :], 0), axis=1)


def compact(chosen, slot_count):
    order_rank = jnp.cumsum(chosen.astype(jnp.int32)) - 1
    target = lax.broadcasted_iota(jnp.int32, (slot_count, chosen.shape[0]), 0)
    return chosen[None, :] & (order_rank[None, :] == target)


def pick_values(selected, values):
    return jnp.sum(jnp.where(selected, values[None, :], jnp.zeros((), values.dtype)), axis=1)


def per_device(
    coupling_list, pair_slot, coupling_weight, integrals, orbital_energy, pair_energy, intersections
):
    group_total = lax.axis_size(PAIRS)
    coup_total = lax.axis_size("coup")
    group_index = lax.axis_index(PAIRS)
    member = lax.axis_index("coup")
    pair_dev = integrals.shape[0]
    ov_dev = intersections.shape[0]
    feature_width = integrals.shape[-1]
    group_pairs = pair_dev * coup_total
    group_couplings = coupling_list.shape[1]
    group_intersections = ov_dev * coup_total
    owner_row = lookup(pair_slot, coupling_list[0])
    reader_row = lookup(pair_slot, coupling_list[1])
    local_pair = owner_row - group_index * group_pairs
    source = reader_row // group_pairs
    read_pair = reader_row % group_pairs
    local_intersection = coupling_list[2] - group_index * group_intersections
    position = lax.iota(jnp.int32, group_couplings)
    ovl_table = lax.all_gather(intersections, "coup", axis=0, tiled=True)
    slot_count = group_couplings // coup_total
    assigned = position // slot_count == member
    row_offset = 0
    intersection_offset = 0
    selected = compact(assigned, slot_count)
    slot_source = pick_values(selected, source)
    slot_intersection = jnp.maximum(
        pick_values(selected, local_intersection) - intersection_offset, 0
    )
    slot_pair = pick_values(selected, local_pair) - row_offset
    slot_weight = pick_values(selected, coupling_weight)
    sources = lax.broadcasted_iota(jnp.int32, (group_total, group_couplings), 0)
    asked_for = source[None, :] == sources
    wanted_here = jnp.max(jnp.where(asked_for, read_pair[None, :], -1), axis=1)
    wanted = two_step_exchange(wanted_here, (("pairs_0", "pairs_1"), "pairs_2"), (1, 0), 0, 0)
    denominator = (
        orbital_energy[:, :, None] + orbital_energy[:, None, :] + pair_energy[:, None, None]
    )
    integral_f = integrals.astype(jnp.float32)
    amplitudes = -integral_f / denominator
    block_size = math.gcd(slot_count, 8)
    for iteration in range(ITERS):
        rounded = amplitudes.astype(jnp.bfloat16)
        strips = lax.all_to_all(rounded, "coup", split_axis=1, concat_axis=0, tiled=True)
        outgoing = jnp.take(strips, wanted, axis=0)
        arrived = lax.all_to_all(outgoing, PAIRS, split_axis=0, concat_axis=0, tiled=True)
        fetched = lax.all_gather(arrived, "coup", axis=1, tiled=True)

        def accumulate(block_turn, partial_value):
            first_slot = block_turn * block_size
            source_block = lax.dynamic_slice_in_dim(slot_source, first_slot, block_size)
            intersection_block = lax.dynamic_slice_in_dim(slot_intersection, first_slot, block_size)
            pair_block = lax.dynamic_slice_in_dim(slot_pair, first_slot, block_size)
            weight_block = lax.dynamic_slice_in_dim(slot_weight, first_slot, block_size)
            amp_block = jnp.take(fetched, source_block, axis=0)
            ovl_block = jnp.take(ovl_table, intersection_block, axis=0)
            left_product = jnp.einsum(
                "sab,sbc->sac", ovl_block, amp_block, preferred_element_type=jnp.float32
            ).astype(jnp.bfloat16)
            full_product = jnp.einsum(
                "sac,sdc->sad", left_product, ovl_block, preferred_element_type=jnp.float32
            )
            row_index = lax.broadcasted_iota(jnp.int32, (group_pairs, block_size), 0)
            spread = jnp.where(pair_block[None, :] == row_index, weight_block[None, :], 0.0)
            return partial_value + jnp.einsum(
                "ps,sad->pad", spread, full_product, precision=lax.Precision.HIGHEST
            )

        partial_value = lax.fori_loop(
            0,
            slot_count // block_size,
            accumulate,
            jnp.zeros((group_pairs, feature_width, feature_width), jnp.float32),
        )
        coupled = sum_at_owner(partial_value, "coup", 0)
        amplitudes = -(integral_f + coupled) / denominator
    return amplitudes


def solution(mesh):
    split = Mesh(
        mesh.devices.reshape(4, 4, 2, mesh.shape["coup"]), ("pairs_0", "pairs_1", "pairs_2", "coup")
    )
    in_specs = (
        P(None, PAIRS),
        P(),
        P(PAIRS),
        P(PAIRS_COUP, None, None),
        P(PAIRS_COUP, None),
        P(PAIRS_COUP),
        P(PAIRS_COUP, None, None),
    )
    out_specs = P(PAIRS_COUP, None, None)
    return jax.shard_map(
        per_device, mesh=split, in_specs=in_specs, out_specs=out_specs, check_vma=False
    )
```

profile of v0, /device:TPU:0, one launch (start us, length us, event | category | flops | bytes accessed | tf_op | source)
XLA Modules:
  0.0 719.8 jit_solution(7936679419225528113)
XLA Ops:
  6.5 0.7 all-gather.4.cloned.1.call-update
  7.3 0.8 subtract_bitcast_fusion
  8.1 0.8 select_reduce_fusion
  9.2 3.7 all_to_all.54
  13.6 8.2 %all-to-all-start.2 = ((s32[16,2,1]{1,2,0:T(1,128)}), s32[16,2,1]{1,2,0:T(1,128)S(1)}, u32[]{:S(2)}, u32[]{:S(2)}) async-start(s32[16,2,1]{1,2,0:T(1,128)} %copy.27), calls=%async_computation.2 | async-start | bytes 16384 | tf_op jit(solution)/shard_map/all_to_all | solution.py:29
  22.4 1.3 fusion.47
  23.7 0.7 copy.49
  24.9 3.5 reduce.8
  28.4 1.3 reshape.292
  29.7 4.3 all-to-all-start
  34.6 0.7 reduce.7
  35.4 12.0 %all-to-all-done = bf16[4,2,25088]{2,1,0:T(2,128)(2,1)S(1)} async-done(((bf16[4,2,25088]{2,1,0:T(2,128)(2,1)}), bf16[4,2,25088]{2,1,0:T(2,128)(2,1)S(1)}, u32[]{:S(2)}, u32[]{:S(2)}) %all-to-all-start) | async-done | bytes 401440 | tf_op jit(solution)/shard_map/all_to_all | solution.py:104
  48.2 2.6 gather_fusion.4
  50.8 2.5 broadcast_select_fusion.6
  53.3 52.2 %all_to_all.55 = bf16[32,112,448]{2,1,0:T(8,128)(2,1)} all-to-all(bf16[32,112,448]{2,1,0:T(8,128)(2,1)S(1)} %broadcast_select_fusion.6), channel_id=1, replica_groups=mesh['pairs_0'=4,'pairs_1'=4,'pairs_2'=2,'coup'=4] {'pairs_0','pairs_1',..., dimensions={0} | all-to-all | bytes 6422528 | tf_op jit(solution)/shard_map/all_to_all | solution.py:106
  106.4 131.8 %all-gather.6.cloned.1.call-done = bf16[32,448,448]{2,1,0:T(8,128)(2,1)} async-done(((bf16[32,112,448]{2,1,0:T(8,128)(2,1)}), bf16[32,448,448]{2,1,0:T(8,128)(2,1)}) %all-gather.6.cloned.1.call-update) | async-done | bytes 12845072 | tf_op jit(solution)/shard_map/all_gather | solution.py:107
  238.2 81.3 %while.28 = (s32[]{:T(128)}, f32[4,448,448]{2,0,1:T(4,128)}, s32[16]{0:T(128)S(1)}, f32[16]{0:T(128)S(1)}, s32[16]{0:T(128)S(1)}, /*index=5*/bf16[16,448,448]{2,...) while((s32[]{:T(128)}, f32[4,448,448]{2,0,1:T(4,128)}, ...), condition=%wide.region_9.13_spmd.clone, body=%wide.region_8.12_spmd.clone.sunk | while | flops 2962393088 | bytes 38544024 | solution.py:129
  238.3 7.8 %gather_fusion = bf16[8,448,448]{2,1,0:T(8,128)(2,1)} fusion(bf16[32,448,448]{2,1,0:T(8,128)(2,1)} %get-tuple-element.542, s32[1024]{0:T(1024)S(1)} %pad_clamp_fusion.9), kind=kCustom, calls=%fused_computation.2.clone.clone.1 | custom fusion | bytes 6422560 | tf_op jit(solution)/shard_map/while/body/eval_jaxpr/jit(_take)/gather | solution.py:115
  246.0 5.6 gather_fusion.1
  251.7 11.3 %fusion.74 = f32[8,448,448]{2,1,0:T(8,128)} fusion(bf16[8,448,448]{2,1,0:T(8,128)(2,1)} %gather_fusion, pred[8]{0:T(512)(128)(4,1)S(1)} %get-tuple-element.496, bf16[8,448,448]{2,1,0:T(8,128)(2,1)} %gather_fusion.1, pred[8]{0:T(512)(128)(4,1)S(1)} %get-tuple-element.498), kind=kOutput, calls=%fused_computation.11.clone.1 | convolution fusion | flops 2883715072 | bytes 12845072 | tf_op jit(solution)/shard_map/while/body/eval_jaxpr/sac,sdc->sad/dot_general | solution.py:120
  263.1 15.4 %select_add_fusion.4 = f32[4,448,448]{2,0,1:T(4,128)} fusion(f32[4,448,448]{2,0,1:T(4,128)} %get-tuple-element.524, f32[8,448,448]{2,1,0:T(8,128)} %fusion.74, pred[]{:T(512)S(6)} %compare.23, f32[8]{0:T(128)S(1)} %dynamic_slice.76, s32[8]{0:T(128)S(1)} %dynamic_slice.77), kind=kOutput, calls=%fused_computation.10.clone.1 | convolution fusion | flops 78676032 | bytes 12845121 | tf_op jit(solution)/shard_map/while/body/eval_jaxpr/ps,sad->pad/dot_general | solution.py:125
  278.6 7.8 %gather_fusion = bf16[8,448,448]{2,1,0:T(8,128)(2,1)} fusion(bf16[32,448,448]{2,1,0:T(8,128)(2,1)} %get-tuple-element.542, s32[1024]{0:T(1024)S(1)} %pad_clamp_fusion.9), kind=kCustom, calls=%fused_computation.2.clone.clone.1 | custom fusion | bytes 6422560 | tf_op jit(solution)/shard_map/while/body/eval_jaxpr/jit(_take)/gather | solution.py:115
  286.4 5.6 gather_fusion.1
  292.0 11.3 %fusion.74 = f32[8,448,448]{2,1,0:T(8,128)} fusion(bf16[8,448,448]{2,1,0:T(8,128)(2,1)} %gather_fusion, pred[8]{0:T(512)(128)(4,1)S(1)} %get-tuple-element.496, bf16[8,448,448]{2,1,0:T(8,128)(2,1)} %gather_fusion.1, pred[8]{0:T(512)(128)(4,1)S(1)} %get-tuple-element.498), kind=kOutput, calls=%fused_computation.11.clone.1 | convolution fusion | flops 2883715072 | bytes 12845072 | tf_op jit(solution)/shard_map/while/body/eval_jaxpr/sac,sdc->sad/dot_general | solution.py:120
  303.4 16.0 %select_add_fusion.4 = f32[4,448,448]{2,0,1:T(4,128)} fusion(f32[4,448,448]{2,0,1:T(4,128)} %get-tuple-element.524, f32[8,448,448]{2,1,0:T(8,128)} %fusion.74, pred[]{:T(512)S(6)} %compare.23, f32[8]{0:T(128)S(1)} %dynamic_slice.76, s32[8]{0:T(128)S(1)} %dynamic_slice.77), kind=kOutput, calls=%fused_computation.10.clone.1 | convolution fusion | flops 78676032 | bytes 12845121 | tf_op jit(solution)/shard_map/while/body/eval_jaxpr/ps,sad->pad/dot_general | solution.py:125
  319.5 3.2 copy.47
  322.7 47.1 %all_to_all.56 = f32[4,1,448,448]{3,2,1,0:T(8,128)} all-to-all(f32[4,1,448,448]{3,2,1,0:T(8,128)S(1)} %bitcast.44), channel_id=1, replica_groups=mesh['pairs_0'=4,'pairs_1'=4,'pairs_2'=2,'coup'=4] {'coup'}, dimensions={0} | all-to-all | bytes 6422528 | tf_op jit(solution)/shard_map/all_to_all | solution.py:41
  369.8 2.6 reduce_sum.82
  372.7 0.7 copy.48
  373.4 3.5 reduce.9
  377.4 9.8 %all_to_all.57 = bf16[4,2,25088]{2,1,0:T(2,128)(2,1)S(1)} all-to-all(bf16[4,2,25088]{2,1,0:T(2,128)(2,1)S(1)} %reshape.294), channel_id=1, replica_groups=mesh['pairs_0'=4,'pairs_1'=4,'pairs_2'=2,'coup'=4] {'coup'}, dimensions={0} | all-to-all | bytes 802816 | tf_op jit(solution)/shard_map/all_to_all | solution.py:104
  388.0 2.6 gather_fusion.5
  390.6 2.4 broadcast_select_fusion.7
  393.0 52.0 %all_to_all.58 = bf16[32,112,448]{2,1,0:T(8,128)(2,1)} all-to-all(bf16[32,112,448]{2,1,0:T(8,128)(2,1)S(1)} %broadcast_select_fusion.7), channel_id=1, replica_groups=mesh['pairs_0'=4,'pairs_1'=4,'pairs_2'=2,'coup'=4] {'pairs_0','pairs_1',..., dimensions={0} | all-to-all | bytes 6422528 | tf_op jit(solution)/shard_map/all_to_all | solution.py:106
  445.0 132.7 %all-gather.8.cloned.1.call-done = bf16[32,448,448]{2,1,0:T(8,128)(2,1)} async-done(((bf16[32,112,448]{2,1,0:T(8,128)(2,1)}), bf16[32,448,448]{2,1,0:T(8,128)(2,1)}) %all-gather.8.cloned.1.call-update) | async-done | bytes 12845072 | tf_op jit(solution)/shard_map/all_gather | solution.py:107
  577.7 81.3 %while.29 = (s32[]{:T(128)}, f32[4,448,448]{2,0,1:T(4,128)}, s32[16]{0:T(128)S(1)}, f32[16]{0:T(128)S(1)}, s32[16]{0:T(128)S(1)}, /*index=5*/bf16[16,448,448]{2,...) while((s32[]{:T(128)}, f32[4,448,448]{2,0,1:T(4,128)}, ...), condition=%wide.region_12.16_spmd.clone, body=%wide.region_11.15_spmd.clone.sunk | while | flops 2962393088 | bytes 38544024 | solution.py:129
  577.8 7.8 %gather_fusion.2 = bf16[8,448,448]{2,1,0:T(8,128)(2,1)} fusion(bf16[32,448,448]{2,1,0:T(8,128)(2,1)} %get-tuple-element.578, s32[1024]{0:T(1024)S(1)} %pad_clamp_fusion.11), kind=kCustom, calls=%fused_computation.5.clone.clone.1 | custom fusion | bytes 6422560 | tf_op jit(solution)/shard_map/while/body/eval_jaxpr/jit(_take)/gather | solution.py:115
  585.6 5.6 gather_fusion.3
  591.2 11.3 %fusion.79 = f32[8,448,448]{2,1,0:T(8,128)} fusion(bf16[8,448,448]{2,1,0:T(8,128)(2,1)} %gather_fusion.2, pred[8]{0:T(512)(128)(4,1)S(1)} %get-tuple-element.508, bf16[8,448,448]{2,1,0:T(8,128)(2,1)} %gather_fusion.3, pred[8]{0:T(512)(128)(4,1)S(1)} %get-tuple-element.510), kind=kOutput, calls=%fused_computation.35.clone.1 | convolution fusion | flops 2883715072 | bytes 12845072 | tf_op jit(solution)/shard_map/while/body/eval_jaxpr/sac,sdc->sad/dot_general | solution.py:120
  602.6 15.4 %select_add_fusion.5 = f32[4,448,448]{2,0,1:T(4,128)} fusion(f32[4,448,448]{2,0,1:T(4,128)} %get-tuple-element.560, f32[8,448,448]{2,1,0:T(8,128)} %fusion.79, pred[]{:T(512)S(6)} %compare.24, f32[8]{0:T(128)S(1)} %dynamic_slice.78, s32[8]{0:T(128)S(1)} %dynamic_slice.79), kind=kOutput, calls=%fused_computation.34.clone.1 | convolution fusion | flops 78676032 | bytes 12845121 | tf_op jit(solution)/shard_map/while/body/eval_jaxpr/ps,sad->pad/dot_general | solution.py:125
  618.2 7.8 %gather_fusion.2 = bf16[8,448,448]{2,1,0:T(8,128)(2,1)} fusion(bf16[32,448,448]{2,1,0:T(8,128)(2,1)} %get-tuple-element.578, s32[1024]{0:T(1024)S(1)} %pad_clamp_fusion.11), kind=kCustom, calls=%fused_computation.5.clone.clone.1 | custom fusion | bytes 6422560 | tf_op jit(solution)/shard_map/while/body/eval_jaxpr/jit(_take)/gather | solution.py:115
  625.9 5.6 gather_fusion.3
  631.6 11.3 %fusion.79 = f32[8,448,448]{2,1,0:T(8,128)} fusion(bf16[8,448,448]{2,1,0:T(8,128)(2,1)} %gather_fusion.2, pred[8]{0:T(512)(128)(4,1)S(1)} %get-tuple-element.508, bf16[8,448,448]{2,1,0:T(8,128)(2,1)} %gather_fusion.3, pred[8]{0:T(512)(128)(4,1)S(1)} %get-tuple-element.510), kind=kOutput, calls=%fused_computation.35.clone.1 | convolution fusion | flops 2883715072 | bytes 12845072 | tf_op jit(solution)/shard_map/while/body/eval_jaxpr/sac,sdc->sad/dot_general | solution.py:120
  643.0 16.0 %select_add_fusion.5 = f32[4,448,448]{2,0,1:T(4,128)} fusion(f32[4,448,448]{2,0,1:T(4,128)} %get-tuple-element.560, f32[8,448,448]{2,1,0:T(8,128)} %fusion.79, pred[]{:T(512)S(6)} %compare.24, f32[8]{0:T(128)S(1)} %dynamic_slice.78, s32[8]{0:T(128)S(1)} %dynamic_slice.79), kind=kOutput, calls=%fused_computation.34.clone.1 | convolution fusion | flops 78676032 | bytes 12845121 | tf_op jit(solution)/shard_map/while/body/eval_jaxpr/ps,sad->pad/dot_general | solution.py:125
  659.0 3.2 copy.46
  662.2 46.9 %all_to_all.59 = f32[4,1,448,448]{3,2,1,0:T(8,128)} all-to-all(f32[4,1,448,448]{3,2,1,0:T(8,128)S(1)} %bitcast.45), channel_id=1, replica_groups=mesh['pairs_0'=4,'pairs_1'=4,'pairs_2'=2,'coup'=4] {'coup'}, dimensions={0} | all-to-all | bytes 6422528 | tf_op jit(solution)/shard_map/all_to_all | solution.py:41
  709.1 2.6 reduce_sum.84
  711.7 1.2 fusion.52
  (59 shorter events, 6.3 us)
Async XLA Ops:
  6.5 99.9 %all-gather.4.cloned.1.call-start = ((), (), s32[]{:S(2)}) async-start(), calls=%async_computation.8 | async-start | bytes 9175040 | tf_op jit(solution)/shard_map/all_gather | solution.py:80
  13.6 16.1 %all-to-all-start.2 = ((s32[16,2,1]{1,2,0:T(1,128)}), s32[16,2,1]{1,2,0:T(1,128)S(1)}, u32[]{:S(2)}, u32[]{:S(2)}) async-start(s32[16,2,1]{1,2,0:T(1,128)} %copy.27), calls=%async_computation.2 | async-start | bytes 16384 | tf_op jit(solution)/shard_map/all_to_all | solution.py:29
  29.7 17.8 %all-to-all-start = ((bf16[4,2,25088]{2,1,0:T(2,128)(2,1)}), bf16[4,2,25088]{2,1,0:T(2,128)(2,1)S(1)}, u32[]{:S(2)}, u32[]{:S(2)}) async-start(bf16[4,2,25088]{2,1,0:T(2,128)(2,1)} %reshape.292), calls=%async_computation | async-start | bytes 802816 | tf_op jit(solution)/shard_map/all_to_all | solution.py:104
  34.0 204.2 %all-gather.6.cloned.1.call-start = ((), (), s32[]{:S(2)}) async-start(), calls=%async_computation.9 | async-start | bytes 18350080 | tf_op jit(solution)/shard_map/all_gather | solution.py:107
  105.5 0.7 copy-start.2
  105.5 472.3 %all-gather.8.cloned.1.call-start = ((), (), s32[]{:S(2)}) async-start(), calls=%async_computation.10 | async-start | bytes 18350080 | tf_op jit(solution)/shard_map/all_gather | solution.py:107
  369.8 2.6 copy-start
  369.8 2.6 copy-start.1
Sparse Core Ops, SparseCore 0:
  9.0 81.0 all-gather.3
  105.6 132.5 all-gather.5
  445.2 132.5 all-gather.7
where the time goes:
time: 726 us; the launch traced here: 720 us
  waiting for transfers between devices  277 us (38%)
  blocking collectives  212 us (29%)
  matrix products  108 us (15%)
  local copies, waits for them, and re-layouts  72.7 us (10%)
  other arithmetic  23.2 us (3%)
  between operations  14.4 us (2%)
  starting transfers between devices  12.7 us (2%)
    all_gather x2, waiting for transfers between devices, per_device(): fetched = lax.all_gather(arrived, 'coup', axis=1, tiled=True)  264 us
    all_to_all x2, blocking collectives, per_device(): lax.all_to_all(outgoing, PAIRS, split_axis=0, concat_axis=0, tiled=True)  104 us
    all_to_all x2, blocking collectives, sum_at_owner(): tiles = lax.all_to_all(in_blocks(x, dim, peers), axis, 0, 0, tiled=True)  94 us
    dot_general x4, matrix products, accumulate(): jnp.einsum('ps,sad->pad', spread, full_product, precision=lax.Precision.H...  62.9 us
    dot_general x4, matrix products, accumulate(): jnp.einsum('sac,sdc->sad', left_product, ovl_block, preferred_element_typ...  45.1 us
    gather x4, local copies, waits for them, and re-layouts, accumulate(): amp_block = jnp.take(fetched, source_block, axis=0)  31 us
    gather x4, local copies, waits for them, and re-layouts, accumulate(): ovl_block = jnp.take(ovl_table, intersection_block, axis=0)  22.6 us
  transfers between devices with their start and end apart: 5, of which 3 were waited for; matrix products, arithmetic and copies ran while one was open for 2% of the time, Pallas kernels for 0%

commit v1 on v0

v1 whole, which is shorter than its diff:
```python
import functools

import jax
import jax.numpy as jnp
from jax import lax
from jax.experimental import pallas as pl
from jax.experimental.pallas import tpu as pltpu
from jax.sharding import Mesh
from jax.sharding import PartitionSpec as P


ITERS = 2
PAIRS = ("pairs_0", "pairs_1", "pairs_2")
PAIRS_COUP = ("pairs_0", "pairs_1", "pairs_2", "coup")


def lookup(lookup_table, queries):
    columns = lax.broadcasted_iota(jnp.int32, (queries.shape[0], lookup_table.shape[0]), 1)
    return jnp.sum(jnp.where(queries[:, None] == columns, lookup_table[None, :], 0), axis=1)


def shift(x, step):
    peers = lax.axis_size("coup")
    return lax.ppermute(x, "coup", [(i, (i + step) % peers) for i in range(peers)])


def exchange_wanted(wanted_here):
    tiles = wanted_here.reshape(16, 2, 1)
    tiles = lax.all_to_all(tiles, "pairs_2", 1, 1, tiled=True)
    tiles = lax.all_to_all(tiles, ("pairs_0", "pairs_1"), 0, 0, tiled=True)
    return tiles.reshape(32)


def couple_kernel(
    slices, sched, weights, t_hbm, o_own, o_next, o_far_a, o_far_b, o_last, kept, out_1, out_2, out_3,
    acc, t_buf, o_buf, even_0, even_1, odd_0, odd_1, t_sems, o_sems,
):
    sources, strip = t_buf.shape[0], t_buf.shape[1]
    count = 2 * sources
    offset = pl.multiple_of(sched[2 * count], 16)
    lane = pl.multiple_of(sched[2 * count + 1], 128)
    member = sched[2 * count + 2]
    copies, first = [], 0
    for i, piece in enumerate((o_own, o_next, o_far_a, o_far_b, o_last)):
        size = piece.shape[0]
        copies.append(pltpu.make_async_copy(piece, o_buf.at[pl.ds(first, size)], o_sems.at[i]))
        first += size
    copies.append(pltpu.make_async_copy(t_hbm, t_buf, t_sems.at[0]))
    for copy in copies:
        copy.start()
    for ref in (acc, even_0, even_1, odd_0, odd_1):
        ref[...] = jnp.zeros_like(ref)
    for copy in copies:
        copy.wait()

    def right(h, s, ref):
        product = lax.dot_general(
            t_buf[h], o_buf[sched[2 * h + s]], (((1,), (1,)), ((), ())), preferred_element_type=jnp.float32
        )
        ref[pl.ds(offset, strip), :] = product.astype(jnp.bfloat16)

    def left(h, s, ref):
        k = 2 * h + s
        product = jnp.dot(
            o_buf[sched[k], :, pl.ds(lane, 256)], ref[...], preferred_element_type=jnp.float32
        )
        acc[sched[count + k]] += weights[k] * product

    right(0, 0, even_0)
    right(0, 1, even_1)

    def step(i, carry):
        h = 2 * i
        right(h + 1, 0, odd_0)
        left(h, 0, even_0)
        right(h + 1, 1, odd_1)
        left(h, 1, even_1)
        after = jnp.minimum(h + 2, sources - 1)
        right(after, 0, even_0)
        left(h + 1, 0, odd_0)
        right(after, 1, even_1)
        left(h + 1, 1, odd_1)
        return carry

    lax.fori_loop(0, sources // 2, step, 0)
    members = acc.shape[0]
    for d, out in enumerate((kept, out_1, out_2, out_3)):
        peer = lax.rem(member + d, members)
        if slices:
            rows = pl.ds(pl.multiple_of(peer * strip, 16), strip)
            for r in range(members):
                out[r] = acc[lax.rem(peer + r, members), rows, :].astype(out.dtype)
        else:
            out[...] = acc[peer].astype(out.dtype)


def couple(sched, weights, strips, pieces, coup, slices):
    _, strip, lanes = strips.shape
    width = pieces[0].shape[1]
    part = (coup, strip, width) if slices else (width, width)
    total = sum(piece.shape[0] for piece in pieces)
    whole = pl.BlockSpec(part, lambda i, *_: (0,) * len(part))
    half = pltpu.VMEM((256, width), jnp.bfloat16)
    return pl.pallas_call(
        functools.partial(couple_kernel, slices),
        out_shape=[jax.ShapeDtypeStruct(part, jnp.float32)] + [jax.ShapeDtypeStruct(part, jnp.bfloat16)] * 3,
        grid_spec=pltpu.PrefetchScalarGridSpec(
            num_scalar_prefetch=2,
            grid=(1,),
            in_specs=[pl.BlockSpec(memory_space=pl.ANY)] * (1 + len(pieces)),
            out_specs=[whole] * 4,
            scratch_shapes=[
                pltpu.VMEM((coup, width, width), jnp.float32),
                pltpu.VMEM(strips.shape, jnp.bfloat16),
                pltpu.VMEM((total, width, lanes), jnp.bfloat16),
                half, half, half, half,
                pltpu.SemaphoreType.DMA((1,)),
                pltpu.SemaphoreType.DMA((len(pieces),)),
            ],
        ),
        compiler_params=pltpu.CompilerParams(vmem_limit_bytes=60 * 2**20),
        name="couple_strips" if slices else "couple_pairs",
    )(sched, weights, strips, *pieces)


def sum_parts(kept, parts):
    for d, part in enumerate(parts):
        kept = kept + shift(part, d + 1).astype(jnp.float32)
    return kept


def amplitudes_of(
    coupling_list, pair_slot, coupling_weight, integrals, orbital_energy, pair_energy, intersections
):
    groups = lax.axis_size(PAIRS)
    coup = lax.axis_size("coup")
    group_index = lax.axis_index(PAIRS)
    member = lax.axis_index("coup")
    ov_dev, width = intersections.shape[0], integrals.shape[-1]
    count = coupling_list.shape[1]
    strip = width // coup
    lanes = -width % 128

    padded = jnp.pad(intersections, ((0, 0), (0, 0), (0, lanes)))
    half = ov_dev // 2
    o_next, o_last = shift(padded, -1), shift(padded, 1)
    far_a, far_b = shift(o_last[:half], 1), shift(o_next[half:], -1)
    pieces = (padded, o_next, far_a, far_b, o_last)

    owner_row = lookup(pair_slot, coupling_list[0]) - group_index * coup
    reader_row = lookup(pair_slot, coupling_list[1])
    source, read_pair = reader_row // coup, reader_row % coup
    local_o = coupling_list[2] - group_index * (ov_dev * coup)
    local_o = (local_o - member * ov_dev) % (ov_dev * coup)
    position = lax.iota(jnp.int32, count)
    twin = jnp.max(
        jnp.where((source[None, :] == source[:, None]) & (position[None, :] < position[:, None]), 1, 0), axis=1
    )
    slot = 2 * source + twin
    chosen = slot[None, :] == position[:, None]
    pick = lambda v: jnp.sum(jnp.where(chosen, v[None, :], jnp.zeros((), v.dtype)), axis=1)
    strip_row = member * strip
    lane_tile = jnp.minimum(strip_row // 128, 2) * 128
    sched = jnp.concatenate(
        [pick(local_o), pick(owner_row), jnp.stack([strip_row - lane_tile, lane_tile, member])]
    ).astype(jnp.int32)
    weights = pick(coupling_weight)
    asked = source[None, :] == lax.broadcasted_iota(jnp.int32, (groups, count), 0)
    wanted = exchange_wanted(jnp.max(jnp.where(asked, read_pair[None, :], 0), axis=1))

    flipped = jnp.pad(jnp.transpose(integrals[0]), ((0, 0), (0, lanes)))
    rows_of = lambda d: lax.dynamic_slice_in_dim(flipped, lax.rem(member + d, coup) * strip, strip)
    sent = [shift(rows_of(coup - e), coup - e) for e in range(1, coup)]
    integral_strips = jnp.stack([rows_of(0)] + sent)
    energies = jnp.concatenate([orbital_energy[0], pair_energy])[None]
    energies = jnp.concatenate([energies] + [shift(energies, -e) for e in range(1, coup)])
    orbital, pair = energies[:, :width], energies[:, width]
    own_rows = lax.dynamic_slice_in_dim(orbital, strip_row, strip, axis=1)
    all_columns = jnp.pad(orbital, ((0, 0), (0, lanes)))
    strip_denominator = own_rows[:, :, None] + all_columns[:, None, :] + pair[:, None, None]
    integral_f = integral_strips.astype(jnp.float32)
    amplitudes = -integral_f / strip_denominator
    wanted = (wanted - member) % coup

    for iteration in range(ITERS):
        rounded = amplitudes.astype(jnp.bfloat16)
        outgoing = rounded.at[wanted].get(mode="promise_in_bounds")
        arrived = lax.all_to_all(outgoing, PAIRS, 0, 0, tiled=True)
        last = iteration == ITERS - 1
        kept, *parts = couple(sched, weights, arrived, pieces, coup, not last)
        coupled = sum_parts(kept, parts)
        if not last:
            coupled = jnp.pad(coupled, ((0, 0), (0, 0), (0, lanes)))
            amplitudes = -(integral_f + coupled) / strip_denominator
    denominator = orbital_energy[:, :, None] + orbital_energy[:, None, :] + pair_energy[:, None, None]
    return -(integrals.astype(jnp.float32) + jnp.transpose(coupled)[None]) / denominator


def solution(mesh):
    split = Mesh(
        mesh.devices.reshape(4, 4, 2, mesh.shape["coup"]), ("pairs_0", "pairs_1", "pairs_2", "coup")
    )
    in_specs = (
        P(None, PAIRS),
        P(),
        P(PAIRS),
        P(PAIRS_COUP, None, None),
        P(PAIRS_COUP, None),
        P(PAIRS_COUP),
        P(PAIRS_COUP, None, None),
    )
    return jax.shard_map(
        amplitudes_of, mesh=split, in_specs=in_specs, out_specs=P(PAIRS_COUP, None, None), check_vma=False
    )
```

time: 726 us -> 276 us (0.38)
  waiting for transfers between devices: 277 us -> 103 us
  blocking collectives: 212 us -> 55.8 us
  matrix products: 108 us -> 0 us
  local copies, waits for them, and re-layouts: 72.7 us -> 16 us
  Pallas kernels: 0 us -> 48.7 us
  starting transfers between devices: 12.7 us -> 38.1 us
  between operations: 14.4 us -> 0.91 us
  other arithmetic: 23.2 us -> 11.8 us
    all_gather x3 -> x0, waiting for transfers between devices: 264 us -> none  [the longest x2 264 us: per_device(): fetched = lax.all_gather(arrived, 'coup', axis=1, tiled=True)]
    all_to_all x6 -> x2, blocking collectives: 212 us -> 55.8 us  [the longest x1 52.1 us: amplitudes_of(): arrived = lax.all_to_all(outgoing, PAIRS, 0, 0, tiled=True)]
    dot_general x8 -> x0, matrix products: 108 us -> none  [the longest x4 62.9 us: accumulate(): jnp.einsum('ps,sad->pad', spread, full_product, precision=lax.Precision.H...]
    ppermute x0 -> x16, waiting for transfers between devices: none -> 95.9 us  [shift(): lax.ppermute(x, 'coup', [(i, (i + step) % peers) for i in range(peers)])]
    gather x10 -> x2, local copies, waits for them, and re-layouts: 58.8 us -> 5.37 us  [amplitudes_of(): outgoing = rounded.at[wanted].get(mode='promise_in_bounds')]
    pallas_call x0 -> x2, Pallas kernels: none -> 48.7 us  [couple(): pl.pallas_call(functools.partial(couple_kernel, slices), out_shape=[jax.S...]
    ppermute x0 -> x16, starting transfers between devices: none -> 25.2 us  [shift(): lax.ppermute(x, 'coup', [(i, (i + step) % peers) for i in range(peers)])]
  transfers between devices with their start and end apart: 5 -> 18, of which waited for: 3 -> 9; matrix products, arithmetic and copies ran while one was open for 2% -> 5% of each run, Pallas kernels for 0% -> 0%
where the time goes in v1:
time: 276 us; the launch traced here: 275 us
  waiting for transfers between devices  103 us (37%)
  blocking collectives  55.8 us (20%)
  Pallas kernels  48.7 us (18%)
  starting transfers between devices  38.1 us (14%)
  local copies, waits for them, and re-layouts  16 us (6%)
  other arithmetic  11.8 us (4%)
    ppermute x16, waiting for transfers between devices, shift(): lax.ppermute(x, 'coup', [(i, (i + step) % peers) for i in range(peers)])  95.9 us
    all_to_all x1, blocking collectives, amplitudes_of(): arrived = lax.all_to_all(outgoing, PAIRS, 0, 0, tiled=True)  52.1 us
    pallas_call x2, Pallas kernels, couple(): pl.pallas_call(functools.partial(couple_kernel, slices), out_shape=[jax.S...  48.7 us
    ppermute x16, starting transfers between devices, shift(): lax.ppermute(x, 'coup', [(i, (i + step) % peers) for i in range(peers)])  25.2 us
    all_to_all x1, starting transfers between devices, exchange_wanted(): tiles = lax.all_to_all(tiles, ('pairs_0', 'pairs_1'), 0, 0, tiled=True)  8.05 us
    all_to_all x1, waiting for transfers between devices, exchange_wanted(): tiles = lax.all_to_all(tiles, ('pairs_0', 'pairs_1'), 0, 0, tiled=True)  7.51 us
  transfers between devices with their start and end apart: 18, of which 9 were waited for; matrix products, arithmetic and copies ran while one was open for 5% of the time, Pallas kernels for 0%

profile of v1, /device:TPU:0, one launch (start us, length us, event | category | flops | bytes accessed | tf_op | source)
XLA Modules:
  0.0 274.5 jit_solution(12712260428254307704)
XLA Ops:
  0.7 0.8 pad_maximum_fusion.2
  1.4 2.9 %collective-permute-start.3 = (f32[1,449]{1,0:T(1,128)S(1)}, f32[1,449]{1,0:T(1,128)S(1)}, u32[]{:S(2)}, u32[]{:S(2)}) collective-permute-start(f32[1,449]{1,0:T(1,128)S(1)} %bitcast.43), channel_id=1, source_target_pairs={{0,3},{1,0},{2,1},{3,2},{4,7},{5,4},{6,5},{7,6},{8,11},{9,8},{10,9... | collective-permute-start | bytes 5396 | tf_op jit(solution)/shard_map/ppermute | solution.py:24
  4.3 0.8 collective-permute-start.4
  5.1 0.9 collective-permute-start.5
  6.0 1.2 copy.24
  7.3 1.9 collective-permute-start.1
  9.2 1.4 collective-permute-start.2
  10.6 1.3 fusion.9
  11.9 0.8 select_reduce_fusion.2
  12.7 0.6 and_select_fusion.1
  13.9 3.7 %all_to_all.20 = s32[16,2,1]{0,2,1:T(1,128)S(1)} all-to-all(s32[16,2,1]{0,2,1:T(1,128)S(1)} %copy.26), channel_id=1, replica_groups=mesh['pairs_0'=4,'pairs_1'=4,'pairs_2'=2,'coup'=4] {'pairs_2'}, dimensions={1} | all-to-all | bytes 256 | tf_op jit(solution)/shard_map/all_to_all | solution.py:29
  17.6 0.7 copy.27
  18.3 8.0 %all-to-all-start.1 = ((s32[16,2,1]{1,2,0:T(1,128)}), s32[16,2,1]{1,2,0:T(1,128)S(1)}, u32[]{:S(2)}, u32[]{:S(2)}) async-start(s32[16,2,1]{1,2,0:T(1,128)} %copy.27), calls=%async_computation.1 | async-start | bytes 16384 | tf_op jit(solution)/shard_map/all_to_all | solution.py:30
  26.4 7.5 %all-to-all-done.1 = s32[16,2,1]{1,2,0:T(1,128)S(1)} async-done(((s32[16,2,1]{1,2,0:T(1,128)}), s32[16,2,1]{1,2,0:T(1,128)S(1)}, u32[]{:S(2)}, u32[]{:S(2)}) %all-to-all-start.1) | async-done | bytes 160 | tf_op jit(solution)/shard_map/all_to_all | solution.py:30
  34.1 1.9 collective-permute-start
  36.3 2.6 collective-permute-done
  39.2 2.6 gather_fusion
  41.8 4.9 %all-to-all-start.2 = ((bf16[32,112,512]{2,1,0:T(8,128)(2,1)}), bf16[32,112,512]{2,1,0:T(8,128)(2,1)}, u32[]{:S(2)}, u32[]{:S(2)}) async-start(bf16[32,112,512]{2,1,0:T(8,128)(2,1)} %gather_fusion), calls=%async_computation.2 | async-start | bytes 7340032 | tf_op jit(solution)/shard_map/all_to_all | solution.py:188
  46.7 1.7 pad.18.o_own
  48.4 0.7 collective-permute-start.7
  49.2 2.6 collective-permute-start.6
  51.7 40.1 %collective-permute-done.7.o_last = bf16[4,448,512]{2,1,0:T(8,128)(2,1)S(1)} collective-permute-done((bf16[4,448,512]{2,1,0:T(8,128)(2,1)S(1)}, bf16[4,448,512]{2,1,0:T(8,128)(2,1)S(1)}, u32[]{:S(2)}, u32[]{:S(2)}) %collective-permute-start.7) | collective-permute-done | bytes 1835040 | tf_op jit(solution)/shard_map/ppermute | solution.py:24
  91.9 1.0 slice.33
  92.9 0.5 copy-done.1
  93.4 1.1 slice.34
  94.9 2.7 collective-permute-start.9
  97.6 0.9 select_reduce_fusion.4
  98.6 0.7 multiply_add_fusion
  99.2 0.6 copy-done.14
  99.8 1.3 select_reduce_fusion.1
  101.1 1.3 concatenate.9.sched
  102.4 1.4 select_reduce_fusion.weights
  103.8 12.3 %collective-permute-done.8.o_far_a = bf16[2,448,512]{2,1,0:T(8,128)(2,1)S(1)} collective-permute-done((bf16[2,448,512]{2,1,0:T(8,128)(2,1)}, bf16[2,448,512]{2,1,0:T(8,128)(2,1)S(1)}, u32[]{:S(2)}, u32[]{:S(2)}) %collective-permute-start.8) | collective-permute-done | bytes 917536 | tf_op jit(solution)/shard_map/ppermute | solution.py:24
  116.1 0.9 collective-permute-done.9.o_far_b
  117.0 24.3 %couple_strips.1 = (f32[4,112,448]{2,1,0:T(8,128)}, bf16[4,112,448]{2,1,0:T(8,128)(2,1)}, bf16[4,112,448]{2,1,0:T(8,128)(2,1)}, bf16[4,112,448]{2,1,0:T(8,128)(2,1)}) custom-call(s32[131]{0:T(256)} %concatenate.9.sched, f32[64]{0:T(128)} %select_reduce_fusion.weights, bf16[32,112,512]{2,1,0:T(8,128)(2,1)} %all-to-all-done.2.t_hbm, ...), custom_call_target="tpu_custom_call" | custom-call | tf_op jit(solution)/shard_map/couple_strips/pallas_call | solution.py:104
  141.3 0.6 collective-permute-start.10
  141.9 4.8 %collective-permute-start.11 = (bf16[4,112,448]{2,1,0:T(8,128)(2,1)}, bf16[4,112,448]{2,1,0:T(8,128)(2,1)S(1)}, u32[]{:S(2)}, u32[]{:S(2)}) collective-permute-start(bf16[4,112,448]{2,1,0:T(8,128)(2,1)} %get-tuple-element.15), channel_id=1, source_target_pairs={{0,2},{1,3},{2,0},{3,1},{4,6},{5,7},{6,4},{7,5},{8,10},{9,11},{10,... | collective-permute-start | bytes 1204232 | tf_op jit(solution)/shard_map/ppermute | solution.py:24
  146.8 9.2 %collective-permute-done.10 = bf16[4,112,448]{2,1,0:T(8,128)(2,1)S(1)} collective-permute-done((bf16[4,112,448]{2,1,0:T(8,128)(2,1)}, bf16[4,112,448]{2,1,0:T(8,128)(2,1)S(1)}, u32[]{:S(2)}, u32[]{:S(2)}) %collective-permute-start.10) | collective-permute-done | bytes 401440 | tf_op jit(solution)/shard_map/ppermute | solution.py:24
  156.0 9.6 %collective-permute-done.11 = bf16[4,112,448]{2,1,0:T(8,128)(2,1)S(1)} collective-permute-done((bf16[4,112,448]{2,1,0:T(8,128)(2,1)}, bf16[4,112,448]{2,1,0:T(8,128)(2,1)S(1)}, u32[]{:S(2)}, u32[]{:S(2)}) %collective-permute-start.11) | collective-permute-done | bytes 401440 | tf_op jit(solution)/shard_map/ppermute | solution.py:24
  165.5 1.5 convert_add_fusion.1
  167.3 2.7 gather_fusion.1
  170.1 52.1 %all_to_all.21.t_hbm = bf16[32,112,512]{2,1,0:T(8,128)(2,1)} all-to-all(bf16[32,112,512]{2,1,0:T(8,128)(2,1)} %gather_fusion.1), channel_id=1, replica_groups=mesh['pairs_0'=4,'pairs_1'=4,'pairs_2'=2,'coup'=4] {'pairs_0','pairs_1',..., dimensions={0} | all-to-all | bytes 7340032 | tf_op jit(solution)/shard_map/all_to_all | solution.py:188
  222.2 24.3 %couple_pairs.1 = (f32[448,448]{1,0:T(8,128)}, bf16[448,448]{1,0:T(8,128)(2,1)}, bf16[448,448]{1,0:T(8,128)(2,1)}, bf16[448,448]{1,0:T(8,128)(2,1)}) custom-call(s32[131]{0:T(256)} %concatenate.9.sched, f32[64]{0:T(128)} %select_reduce_fusion.weights, bf16[32,112,512]{2,1,0:T(8,128)(2,1)} %all_to_all.21.t_hbm, bf16[4,448,512]{2,1,0:T(8,128)(2,1)} %copy-done, ...), custom_call_target="tpu_custom_call" | custom-call | tf_op jit(solution)/shard_map/couple_pairs/pallas_call | solution.py:104
  246.8 3.7 %collective-permute-start.14 = (bf16[448,448]{1,0:T(8,128)(2,1)}, bf16[448,448]{1,0:T(8,128)(2,1)S(1)}, u32[]{:S(2)}, u32[]{:S(2)}) collective-permute-start(bf16[448,448]{1,0:T(8,128)(2,1)} %get-tuple-element.19), channel_id=1, source_target_pairs={{0,2},{1,3},{2,0},{3,1},{4,6},{5,7},{6,4},{7,5},{8,10},{9,11},{10,... | collective-permute-start | bytes 1204232 | tf_op jit(solution)/shard_map/ppermute | solution.py:24
  250.5 10.8 %collective-permute-done.13 = bf16[448,448]{1,0:T(8,128)(2,1)S(1)} collective-permute-done((bf16[448,448]{1,0:T(8,128)(2,1)}, bf16[448,448]{1,0:T(8,128)(2,1)S(1)}, u32[]{:S(2)}, u32[]{:S(2)}) %collective-permute-start.13) | collective-permute-done | bytes 401440 | tf_op jit(solution)/shard_map/ppermute | solution.py:24
  261.2 10.4 %collective-permute-done.14 = bf16[448,448]{1,0:T(8,128)(2,1)S(1)} collective-permute-done((bf16[448,448]{1,0:T(8,128)(2,1)}, bf16[448,448]{1,0:T(8,128)(2,1)S(1)}, u32[]{:S(2)}, u32[]{:S(2)}) %collective-permute-start.14) | collective-permute-done | bytes 401440 | tf_op jit(solution)/shard_map/ppermute | solution.py:24
  271.7 1.6 fusion.6
  273.3 1.2 copy.28
  (57 shorter events, 2.5 us)
Async XLA Ops:
  1.4 32.6 %collective-permute-start.3 = (f32[1,449]{1,0:T(1,128)S(1)}, f32[1,449]{1,0:T(1,128)S(1)}, u32[]{:S(2)}, u32[]{:S(2)}) collective-permute-start(f32[1,449]{1,0:T(1,128)S(1)} %bitcast.43), channel_id=1, source_target_pairs={{0,3},{1,0},{2,1},{3,2},{4,7},{5,4},{6,5},{7,6},{8,11},{9,8},{10,9... | collective-permute-start | bytes 5396 | tf_op jit(solution)/shard_map/ppermute | solution.py:24
  4.3 31.7 %collective-permute-start.4 = (f32[1,449]{1,0:T(1,128)S(1)}, f32[1,449]{1,0:T(1,128)S(1)}, u32[]{:S(2)}, u32[]{:S(2)}) collective-permute-start(f32[1,449]{1,0:T(1,128)S(1)} %bitcast.44), channel_id=1, source_target_pairs={{0,2},{1,3},{2,0},{3,1},{4,6},{5,7},{6,4},{7,5},{8,10},{9,11},{10,... | collective-permute-start | bytes 5396 | tf_op jit(solution)/shard_map/ppermute | solution.py:24
  5.1 30.9 %collective-permute-start.5 = (f32[1,449]{1,0:T(1,128)S(1)}, f32[1,449]{1,0:T(1,128)S(1)}, u32[]{:S(2)}, u32[]{:S(2)}) collective-permute-start(f32[1,449]{1,0:T(1,128)S(1)} %bitcast.45), channel_id=1, source_target_pairs={{0,1},{1,2},{2,3},{3,0},{4,5},{5,6},{6,7},{7,4},{8,9},{9,10},{10,1... | collective-permute-start | bytes 5396 | tf_op jit(solution)/shard_map/ppermute | solution.py:24
  7.3 29.1 %collective-permute-start.1 = (bf16[112,512]{1,0:T(8,128)(2,1)S(1)}, bf16[112,512]{1,0:T(8,128)(2,1)S(1)}, u32[]{:S(2)}, u32[]{:S(2)}) collective-permute-start(bf16[112,512]{1,0:T(8,128)(2,1)S(1)} %get-tuple-element.27), channel_id=1, source_target_pairs={{0,2},{1,3},{2,0},{3,1},{4,6},{5,7},{6,4},{7,5},{8,10},{9,11},{10,... | collective-permute-start | bytes 344072 | tf_op jit(solution)/shard_map/ppermute | solution.py:24
  9.2 27.1 %collective-permute-start.2 = (bf16[112,512]{1,0:T(8,128)(2,1)S(1)}, bf16[112,512]{1,0:T(8,128)(2,1)S(1)}, u32[]{:S(2)}, u32[]{:S(2)}) collective-permute-start(bf16[112,512]{1,0:T(8,128)(2,1)S(1)} %get-tuple-element.28), channel_id=1, source_target_pairs={{0,1},{1,2},{2,3},{3,0},{4,5},{5,6},{6,7},{7,4},{8,9},{9,10},{10,1... | collective-permute-start | bytes 344072 | tf_op jit(solution)/shard_map/ppermute | solution.py:24
  13.3 0.6 copy-start.15
  18.3 15.6 %all-to-all-start.1 = ((s32[16,2,1]{1,2,0:T(1,128)}), s32[16,2,1]{1,2,0:T(1,128)S(1)}, u32[]{:S(2)}, u32[]{:S(2)}) async-start(s32[16,2,1]{1,2,0:T(1,128)} %copy.27), calls=%async_computation.1 | async-start | bytes 16384 | tf_op jit(solution)/shard_map/all_to_all | solution.py:30
  34.0 7.8 %copy-start.11 = (s32[1024]{0:T(1024)}, s32[1024]{0:T(1024)S(1)}, u32[]{:S(2)}) copy-start(s32[1024]{0:T(1024)S(1)} %pad_clamp_fusion) | copy-start | bytes 12292
  34.1 4.9 %collective-permute-start = (bf16[112,512]{1,0:T(8,128)(2,1)S(1)}, bf16[112,512]{1,0:T(8,128)(2,1)S(1)}, u32[]{:S(2)}, u32[]{:S(2)}) collective-permute-start(bf16[112,512]{1,0:T(8,128)(2,1)S(1)} %get-tuple-element.26), channel_id=1, source_target_pairs={{0,3},{1,0},{2,1},{3,2},{4,7},{5,4},{6,5},{7,6},{8,11},{9,8},{10,9... | collective-permute-start | bytes 344072 | tf_op jit(solution)/shard_map/ppermute | solution.py:24
  36.0 5.8 %copy-start.6 = (f32[4,512]{1,0:T(4,128)}, f32[4,512]{1,0:T(4,128)S(1)}, u32[]{:S(2)}) copy-start(f32[4,512]{1,0:T(4,128)S(1)} %pad.17) | copy-start | bytes 24580
  36.2 5.6 %copy-start.12 = (f32[4]{0:T(128)}, f32[4]{0:T(128)S(1)}, u32[]{:S(2)}) copy-start(f32[4]{0:T(128)S(1)} %maximum_reduce_fusion) | copy-start | bytes 52
  36.3 5.5 %copy-start.9 = (f32[4,112]{1,0:T(4,128)}, f32[4,112]{1,0:T(4,128)S(1)}, u32[]{:S(2)}) copy-start(f32[4,112]{1,0:T(4,128)S(1)} %constant_dynamic-slice_fusion) | copy-start | bytes 5380
  38.9 2.9 %copy-start.4 = (bf16[112,512]{1,0:T(8,128)(2,1)}, bf16[112,512]{1,0:T(8,128)(2,1)S(1)}, u32[]{:S(2)}) copy-start(bf16[112,512]{1,0:T(8,128)(2,1)S(1)} %collective-permute-done) | copy-start | bytes 344068
  41.8 75.1 %all-to-all-start.2 = ((bf16[32,112,512]{2,1,0:T(8,128)(2,1)}), bf16[32,112,512]{2,1,0:T(8,128)(2,1)}, u32[]{:S(2)}, u32[]{:S(2)}) async-start(bf16[32,112,512]{2,1,0:T(8,128)(2,1)} %gather_fusion), calls=%async_computation.2 | async-start | bytes 7340032 | tf_op jit(solution)/shard_map/all_to_all | solution.py:188
  48.4 68.5 %copy-start = (bf16[4,448,512]{2,1,0:T(8,128)(2,1)}, bf16[4,448,512]{2,1,0:T(8,128)(2,1)S(1)}, u32[]{:S(2)}) copy-start(bf16[4,448,512]{2,1,0:T(8,128)(2,1)S(1)} %pad.18.o_own) | copy-start | bytes 5505028
  48.4 43.4 %collective-permute-start.7 = (bf16[4,448,512]{2,1,0:T(8,128)(2,1)S(1)}, bf16[4,448,512]{2,1,0:T(8,128)(2,1)S(1)}, u32[]{:S(2)}, u32[]{:S(2)}) collective-permute-start(bf16[4,448,512]{2,1,0:T(8,128)(2,1)S(1)} %pad.18.o_own), channel_id=1, source_target_pairs={{0,1},{1,2},{2,3},{3,0},{4,5},{5,6},{6,7},{7,4},{8,9},{9,10},{10,1... | collective-permute-start | bytes 5505032 | tf_op jit(solution)/shard_map/ppermute | solution.py:24
  49.2 43.7 %collective-permute-start.6 = (bf16[4,448,512]{2,1,0:T(8,128)(2,1)S(1)}, bf16[4,448,512]{2,1,0:T(8,128)(2,1)S(1)}, u32[]{:S(2)}, u32[]{:S(2)}) collective-permute-start(bf16[4,448,512]{2,1,0:T(8,128)(2,1)S(1)} %pad.18.o_own), channel_id=1, source_target_pairs={{0,3},{1,0},{2,1},{3,2},{4,7},{5,4},{6,5},{7,6},{8,11},{9,8},{10,9... | collective-permute-start | bytes 5505032 | tf_op jit(solution)/shard_map/ppermute | solution.py:24
  91.9 1.5 copy-start.1
  92.9 23.2 %collective-permute-start.8 = (bf16[2,448,512]{2,1,0:T(8,128)(2,1)}, bf16[2,448,512]{2,1,0:T(8,128)(2,1)S(1)}, u32[]{:S(2)}, u32[]{:S(2)}) collective-permute-start(bf16[2,448,512]{2,1,0:T(8,128)(2,1)} %slice.33), channel_id=1, source_target_pairs={{0,1},{1,2},{2,3},{3,0},{4,5},{5,6},{6,7},{7,4},{8,9},{9,10},{10,1... | collective-permute-start | bytes 2752520 | tf_op jit(solution)/shard_map/ppermute | solution.py:24
  93.4 1.5 copy-start.2
  94.9 22.1 %collective-permute-start.9 = (bf16[2,448,512]{2,1,0:T(8,128)(2,1)}, bf16[2,448,512]{2,1,0:T(8,128)(2,1)}, u32[]{:S(2)}, u32[]{:S(2)}) collective-permute-start(bf16[2,448,512]{2,1,0:T(8,128)(2,1)} %slice.34), channel_id=1, source_target_pairs={{0,3},{1,0},{2,1},{3,2},{4,7},{5,4},{6,5},{7,6},{8,11},{9,8},{10,9... | collective-permute-start | bytes 2752520 | tf_op jit(solution)/shard_map/ppermute | solution.py:24
  99.2 0.6 copy-start.14
  116.1 0.9 copy-start.3
  117.0 50.0 %copy-start.5 = (bf16[112,512]{1,0:T(8,128)(2,1)S(1)}, bf16[112,512]{1,0:T(8,128)(2,1)}, u32[]{:S(2)}) copy-start(bf16[112,512]{1,0:T(8,128)(2,1)} %copy-done.4) | copy-start | bytes 344068
  117.0 50.0 %copy-start.7 = (f32[4,512]{1,0:T(4,128)S(1)}, f32[4,512]{1,0:T(4,128)}, u32[]{:S(2)}) copy-start(f32[4,512]{1,0:T(4,128)} %copy-done.6) | copy-start | bytes 24580
  117.0 50.0 %copy-start.10 = (f32[4,112]{1,0:T(4,128)S(1)}, f32[4,112]{1,0:T(4,128)}, u32[]{:S(2)}) copy-start(f32[4,112]{1,0:T(4,128)} %copy-done.9) | copy-start | bytes 5380
  117.0 50.0 %copy-start.13 = (f32[4]{0:T(128)S(1)}, f32[4]{0:T(128)}, u32[]{:S(2)}) copy-start(f32[4]{0:T(128)} %copy-done.12) | copy-start | bytes 52
  141.3 14.6 %collective-permute-start.10 = (bf16[4,112,448]{2,1,0:T(8,128)(2,1)}, bf16[4,112,448]{2,1,0:T(8,128)(2,1)S(1)}, u32[]{:S(2)}, u32[]{:S(2)}) collective-permute-start(bf16[4,112,448]{2,1,0:T(8,128)(2,1)} %get-tuple-element.14), channel_id=1, source_target_pairs={{0,1},{1,2},{2,3},{3,0},{4,5},{5,6},{6,7},{7,4},{8,9},{9,10},{10,1... | collective-permute-start | bytes 1204232 | tf_op jit(solution)/shard_map/ppermute | solution.py:24
  141.9 23.6 %collective-permute-start.11 = (bf16[4,112,448]{2,1,0:T(8,128)(2,1)}, bf16[4,112,448]{2,1,0:T(8,128)(2,1)S(1)}, u32[]{:S(2)}, u32[]{:S(2)}) collective-permute-start(bf16[4,112,448]{2,1,0:T(8,128)(2,1)} %get-tuple-element.15), channel_id=1, source_target_pairs={{0,2},{1,3},{2,0},{3,1},{4,6},{5,7},{6,4},{7,5},{8,10},{9,11},{10,... | collective-permute-start | bytes 1204232 | tf_op jit(solution)/shard_map/ppermute | solution.py:24
  146.7 18.8 %collective-permute-start.12 = (bf16[4,112,448]{2,1,0:T(8,128)(2,1)}, bf16[4,112,448]{2,1,0:T(8,128)(2,1)S(1)}, u32[]{:S(2)}, u32[]{:S(2)}) collective-permute-start(bf16[4,112,448]{2,1,0:T(8,128)(2,1)} %get-tuple-element.16), channel_id=1, source_target_pairs={{0,3},{1,0},{2,1},{3,2},{4,7},{5,4},{6,5},{7,6},{8,11},{9,8},{10,9... | collective-permute-start | bytes 1204232 | tf_op jit(solution)/shard_map/ppermute | solution.py:24
  222.2 49.5 %copy-start.8 = (f32[1,448]{1,0:T(1,128)S(1)}, f32[1,448]{1,0:T(1,128)}, u32[]{:S(2)}) copy-start(f32[1,448]{1,0:T(1,128)} %param.11) | copy-start | bytes 5380
  246.5 14.7 %collective-permute-start.13 = (bf16[448,448]{1,0:T(8,128)(2,1)}, bf16[448,448]{1,0:T(8,128)(2,1)S(1)}, u32[]{:S(2)}, u32[]{:S(2)}) collective-permute-start(bf16[448,448]{1,0:T(8,128)(2,1)} %get-tuple-element.18), channel_id=1, source_target_pairs={{0,1},{1,2},{2,3},{3,0},{4,5},{5,6},{6,7},{7,4},{8,9},{9,10},{10,1... | collective-permute-start | bytes 1204232 | tf_op jit(solution)/shard_map/ppermute | solution.py:24
  246.8 24.9 %collective-permute-start.14 = (bf16[448,448]{1,0:T(8,128)(2,1)}, bf16[448,448]{1,0:T(8,128)(2,1)S(1)}, u32[]{:S(2)}, u32[]{:S(2)}) collective-permute-start(bf16[448,448]{1,0:T(8,128)(2,1)} %get-tuple-element.19), channel_id=1, source_target_pairs={{0,2},{1,3},{2,0},{3,1},{4,6},{5,7},{6,4},{7,5},{8,10},{9,11},{10,... | collective-permute-start | bytes 1204232 | tf_op jit(solution)/shard_map/ppermute | solution.py:24
  250.4 21.2 %collective-permute-start.15 = (bf16[448,448]{1,0:T(8,128)(2,1)}, bf16[448,448]{1,0:T(8,128)(2,1)S(1)}, u32[]{:S(2)}, u32[]{:S(2)}) collective-permute-start(bf16[448,448]{1,0:T(8,128)(2,1)} %get-tuple-element.20), channel_id=1, source_target_pairs={{0,3},{1,0},{2,1},{3,2},{4,7},{5,4},{6,5},{7,6},{8,11},{9,8},{10,9... | collective-permute-start | bytes 1204232 | tf_op jit(solution)/shard_map/ppermute | solution.py:24

commit v2 on v1

--- a/solution.py
+++ b/solution.py
@@ -32,7 +32,7 @@
 
 
 def couple_kernel(
-    slices, sched, weights, t_hbm, o_own, o_next, o_far_a, o_far_b, o_last, kept, out_1, out_2, out_3,
+    slices, sched, weights, t_hbm, o_own, o_1, o_2, o_3, o_4, o_5, o_6, kept, out_1, out_2, out_3,
     acc, t_buf, o_buf, even_0, even_1, odd_0, odd_1, t_sems, o_sems,
 ):
     sources, strip = t_buf.shape[0], t_buf.shape[1]
@@ -41,7 +41,7 @@
     lane = pl.multiple_of(sched[2 * count + 1], 128)
     member = sched[2 * count + 2]
     copies, first = [], 0
-    for i, piece in enumerate((o_own, o_next, o_far_a, o_far_b, o_last)):
+    for i, piece in enumerate((o_own, o_1, o_2, o_3, o_4, o_5, o_6)):
         size = piece.shape[0]
         copies.append(pltpu.make_async_copy(piece, o_buf.at[pl.ds(first, size)], o_sems.at[i]))
         first += size
@@ -141,11 +141,13 @@
     strip = width // coup
     lanes = -width % 128
 
+    half = ov_dev // 2
     padded = jnp.pad(intersections, ((0, 0), (0, 0), (0, lanes)))
-    half = ov_dev // 2
-    o_next, o_last = shift(padded, -1), shift(padded, 1)
-    far_a, far_b = shift(o_last[:half], 1), shift(o_next[half:], -1)
-    pieces = (padded, o_next, far_a, far_b, o_last)
+    low, high = padded[:half], padded[half:]
+    last_low, next_high = shift(low, 1), shift(high, -1)
+    last_high, next_low = shift(high, 1), shift(low, -1)
+    far_low, far_high = shift(last_low, 1), shift(next_high, -1)
+    pieces = (padded, next_low, next_high, far_low, far_high, last_low, last_high)
 
     owner_row = lookup(pair_slot, coupling_list[0]) - group_index * coup
     reader_row = lookup(pair_slot, coupling_list[1])

time: 276 us -> 273 us (0.989)
    ppermute x16 -> x18, starting transfers between devices: 25.2 us -> 27.1 us  [shift(): lax.ppermute(x, 'coup', [(i, (i + step) % peers) for i in range(peers)])]
    ppermute x16 -> x18, waiting for transfers between devices: 95.9 us -> 96 us  [shift(): lax.ppermute(x, 'coup', [(i, (i + step) % peers) for i in range(peers)])]
  transfers between devices with their start and end apart: 18 -> 20, of which waited for: 9 -> 11; matrix products, arithmetic and copies ran while one was open for 5% -> 4% of each run, Pallas kernels for 0% -> 0%
where the time goes in v2:
time: 273 us; the launch traced here: 272 us
  waiting for transfers between devices  104 us (38%)
  blocking collectives  56 us (21%)
  Pallas kernels  48.5 us (18%)
  starting transfers between devices  40.1 us (15%)
  local copies, waits for them, and re-layouts  13.6 us (5%)
  other arithmetic  9.12 us (3%)
    ppermute x18, waiting for transfers between devices, shift(): lax.ppermute(x, 'coup', [(i, (i + step) % peers) for i in range(peers)])  96 us
    all_to_all x1, blocking collectives, amplitudes_of(): arrived = lax.all_to_all(outgoing, PAIRS, 0, 0, tiled=True)  52.3 us
    pallas_call x2, Pallas kernels, couple(): pl.pallas_call(functools.partial(couple_kernel, slices), out_shape=[jax.S...  48.5 us
    ppermute x18, starting transfers between devices, shift(): lax.ppermute(x, 'coup', [(i, (i + step) % peers) for i in range(peers)])  27.1 us
    all_to_all x1, starting transfers between devices, exchange_wanted(): tiles = lax.all_to_all(tiles, ('pairs_0', 'pairs_1'), 0, 0, tiled=True)  8.05 us
    all_to_all x1, waiting for transfers between devices, exchange_wanted(): tiles = lax.all_to_all(tiles, ('pairs_0', 'pairs_1'), 0, 0, tiled=True)  7.51 us
  transfers between devices with their start and end apart: 20, of which 11 were waited for; matrix products, arithmetic and copies ran while one was open for 4% of the time, Pallas kernels for 0%

profile of v2, /device:TPU:0, one launch (start us, length us, event | category | flops | bytes accessed | tf_op | source)
XLA Modules:
  0.0 271.8 jit_solution(5399158061845471984)
XLA Ops:
  0.7 0.8 pad_maximum_fusion.2
  1.4 2.9 %collective-permute-start.3 = (f32[1,449]{1,0:T(1,128)S(1)}, f32[1,449]{1,0:T(1,128)S(1)}, u32[]{:S(2)}, u32[]{:S(2)}) collective-permute-start(f32[1,449]{1,0:T(1,128)S(1)} %bitcast.43), channel_id=1, source_target_pairs={{0,3},{1,0},{2,1},{3,2},{4,7},{5,4},{6,5},{7,6},{8,11},{9,8},{10,9... | collective-permute-start | bytes 5396 | tf_op jit(solution)/shard_map/ppermute | solution.py:24
  4.3 0.8 collective-permute-start.4
  5.1 0.9 collective-permute-start.5
  6.0 1.2 copy.24
  7.3 1.9 collective-permute-start.1
  9.2 1.4 collective-permute-start.2
  10.6 1.4 fusion.9
  11.9 0.8 select_reduce_fusion.2
  12.8 0.6 and_select_fusion.1
  13.6 0.3 copy-done.14
  14.0 3.7 %all_to_all.20 = s32[16,2,1]{0,2,1:T(1,128)S(1)} all-to-all(s32[16,2,1]{0,2,1:T(1,128)S(1)} %copy.26), channel_id=1, replica_groups=mesh['pairs_0'=4,'pairs_1'=4,'pairs_2'=2,'coup'=4] {'pairs_2'}, dimensions={1} | all-to-all | bytes 256 | tf_op jit(solution)/shard_map/all_to_all | solution.py:29
  17.7 0.7 copy.27
  18.4 8.0 %all-to-all-start.1 = ((s32[16,2,1]{1,2,0:T(1,128)}), s32[16,2,1]{1,2,0:T(1,128)S(1)}, u32[]{:S(2)}, u32[]{:S(2)}) async-start(s32[16,2,1]{1,2,0:T(1,128)} %copy.27), calls=%async_computation.1 | async-start | bytes 16384 | tf_op jit(solution)/shard_map/all_to_all | solution.py:30
  26.4 7.5 %all-to-all-done.1 = s32[16,2,1]{1,2,0:T(1,128)S(1)} async-done(((s32[16,2,1]{1,2,0:T(1,128)}), s32[16,2,1]{1,2,0:T(1,128)S(1)}, u32[]{:S(2)}, u32[]{:S(2)}) %all-to-all-start.1) | async-done | bytes 160 | tf_op jit(solution)/shard_map/all_to_all | solution.py:30
  34.1 1.9 collective-permute-start
  36.4 2.6 collective-permute-done
  39.0 0.6 copy-done.2
  39.6 0.2 fusion.1
  39.8 2.6 gather_fusion
  42.5 5.0 %all-to-all-start.2 = ((bf16[32,112,512]{2,1,0:T(8,128)(2,1)}), bf16[32,112,512]{2,1,0:T(8,128)(2,1)}, u32[]{:S(2)}, u32[]{:S(2)}) async-start(bf16[32,112,512]{2,1,0:T(8,128)(2,1)} %gather_fusion), calls=%async_computation.2 | async-start | bytes 7340032 | tf_op jit(solution)/shard_map/all_to_all | solution.py:190
  47.5 1.5 pad_slice_fusion
  48.9 3.1 %collective-permute-start.7 = (bf16[2,448,512]{2,1,0:T(8,128)(2,1)}, bf16[2,448,512]{2,1,0:T(8,128)(2,1)S(1)}, u32[]{:S(2)}, u32[]{:S(2)}) collective-permute-start(bf16[2,448,512]{2,1,0:T(8,128)(2,1)} %get-tuple-element.25), channel_id=1, source_target_pairs={{0,3},{1,0},{2,1},{3,2},{4,7},{5,4},{6,5},{7,6},{8,11},{9,8},{10,9... | collective-permute-start | bytes 2752520 | tf_op jit(solution)/shard_map/ppermute | solution.py:24
  52.0 3.3 %collective-permute-start.6 = (bf16[2,448,512]{2,1,0:T(8,128)(2,1)}, bf16[2,448,512]{2,1,0:T(8,128)(2,1)}, u32[]{:S(2)}, u32[]{:S(2)}) collective-permute-start(bf16[2,448,512]{2,1,0:T(8,128)(2,1)} %get-tuple-element.26), channel_id=1, source_target_pairs={{0,3},{1,0},{2,1},{3,2},{4,7},{5,4},{6,5},{7,6},{8,11},{9,8},{10,9... | collective-permute-start | bytes 2752520 | tf_op jit(solution)/shard_map/ppermute | solution.py:24
  55.3 17.8 %collective-permute-done.7.o_2 = bf16[2,448,512]{2,1,0:T(8,128)(2,1)S(1)} collective-permute-done((bf16[2,448,512]{2,1,0:T(8,128)(2,1)}, bf16[2,448,512]{2,1,0:T(8,128)(2,1)S(1)}, u32[]{:S(2)}, u32[]{:S(2)}) %collective-permute-start.7) | collective-permute-done | bytes 917536 | tf_op jit(solution)/shard_map/ppermute | solution.py:24
  73.1 3.6 %collective-permute-start.10 = (bf16[2,448,512]{2,1,0:T(8,128)(2,1)S(1)}, bf16[2,448,512]{2,1,0:T(8,128)(2,1)}, u32[]{:S(2)}, u32[]{:S(2)}) collective-permute-start(bf16[2,448,512]{2,1,0:T(8,128)(2,1)S(1)} %collective-permute-done.7.o_2), channel_id=1, source_target_pairs={{0,3},{1,0},{2,1},{3,2},{4,7},{5,4},{6,5},{7,6},{8,11},{9,8},{10,9... | collective-permute-start | bytes 2752520 | tf_op jit(solution)/shard_map/ppermute | solution.py:24
  76.8 1.5 pad.18.o_own
  78.7 0.7 concatenate.9.sched
  79.4 1.3 select_reduce_fusion.weights
  80.6 15.8 %collective-permute-done.11.o_6 = bf16[2,448,512]{2,1,0:T(8,128)(2,1)} collective-permute-done((bf16[2,448,512]{2,1,0:T(8,128)(2,1)}, bf16[2,448,512]{2,1,0:T(8,128)(2,1)}, u32[]{:S(2)}, u32[]{:S(2)}) %collective-permute-start.11) | collective-permute-done | bytes 917536 | tf_op jit(solution)/shard_map/ppermute | solution.py:24
  96.4 15.0 %collective-permute-done.10.o_4 = bf16[2,448,512]{2,1,0:T(8,128)(2,1)} collective-permute-done((bf16[2,448,512]{2,1,0:T(8,128)(2,1)S(1)}, bf16[2,448,512]{2,1,0:T(8,128)(2,1)}, u32[]{:S(2)}, u32[]{:S(2)}) %collective-permute-start.10) | collective-permute-done | bytes 917536 | tf_op jit(solution)/shard_map/ppermute | solution.py:24
  111.4 3.5 %collective-permute-done.9.o_3 = bf16[2,448,512]{2,1,0:T(8,128)(2,1)} collective-permute-done((bf16[2,448,512]{2,1,0:T(8,128)(2,1)}, bf16[2,448,512]{2,1,0:T(8,128)(2,1)}, u32[]{:S(2)}, u32[]{:S(2)}) %collective-permute-start.9) | collective-permute-done | bytes 917536 | tf_op jit(solution)/shard_map/ppermute | solution.py:24
  115.0 24.2 %couple_strips.1 = (f32[4,112,448]{2,1,0:T(8,128)}, bf16[4,112,448]{2,1,0:T(8,128)(2,1)}, bf16[4,112,448]{2,1,0:T(8,128)(2,1)}, bf16[4,112,448]{2,1,0:T(8,128)(2,1)}) custom-call(s32[131]{0:T(256)} %concatenate.9.sched, f32[64]{0:T(128)} %select_reduce_fusion.weights, bf16[32,112,512]{2,1,0:T(8,128)(2,1)} %all-to-all-done.2.t_hbm, ...), custom_call_target="tpu_custom_call" | custom-call | tf_op jit(solution)/shard_map/couple_strips/pallas_call | solution.py:104
  139.2 1.9 collective-permute-start.13
  141.2 1.3 collective-permute-start.14
  142.5 19.4 %collective-permute-done.12 = bf16[4,112,448]{2,1,0:T(8,128)(2,1)S(1)} collective-permute-done((bf16[4,112,448]{2,1,0:T(8,128)(2,1)}, bf16[4,112,448]{2,1,0:T(8,128)(2,1)S(1)}, u32[]{:S(2)}, u32[]{:S(2)}) %collective-permute-start.12) | collective-permute-done | bytes 401440 | tf_op jit(solution)/shard_map/ppermute | solution.py:24
  161.9 0.6 collective-permute-done.14
  162.5 1.5 convert_add_fusion.1
  164.0 0.3 fusion.4
  164.3 2.7 %gather_fusion.1 = bf16[32,112,512]{2,1,0:T(8,128)(2,1)} fusion(bf16[4,112,512]{2,1,0:T(8,128)(2,1)S(1)} %fusion.4, s32[1024]{0:T(1024)} %copy-done.9), kind=kCustom, calls=%fused_computation.1 | custom fusion | bytes 7340160 | tf_op jit(solution)/shard_map/gather | solution.py:189
  167.0 52.3 %all_to_all.21.t_hbm = bf16[32,112,512]{2,1,0:T(8,128)(2,1)} all-to-all(bf16[32,112,512]{2,1,0:T(8,128)(2,1)} %gather_fusion.1), channel_id=1, replica_groups=mesh['pairs_0'=4,'pairs_1'=4,'pairs_2'=2,'coup'=4] {'pairs_0','pairs_1',..., dimensions={0} | all-to-all | bytes 7340032 | tf_op jit(solution)/shard_map/all_to_all | solution.py:190
  219.3 24.3 %couple_pairs.1 = (f32[448,448]{1,0:T(8,128)}, bf16[448,448]{1,0:T(8,128)(2,1)}, bf16[448,448]{1,0:T(8,128)(2,1)}, bf16[448,448]{1,0:T(8,128)(2,1)}) custom-call(s32[131]{0:T(256)} %concatenate.9.sched, f32[64]{0:T(128)} %select_reduce_fusion.weights, bf16[32,112,512]{2,1,0:T(8,128)(2,1)} %all_to_all.21.t_hbm, bf16[4,448,512]{2,1,0:T(8,128)(2,1)} %pad.18.o_own, ...), custom_call_target="tpu_custom_call" | custom-call | tf_op jit(solution)/shard_map/couple_pairs/pallas_call | solution.py:104
  243.7 0.3 collective-permute-start.15
  244.0 3.8 %collective-permute-start.16 = (bf16[448,448]{1,0:T(8,128)(2,1)}, bf16[448,448]{1,0:T(8,128)(2,1)S(1)}, u32[]{:S(2)}, u32[]{:S(2)}) collective-permute-start(bf16[448,448]{1,0:T(8,128)(2,1)} %get-tuple-element.19), channel_id=1, source_target_pairs={{0,2},{1,3},{2,0},{3,1},{4,6},{5,7},{6,4},{7,5},{8,10},{9,11},{10,... | collective-permute-start | bytes 1204232 | tf_op jit(solution)/shard_map/ppermute | solution.py:24
  247.8 10.6 %collective-permute-done.15 = bf16[448,448]{1,0:T(8,128)(2,1)S(1)} collective-permute-done((bf16[448,448]{1,0:T(8,128)(2,1)}, bf16[448,448]{1,0:T(8,128)(2,1)S(1)}, u32[]{:S(2)}, u32[]{:S(2)}) %collective-permute-start.15) | collective-permute-done | bytes 401440 | tf_op jit(solution)/shard_map/ppermute | solution.py:24
  258.3 10.6 %collective-permute-done.16 = bf16[448,448]{1,0:T(8,128)(2,1)S(1)} collective-permute-done((bf16[448,448]{1,0:T(8,128)(2,1)}, bf16[448,448]{1,0:T(8,128)(2,1)S(1)}, u32[]{:S(2)}, u32[]{:S(2)}) %collective-permute-start.16) | collective-permute-done | bytes 401440 | tf_op jit(solution)/shard_map/ppermute | solution.py:24
  268.9 1.6 fusion.6
  270.5 1.2 copy.28
  (60 shorter events, 1.3 us)
Async XLA Ops:
  1.4 32.7 %collective-permute-start.3 = (f32[1,449]{1,0:T(1,128)S(1)}, f32[1,449]{1,0:T(1,128)S(1)}, u32[]{:S(2)}, u32[]{:S(2)}) collective-permute-start(f32[1,449]{1,0:T(1,128)S(1)} %bitcast.43), channel_id=1, source_target_pairs={{0,3},{1,0},{2,1},{3,2},{4,7},{5,4},{6,5},{7,6},{8,11},{9,8},{10,9... | collective-permute-start | bytes 5396 | tf_op jit(solution)/shard_map/ppermute | solution.py:24
  4.3 31.8 %collective-permute-start.4 = (f32[1,449]{1,0:T(1,128)S(1)}, f32[1,449]{1,0:T(1,128)S(1)}, u32[]{:S(2)}, u32[]{:S(2)}) collective-permute-start(f32[1,449]{1,0:T(1,128)S(1)} %bitcast.44), channel_id=1, source_target_pairs={{0,2},{1,3},{2,0},{3,1},{4,6},{5,7},{6,4},{7,5},{8,10},{9,11},{10,... | collective-permute-start | bytes 5396 | tf_op jit(solution)/shard_map/ppermute | solution.py:24
  5.1 31.0 %collective-permute-start.5 = (f32[1,449]{1,0:T(1,128)S(1)}, f32[1,449]{1,0:T(1,128)S(1)}, u32[]{:S(2)}, u32[]{:S(2)}) collective-permute-start(f32[1,449]{1,0:T(1,128)S(1)} %bitcast.45), channel_id=1, source_target_pairs={{0,1},{1,2},{2,3},{3,0},{4,5},{5,6},{6,7},{7,4},{8,9},{9,10},{10,1... | collective-permute-start | bytes 5396 | tf_op jit(solution)/shard_map/ppermute | solution.py:24
  7.3 29.1 %collective-permute-start.1 = (bf16[112,512]{1,0:T(8,128)(2,1)S(1)}, bf16[112,512]{1,0:T(8,128)(2,1)S(1)}, u32[]{:S(2)}, u32[]{:S(2)}) collective-permute-start(bf16[112,512]{1,0:T(8,128)(2,1)S(1)} %get-tuple-element.29), channel_id=1, source_target_pairs={{0,2},{1,3},{2,0},{3,1},{4,6},{5,7},{6,4},{7,5},{8,10},{9,11},{10,... | collective-permute-start | bytes 344072 | tf_op jit(solution)/shard_map/ppermute | solution.py:24
  9.2 27.2 %collective-permute-start.2 = (bf16[112,512]{1,0:T(8,128)(2,1)S(1)}, bf16[112,512]{1,0:T(8,128)(2,1)S(1)}, u32[]{:S(2)}, u32[]{:S(2)}) collective-permute-start(bf16[112,512]{1,0:T(8,128)(2,1)S(1)} %get-tuple-element.30), channel_id=1, source_target_pairs={{0,1},{1,2},{2,3},{3,0},{4,5},{5,6},{6,7},{7,4},{8,9},{9,10},{10,1... | collective-permute-start | bytes 344072 | tf_op jit(solution)/shard_map/ppermute | solution.py:24
  13.4 0.5 copy-start.14
  18.4 15.6 %all-to-all-start.1 = ((s32[16,2,1]{1,2,0:T(1,128)}), s32[16,2,1]{1,2,0:T(1,128)S(1)}, u32[]{:S(2)}, u32[]{:S(2)}) async-start(s32[16,2,1]{1,2,0:T(1,128)} %copy.27), calls=%async_computation.1 | async-start | bytes 16384 | tf_op jit(solution)/shard_map/all_to_all | solution.py:30
  34.1 8.4 %copy-start.9 = (s32[1024]{0:T(1024)}, s32[1024]{0:T(1024)S(1)}, u32[]{:S(2)}) copy-start(s32[1024]{0:T(1024)S(1)} %pad_clamp_fusion) | copy-start | bytes 12292
  34.1 4.9 %collective-permute-start = (bf16[112,512]{1,0:T(8,128)(2,1)S(1)}, bf16[112,512]{1,0:T(8,128)(2,1)S(1)}, u32[]{:S(2)}, u32[]{:S(2)}) collective-permute-start(bf16[112,512]{1,0:T(8,128)(2,1)S(1)} %get-tuple-element.28), channel_id=1, source_target_pairs={{0,3},{1,0},{2,1},{3,2},{4,7},{5,4},{6,5},{7,6},{8,11},{9,8},{10,9... | collective-permute-start | bytes 344072 | tf_op jit(solution)/shard_map/ppermute | solution.py:24
  36.1 2.9 %copy-start.4 = (f32[4,512]{1,0:T(4,128)}, f32[4,512]{1,0:T(4,128)S(1)}, u32[]{:S(2)}) copy-start(f32[4,512]{1,0:T(4,128)S(1)} %pad.17) | copy-start | bytes 24580
  36.3 2.7 copy-start.10
  36.4 2.6 copy-start.7
  39.0 0.6 copy-start.2
  42.5 5.0 %copy-start = (bf16[4,448,448]{2,1,0:T(8,128)(2,1)S(1)}, bf16[4,448,448]{2,1,0:T(8,128)(2,1)}, u32[]{:S(2)}) copy-start(bf16[4,448,448]{2,1,0:T(8,128)(2,1)} %param.13) | copy-start | bytes 4816900
  42.5 72.5 %all-to-all-start.2 = ((bf16[32,112,512]{2,1,0:T(8,128)(2,1)}), bf16[32,112,512]{2,1,0:T(8,128)(2,1)}, u32[]{:S(2)}, u32[]{:S(2)}) async-start(bf16[32,112,512]{2,1,0:T(8,128)(2,1)} %gather_fusion), calls=%async_computation.2 | async-start | bytes 7340032 | tf_op jit(solution)/shard_map/all_to_all | solution.py:190
  48.9 24.1 %collective-permute-start.7 = (bf16[2,448,512]{2,1,0:T(8,128)(2,1)}, bf16[2,448,512]{2,1,0:T(8,128)(2,1)S(1)}, u32[]{:S(2)}, u32[]{:S(2)}) collective-permute-start(bf16[2,448,512]{2,1,0:T(8,128)(2,1)} %get-tuple-element.25), channel_id=1, source_target_pairs={{0,3},{1,0},{2,1},{3,2},{4,7},{5,4},{6,5},{7,6},{8,11},{9,8},{10,9... | collective-permute-start | bytes 2752520 | tf_op jit(solution)/shard_map/ppermute | solution.py:24
  52.0 24.8 %collective-permute-start.8 = (bf16[2,448,512]{2,1,0:T(8,128)(2,1)}, bf16[2,448,512]{2,1,0:T(8,128)(2,1)}, u32[]{:S(2)}, u32[]{:S(2)}) collective-permute-start(bf16[2,448,512]{2,1,0:T(8,128)(2,1)} %get-tuple-element.26), channel_id=1, source_target_pairs={{0,1},{1,2},{2,3},{3,0},{4,5},{5,6},{6,7},{7,4},{8,9},{9,10},{10,1... | collective-permute-start | bytes 2752520 | tf_op jit(solution)/shard_map/ppermute | solution.py:24
  52.0 44.4 %collective-permute-start.11 = (bf16[2,448,512]{2,1,0:T(8,128)(2,1)}, bf16[2,448,512]{2,1,0:T(8,128)(2,1)}, u32[]{:S(2)}, u32[]{:S(2)}) collective-permute-start(bf16[2,448,512]{2,1,0:T(8,128)(2,1)} %get-tuple-element.25), channel_id=1, source_target_pairs={{0,1},{1,2},{2,3},{3,0},{4,5},{5,6},{6,7},{7,4},{8,9},{9,10},{10,1... | collective-permute-start | bytes 2752520 | tf_op jit(solution)/shard_map/ppermute | solution.py:24
  52.0 44.4 %collective-permute-start.6 = (bf16[2,448,512]{2,1,0:T(8,128)(2,1)}, bf16[2,448,512]{2,1,0:T(8,128)(2,1)}, u32[]{:S(2)}, u32[]{:S(2)}) collective-permute-start(bf16[2,448,512]{2,1,0:T(8,128)(2,1)} %get-tuple-element.26), channel_id=1, source_target_pairs={{0,3},{1,0},{2,1},{3,2},{4,7},{5,4},{6,5},{7,6},{8,11},{9,8},{10,9... | collective-permute-start | bytes 2752520 | tf_op jit(solution)/shard_map/ppermute | solution.py:24
  73.1 41.9 %copy-start.1 = (bf16[2,448,512]{2,1,0:T(8,128)(2,1)}, bf16[2,448,512]{2,1,0:T(8,128)(2,1)S(1)}, u32[]{:S(2)}) copy-start(bf16[2,448,512]{2,1,0:T(8,128)(2,1)S(1)} %collective-permute-done.7.o_2) | copy-start | bytes 2752516
  73.1 38.3 %collective-permute-start.10 = (bf16[2,448,512]{2,1,0:T(8,128)(2,1)S(1)}, bf16[2,448,512]{2,1,0:T(8,128)(2,1)}, u32[]{:S(2)}, u32[]{:S(2)}) collective-permute-start(bf16[2,448,512]{2,1,0:T(8,128)(2,1)S(1)} %collective-permute-done.7.o_2), channel_id=1, source_target_pairs={{0,3},{1,0},{2,1},{3,2},{4,7},{5,4},{6,5},{7,6},{8,11},{9,8},{10,9... | collective-permute-start | bytes 2752520 | tf_op jit(solution)/shard_map/ppermute | solution.py:24
  76.8 38.2 %collective-permute-start.9 = (bf16[2,448,512]{2,1,0:T(8,128)(2,1)}, bf16[2,448,512]{2,1,0:T(8,128)(2,1)}, u32[]{:S(2)}, u32[]{:S(2)}) collective-permute-start(bf16[2,448,512]{2,1,0:T(8,128)(2,1)} %collective-permute-done.8.o_5), channel_id=1, source_target_pairs={{0,1},{1,2},{2,3},{3,0},{4,5},{5,6},{6,7},{7,4},{8,9},{9,10},{10,1... | collective-permute-start | bytes 2752520 | tf_op jit(solution)/shard_map/ppermute | solution.py:24
  76.8 1.6 copy-start.15
  76.8 1.8 copy-start.12
  76.8 1.8 copy-start.13
  80.6 83.3 %copy-start.3 = (bf16[112,512]{1,0:T(8,128)(2,1)S(1)}, bf16[112,512]{1,0:T(8,128)(2,1)}, u32[]{:S(2)}) copy-start(bf16[112,512]{1,0:T(8,128)(2,1)} %copy-done.2) | copy-start | bytes 344068
  80.6 83.3 %copy-start.5 = (f32[4,512]{1,0:T(4,128)S(1)}, f32[4,512]{1,0:T(4,128)}, u32[]{:S(2)}) copy-start(f32[4,512]{1,0:T(4,128)} %copy-done.4) | copy-start | bytes 24580
  80.6 83.3 %copy-start.8 = (f32[4,112]{1,0:T(4,128)S(1)}, f32[4,112]{1,0:T(4,128)}, u32[]{:S(2)}) copy-start(f32[4,112]{1,0:T(4,128)} %copy-done.7) | copy-start | bytes 5380
  80.6 83.3 %copy-start.11 = (f32[4]{0:T(128)S(1)}, f32[4]{0:T(128)}, u32[]{:S(2)}) copy-start(f32[4]{0:T(128)} %copy-done.10) | copy-start | bytes 52
  139.2 22.7 %collective-permute-start.12 = (bf16[4,112,448]{2,1,0:T(8,128)(2,1)}, bf16[4,112,448]{2,1,0:T(8,128)(2,1)S(1)}, u32[]{:S(2)}, u32[]{:S(2)}) collective-permute-start(bf16[4,112,448]{2,1,0:T(8,128)(2,1)} %get-tuple-element.14), channel_id=1, source_target_pairs={{0,1},{1,2},{2,3},{3,0},{4,5},{5,6},{6,7},{7,4},{8,9},{9,10},{10,1... | collective-permute-start | bytes 1204232 | tf_op jit(solution)/shard_map/ppermute | solution.py:24
  139.2 22.6 %collective-permute-start.13 = (bf16[4,112,448]{2,1,0:T(8,128)(2,1)}, bf16[4,112,448]{2,1,0:T(8,128)(2,1)S(1)}, u32[]{:S(2)}, u32[]{:S(2)}) collective-permute-start(bf16[4,112,448]{2,1,0:T(8,128)(2,1)} %get-tuple-element.15), channel_id=1, source_target_pairs={{0,2},{1,3},{2,0},{3,1},{4,6},{5,7},{6,4},{7,5},{8,10},{9,11},{10,... | collective-permute-start | bytes 1204232 | tf_op jit(solution)/shard_map/ppermute | solution.py:24
  141.2 21.3 %collective-permute-start.14 = (bf16[4,112,448]{2,1,0:T(8,128)(2,1)}, bf16[4,112,448]{2,1,0:T(8,128)(2,1)S(1)}, u32[]{:S(2)}, u32[]{:S(2)}) collective-permute-start(bf16[4,112,448]{2,1,0:T(8,128)(2,1)} %get-tuple-element.16), channel_id=1, source_target_pairs={{0,3},{1,0},{2,1},{3,2},{4,7},{5,4},{6,5},{7,6},{8,11},{9,8},{10,9... | collective-permute-start | bytes 1204232 | tf_op jit(solution)/shard_map/ppermute | solution.py:24
  219.3 49.6 %copy-start.6 = (f32[1,448]{1,0:T(1,128)S(1)}, f32[1,448]{1,0:T(1,128)}, u32[]{:S(2)}) copy-start(f32[1,448]{1,0:T(1,128)} %param.11) | copy-start | bytes 5380
  243.7 14.7 %collective-permute-start.15 = (bf16[448,448]{1,0:T(8,128)(2,1)}, bf16[448,448]{1,0:T(8,128)(2,1)S(1)}, u32[]{:S(2)}, u32[]{:S(2)}) collective-permute-start(bf16[448,448]{1,0:T(8,128)(2,1)} %get-tuple-element.18), channel_id=1, source_target_pairs={{0,1},{1,2},{2,3},{3,0},{4,5},{5,6},{6,7},{7,4},{8,9},{9,10},{10,1... | collective-permute-start | bytes 1204232 | tf_op jit(solution)/shard_map/ppermute | solution.py:24
  244.0 25.0 %collective-permute-start.16 = (bf16[448,448]{1,0:T(8,128)(2,1)}, bf16[448,448]{1,0:T(8,128)(2,1)S(1)}, u32[]{:S(2)}, u32[]{:S(2)}) collective-permute-start(bf16[448,448]{1,0:T(8,128)(2,1)} %get-tuple-element.19), channel_id=1, source_target_pairs={{0,2},{1,3},{2,0},{3,1},{4,6},{5,7},{6,4},{7,5},{8,10},{9,11},{10,... | collective-permute-start | bytes 1204232 | tf_op jit(solution)/shard_map/ppermute | solution.py:24
  247.8 21.2 %collective-permute-start.17 = (bf16[448,448]{1,0:T(8,128)(2,1)}, bf16[448,448]{1,0:T(8,128)(2,1)S(1)}, u32[]{:S(2)}, u32[]{:S(2)}) collective-permute-start(bf16[448,448]{1,0:T(8,128)(2,1)} %get-tuple-element.20), channel_id=1, source_target_pairs={{0,3},{1,0},{2,1},{3,2},{4,7},{5,4},{6,5},{7,6},{8,11},{9,8},{10,9... | collective-permute-start | bytes 1204232 | tf_op jit(solution)/shard_map/ppermute | solution.py:24

commit v3 on v2

--- a/solution.py
+++ b/solution.py
@@ -31,36 +31,44 @@
     return tiles.reshape(32)
 
 
-def couple_kernel(
-    slices, sched, weights, t_hbm, o_own, o_1, o_2, o_3, o_4, o_5, o_6, kept, out_1, out_2, out_3,
-    acc, t_buf, o_buf, even_0, even_1, odd_0, odd_1, t_sems, o_sems,
-):
+def couple_kernel(first, slices, sched, weights, t_hbm, *refs):
+    base, pieces = (0, refs[:7]) if first else (2 * t_hbm.shape[0], refs[:7])
+    refs = refs[7:]
+    if not first:
+        running, refs = refs[0], refs[1:]
+    outs, refs = (refs[:1], refs[1:]) if first else (refs[:4], refs[4:])
+    acc, t_buf, o_buf, even_0, even_1, odd_0, odd_1, sems = refs
     sources, strip = t_buf.shape[0], t_buf.shape[1]
-    count = 2 * sources
+    count = 4 * sources
     offset = pl.multiple_of(sched[2 * count], 16)
     lane = pl.multiple_of(sched[2 * count + 1], 128)
     member = sched[2 * count + 2]
-    copies, first = [], 0
-    for i, piece in enumerate((o_own, o_1, o_2, o_3, o_4, o_5, o_6)):
+    copies, row = [], 0
+    for i, piece in enumerate(pieces):
         size = piece.shape[0]
-        copies.append(pltpu.make_async_copy(piece, o_buf.at[pl.ds(first, size)], o_sems.at[i]))
-        first += size
-    copies.append(pltpu.make_async_copy(t_hbm, t_buf, t_sems.at[0]))
+        copies.append(pltpu.make_async_copy(piece, o_buf.at[pl.ds(row, size)], sems.at[i]))
+        row += size
+    copies.append(pltpu.make_async_copy(t_hbm, t_buf, sems.at[7]))
+    if not first:
+        copies.append(pltpu.make_async_copy(running, acc, sems.at[8]))
     for copy in copies:
         copy.start()
-    for ref in (acc, even_0, even_1, odd_0, odd_1):
+    for ref in (even_0, even_1, odd_0, odd_1):
         ref[...] = jnp.zeros_like(ref)
+    if first:
+        acc[...] = jnp.zeros_like(acc)
     for copy in copies:
         copy.wait()
 
     def right(h, s, ref):
         product = lax.dot_general(
-            t_buf[h], o_buf[sched[2 * h + s]], (((1,), (1,)), ((), ())), preferred_element_type=jnp.float32
+            t_buf[h], o_buf[sched[base + 2 * h + s]], (((1,), (1,)), ((), ())),
+            preferred_element_type=jnp.float32,
         )
         ref[pl.ds(offset, strip), :] = product.astype(jnp.bfloat16)
 
     def left(h, s, ref):
-        k = 2 * h + s
+        k = base + 2 * h + s
         product = jnp.dot(
             o_buf[sched[k], :, pl.ds(lane, 256)], ref[...], preferred_element_type=jnp.float32
         )
@@ -83,8 +91,13 @@
         return carry
 
     lax.fori_loop(0, sources // 2, step, 0)
+    if first:
+        copy = pltpu.make_async_copy(acc, outs[0], sems.at[8])
+        copy.start()
+        copy.wait()
+        return
     members = acc.shape[0]
-    for d, out in enumerate((kept, out_1, out_2, out_3)):
+    for d, out in enumerate(outs):
         peer = lax.rem(member + d, members)
         if slices:
             rows = pl.ds(pl.multiple_of(peer * strip, 16), strip)
@@ -94,33 +107,36 @@
             out[...] = acc[peer].astype(out.dtype)
 
 
-def couple(sched, weights, strips, pieces, coup, slices):
+def couple(sched, weights, strips, pieces, coup, running, slices):
     _, strip, lanes = strips.shape
     width = pieces[0].shape[1]
+    first = running is None
     part = (coup, strip, width) if slices else (width, width)
     total = sum(piece.shape[0] for piece in pieces)
+    anywhere = pl.BlockSpec(memory_space=pl.ANY)
     whole = pl.BlockSpec(part, lambda i, *_: (0,) * len(part))
     half = pltpu.VMEM((256, width), jnp.bfloat16)
+    sums = jax.ShapeDtypeStruct((coup, width, width), jnp.float32)
+    parts = [jax.ShapeDtypeStruct(part, jnp.float32)] + [jax.ShapeDtypeStruct(part, jnp.bfloat16)] * 3
     return pl.pallas_call(
-        functools.partial(couple_kernel, slices),
-        out_shape=[jax.ShapeDtypeStruct(part, jnp.float32)] + [jax.ShapeDtypeStruct(part, jnp.bfloat16)] * 3,
+        functools.partial(couple_kernel, first, slices),
+        out_shape=[sums] if first else parts,
         grid_spec=pltpu.PrefetchScalarGridSpec(
             num_scalar_prefetch=2,
             grid=(1,),
-            in_specs=[pl.BlockSpec(memory_space=pl.ANY)] * (1 + len(pieces)),
-            out_specs=[whole] * 4,
+            in_specs=[anywhere] * (1 + len(pieces) + (0 if first else 1)),
+            out_specs=[anywhere] if first else [whole] * 4,
             scratch_shapes=[
                 pltpu.VMEM((coup, width, width), jnp.float32),
                 pltpu.VMEM(strips.shape, jnp.bfloat16),
                 pltpu.VMEM((total, width, lanes), jnp.bfloat16),
                 half, half, half, half,
-                pltpu.SemaphoreType.DMA((1,)),
-                pltpu.SemaphoreType.DMA((len(pieces),)),
+                pltpu.SemaphoreType.DMA((9,)),
             ],
         ),
         compiler_params=pltpu.CompilerParams(vmem_limit_bytes=60 * 2**20),
-        name="couple_strips" if slices else "couple_pairs",
-    )(sched, weights, strips, *pieces)
+        name="couple_first" if first else "couple_strips" if slices else "couple_pairs",
+    )(sched, weights, strips, *pieces, *([] if first else [running]))
 
 
 def sum_parts(kept, parts):
@@ -158,7 +174,8 @@
     twin = jnp.max(
         jnp.where((source[None, :] == source[:, None]) & (position[None, :] < position[:, None]), 1, 0), axis=1
     )
-    slot = 2 * source + twin
+    core = lax.axis_index("pairs_2")
+    slot = groups * (source % 2 ^ core) + source // 2 * 2 + twin
     chosen = slot[None, :] == position[:, None]
     pick = lambda v: jnp.sum(jnp.where(chosen, v[None, :], jnp.zeros((), v.dtype)), axis=1)
     strip_row = member * strip
@@ -170,32 +187,41 @@
     asked = source[None, :] == lax.broadcasted_iota(jnp.int32, (groups, count), 0)
     wanted = exchange_wanted(jnp.max(jnp.where(asked, read_pair[None, :], 0), axis=1))
 
-    flipped = jnp.pad(jnp.transpose(integrals[0]), ((0, 0), (0, lanes)))
-    rows_of = lambda d: lax.dynamic_slice_in_dim(flipped, lax.rem(member + d, coup) * strip, strip)
-    sent = [shift(rows_of(coup - e), coup - e) for e in range(1, coup)]
-    integral_strips = jnp.stack([rows_of(0)] + sent)
+    denominator = orbital_energy[:, :, None] + orbital_energy[:, None, :] + pair_energy[:, None, None]
+    own_integrals = integrals.astype(jnp.float32)
+
+    def to_strips(matrix):
+        flipped = jnp.pad(jnp.transpose(matrix), ((0, 0), (0, lanes)))
+        rows_of = lambda d: lax.dynamic_slice_in_dim(flipped, lax.rem(member + d, coup) * strip, strip)
+        return jnp.stack([rows_of(0)] + [shift(rows_of(coup - e), coup - e) for e in range(1, coup)])
+
+    rounded = to_strips((-own_integrals / denominator).astype(jnp.bfloat16)[0])
+    integral_strips = to_strips(integrals[0])
     energies = jnp.concatenate([orbital_energy[0], pair_energy])[None]
     energies = jnp.concatenate([energies] + [shift(energies, -e) for e in range(1, coup)])
     orbital, pair = energies[:, :width], energies[:, width]
     own_rows = lax.dynamic_slice_in_dim(orbital, strip_row, strip, axis=1)
     all_columns = jnp.pad(orbital, ((0, 0), (0, lanes)))
     strip_denominator = own_rows[:, :, None] + all_columns[:, None, :] + pair[:, None, None]
-    integral_f = integral_strips.astype(jnp.float32)
-    amplitudes = -integral_f / strip_denominator
-    wanted = (wanted - member) % coup
+    wanted = ((wanted - member) % coup).reshape(groups // 2, 2)
+    wanted_same = jnp.where(core == 0, wanted[:, 0], wanted[:, 1])
+    wanted_other = jnp.where(core == 0, wanted[:, 1], wanted[:, 0])
 
     for iteration in range(ITERS):
-        rounded = amplitudes.astype(jnp.bfloat16)
-        outgoing = rounded.at[wanted].get(mode="promise_in_bounds")
-        arrived = lax.all_to_all(outgoing, PAIRS, 0, 0, tiled=True)
         last = iteration == ITERS - 1
-        kept, *parts = couple(sched, weights, arrived, pieces, coup, not last)
+        other = rounded.at[wanted_other].get(mode="promise_in_bounds")
+        other = lax.ppermute(other, "pairs_2", [(0, 1), (1, 0)])
+        same = rounded.at[wanted_same].get(mode="promise_in_bounds")
+        same = lax.all_to_all(same, PAIRS[:2], 0, 0, tiled=True)
+        other = lax.all_to_all(other, PAIRS[:2], 0, 0, tiled=True)
+        (running,) = couple(sched, weights, same, pieces, coup, None, not last)
+        kept, *parts = couple(sched, weights, other, pieces, coup, running, not last)
         coupled = sum_parts(kept, parts)
         if not last:
             coupled = jnp.pad(coupled, ((0, 0), (0, 0), (0, lanes)))
-            amplitudes = -(integral_f + coupled) / strip_denominator
-    denominator = orbital_energy[:, :, None] + orbital_energy[:, None, :] + pair_energy[:, None, None]
-    return -(integrals.astype(jnp.float32) + jnp.transpose(coupled)[None]) / denominator
+            amplitudes = -(integral_strips.astype(jnp.float32) + coupled) / strip_denominator
+            rounded = amplitudes.astype(jnp.bfloat16)
+    return -(own_integrals + jnp.transpose(coupled)[None]) / denominator
 
 
 def solution(mesh):

time: 273 us -> 285 us (1.044)
  blocking collectives: 56 us -> 36.2 us
  starting transfers between devices: 40.1 us -> 58.2 us
  Pallas kernels: 48.5 us -> 62.9 us
  other arithmetic: 9.12 us -> 6 us
  local copies, waits for them, and re-layouts: 13.6 us -> 16.5 us
    all_to_all x1 -> x3, waiting for transfers between devices: 0.01 us -> 34.2 us  [the longest x1 23.2 us: amplitudes_of(): same = lax.all_to_all(same, PAIRS[:2], 0, 0, tiled=True)]
    ppermute x18 -> x21, waiting for transfers between devices: 96 us -> 62.8 us  [shift(): lax.ppermute(x, 'coup', [(i, (i + step) % peers) for i in range(peers)])]
    all_to_all x1, blocking collectives: 52.3 us -> 32.5 us  [amplitudes_of(): same = lax.all_to_all(same, PAIRS[:2], 0, 0, tiled=True)]
    pallas_call x2 -> x4, Pallas kernels: 48.5 us -> 62.9 us  [couple(): pl.pallas_call(functools.partial(couple_kernel, first, slices), out_shape...]
    all_to_all x1 -> x3, starting transfers between devices: 4.98 us -> 14.2 us  [the longest x2 8.46 us: amplitudes_of(): other = lax.all_to_all(other, PAIRS[:2], 0, 0, tiled=True)]
    ppermute x18 -> x21, starting transfers between devices: 27.1 us -> 35.9 us  [shift(): lax.ppermute(x, 'coup', [(i, (i + step) % peers) for i in range(peers)])]
    gather x2 -> x4, local copies, waits for them, and re-layouts: 5.37 us -> 6.48 us  [the longest x2 3.9 us: amplitudes_of(): other = rounded.at[wanted_other].get(mode='promise_in_bounds')]
  transfers between devices with their start and end apart: 20 -> 27, of which waited for: 11 -> 10; matrix products, arithmetic and copies ran while one was open for 4% -> 4% of each run, Pallas kernels for 0% -> 11%
where the time goes in v3:
time: 285 us; the launch traced here: 284 us
  waiting for transfers between devices  103 us (36%)
  Pallas kernels  62.9 us (22%)
  starting transfers between devices  58.2 us (20%)
  blocking collectives  36.2 us (13%)
  local copies, waits for them, and re-layouts  16.5 us (6%)
  other arithmetic  6 us (2%)
    pallas_call x4, Pallas kernels, couple(): pl.pallas_call(functools.partial(couple_kernel, first, slices), out_shape...  62.9 us
    ppermute x21, waiting for transfers between devices, shift(): lax.ppermute(x, 'coup', [(i, (i + step) % peers) for i in range(peers)])  62.8 us
    ppermute x21, starting transfers between devices, shift(): lax.ppermute(x, 'coup', [(i, (i + step) % peers) for i in range(peers)])  35.9 us
    all_to_all x1, blocking collectives, amplitudes_of(): same = lax.all_to_all(same, PAIRS[:2], 0, 0, tiled=True)  32.5 us
    all_to_all x1, waiting for transfers between devices, amplitudes_of(): same = lax.all_to_all(same, PAIRS[:2], 0, 0, tiled=True)  23.2 us
    all_to_all x2, waiting for transfers between devices, amplitudes_of(): other = lax.all_to_all(other, PAIRS[:2], 0, 0, tiled=True)  10.9 us
    all_to_all x2, starting transfers between devices, amplitudes_of(): other = lax.all_to_all(other, PAIRS[:2], 0, 0, tiled=True)  8.46 us
    all_to_all x1, starting transfers between devices, exchange_wanted(): tiles = lax.all_to_all(tiles, ('pairs_0', 'pairs_1'), 0, 0, tiled=True)  8.05 us
  transfers between devices with their start and end apart: 27, of which 10 were waited for; matrix products, arithmetic and copies ran while one was open for 4% of the time, Pallas kernels for 11%

profile of v3, /device:TPU:0, one launch (start us, length us, event | category | flops | bytes accessed | tf_op | source)
XLA Modules:
  0.0 284.2 jit_solution(17276659097323854192)
XLA Ops:
  0.0 1.2 copy.34
  1.9 1.0 fusion.4
  3.0 2.9 %collective-permute-start.3 = (bf16[112,512]{1,0:T(8,128)(2,1)S(1)}, bf16[112,512]{1,0:T(8,128)(2,1)S(1)}, u32[]{:S(2)}, u32[]{:S(2)}) collective-permute-start(bf16[112,512]{1,0:T(8,128)(2,1)S(1)} %get-tuple-element.32), channel_id=1, source_target_pairs={{0,3},{1,0},{2,1},{3,2},{4,7},{5,4},{6,5},{7,6},{8,11},{9,8},{10,9... | collective-permute-start | bytes 344072 | tf_op jit(solution)/shard_map/ppermute | solution.py:24
  5.9 0.8 collective-permute-start.4
  7.2 3.7 %all_to_all.30 = s32[16,2,1]{0,2,1:T(1,128)S(1)} all-to-all(s32[16,2,1]{0,2,1:T(1,128)S(1)} %copy.36), channel_id=1, replica_groups=mesh['pairs_0'=4,'pairs_1'=4,'pairs_2'=2,'coup'=4] {'pairs_2'}, dimensions={1} | all-to-all | bytes 256 | tf_op jit(solution)/shard_map/all_to_all | solution.py:29
  10.9 0.7 copy.37
  11.6 8.0 %all-to-all-start.1 = ((s32[16,2,1]{1,2,0:T(1,128)}), s32[16,2,1]{1,2,0:T(1,128)S(1)}, u32[]{:S(2)}, u32[]{:S(2)}) async-start(s32[16,2,1]{1,2,0:T(1,128)} %copy.37), calls=%async_computation.1 | async-start | bytes 16384 | tf_op jit(solution)/shard_map/all_to_all | solution.py:30
  19.7 1.0 collective-permute-start.5
  20.6 6.6 %all-to-all-done.1 = s32[16,2,1]{1,2,0:T(1,128)S(1)} async-done(((s32[16,2,1]{1,2,0:T(1,128)}), s32[16,2,1]{1,2,0:T(1,128)S(1)}, u32[]{:S(2)}, u32[]{:S(2)}) %all-to-all-start.1) | async-done | bytes 160 | tf_op jit(solution)/shard_map/all_to_all | solution.py:30
  27.4 2.0 gather_fusion
  29.4 1.9 gather_fusion.1
  31.3 5.7 %all-to-all-start.3 = ((bf16[16,112,512]{2,1,0:T(8,128)(2,1)}), bf16[16,112,512]{2,1,0:T(8,128)(2,1)}, u32[]{:S(2)}, u32[]{:S(2)}) async-start(bf16[16,112,512]{2,1,0:T(8,128)(2,1)} %gather_fusion.1), calls=%async_computation.3 | async-start | bytes 3670016 | tf_op jit(solution)/shard_map/all_to_all | solution.py:215
  37.1 1.5 pad_slice_fusion
  38.6 3.2 %collective-permute-start.8 = (bf16[2,448,512]{2,1,0:T(8,128)(2,1)}, bf16[2,448,512]{2,1,0:T(8,128)(2,1)S(1)}, u32[]{:S(2)}, u32[]{:S(2)}) collective-permute-start(bf16[2,448,512]{2,1,0:T(8,128)(2,1)} %get-tuple-element.25), channel_id=1, source_target_pairs={{0,3},{1,0},{2,1},{3,2},{4,7},{5,4},{6,5},{7,6},{8,11},{9,8},{10,9... | collective-permute-start | bytes 2752520 | tf_op jit(solution)/shard_map/ppermute | solution.py:24
  41.8 23.2 %all-to-all-done.3.t_hbm = bf16[16,112,512]{2,1,0:T(8,128)(2,1)} async-done(((bf16[16,112,512]{2,1,0:T(8,128)(2,1)}), bf16[16,112,512]{2,1,0:T(8,128)(2,1)}, u32[]{:S(2)}, u32[]{:S(2)}) %all-to-all-start.3) | async-done | bytes 1835040 | tf_op jit(solution)/shard_map/all_to_all | solution.py:215
  65.0 4.7 %all-to-all-start.2 = ((bf16[16,112,512]{2,1,0:T(8,128)(2,1)}), bf16[16,112,512]{2,1,0:T(8,128)(2,1)}, u32[]{:S(2)}, u32[]{:S(2)}) async-start(bf16[16,112,512]{2,1,0:T(8,128)(2,1)} %collective-permute-done.6), calls=%async_computation.2 | async-start | bytes 3670016 | tf_op jit(solution)/shard_map/all_to_all | solution.py:216
  69.9 3.2 %collective-permute-start.7 = (bf16[2,448,512]{2,1,0:T(8,128)(2,1)}, bf16[2,448,512]{2,1,0:T(8,128)(2,1)}, u32[]{:S(2)}, u32[]{:S(2)}) collective-permute-start(bf16[2,448,512]{2,1,0:T(8,128)(2,1)} %get-tuple-element.26), channel_id=1, source_target_pairs={{0,3},{1,0},{2,1},{3,2},{4,7},{5,4},{6,5},{7,6},{8,11},{9,8},{10,9... | collective-permute-start | bytes 2752520 | tf_op jit(solution)/shard_map/ppermute | solution.py:24
  73.1 3.2 %collective-permute-start.11 = (bf16[2,448,512]{2,1,0:T(8,128)(2,1)S(1)}, bf16[2,448,512]{2,1,0:T(8,128)(2,1)}, u32[]{:S(2)}, u32[]{:S(2)}) collective-permute-start(bf16[2,448,512]{2,1,0:T(8,128)(2,1)S(1)} %collective-permute-done.8.refs_2_), channel_id=1, source_target_pairs={{0,3},{1,0},{2,1},{3,2},{4,7},{5,4},{6,5},{7,6},{8,11},{9,8},{10,9... | collective-permute-start | bytes 2752520 | tf_op jit(solution)/shard_map/ppermute | solution.py:24
  76.3 3.0 %pad.21.refs_0_ = bf16[4,448,512]{2,1,0:T(8,128)(2,1)} pad(bf16[4,448,448]{2,1,0:T(8,128)(2,1)} %param.13, bf16[]{:T(256)} %constant.121.clone.1), padding=0_0x0_0x0_64 | pad | bytes 3440642 | tf_op jit(solution)/shard_map/jit(_pad)/pad | solution.py:161
  79.6 0.6 concatenate.9.sched
  80.3 0.7 select_reduce_fusion.weights
  81.0 13.5 %collective-permute-done.12.refs_6_ = bf16[2,448,512]{2,1,0:T(8,128)(2,1)S(1)} collective-permute-done((bf16[2,448,512]{2,1,0:T(8,128)(2,1)}, bf16[2,448,512]{2,1,0:T(8,128)(2,1)S(1)}, u32[]{:S(2)}, u32[]{:S(2)}) %collective-permute-start.12) | collective-permute-done | bytes 917536 | tf_op jit(solution)/shard_map/ppermute | solution.py:24
  94.5 17.6 %collective-permute-done.10.refs_3_ = bf16[2,448,512]{2,1,0:T(8,128)(2,1)} collective-permute-done((bf16[2,448,512]{2,1,0:T(8,128)(2,1)S(1)}, bf16[2,448,512]{2,1,0:T(8,128)(2,1)}, u32[]{:S(2)}, u32[]{:S(2)}) %collective-permute-start.10) | collective-permute-done | bytes 917536 | tf_op jit(solution)/shard_map/ppermute | solution.py:24
  112.1 15.3 %couple_first.2.refs_7_ = f32[4,448,448]{2,1,0:T(8,128)} custom-call(s32[131]{0:T(256)} %concatenate.9.sched, f32[64]{0:T(128)} %select_reduce_fusion.weights, bf16[16,112,512]{2,1,0:T(8,128)(2,1)} %all-to-all-done.3.t_hbm, bf16[4,448,512]{2,1,0:T(8,128)(2,1)} %pad.21.refs_0_, bf16[2,448,512]{2,1,0:T(8,128)(2,1)} %collective-permute-done.7.refs_1_, ...), custom_call_target="tpu_custom_call" | custom-call | tf_op jit(solution)/shard_map/couple_first/pallas_call | solution.py:121
  127.4 16.2 %couple_strips.1 = (f32[4,112,448]{2,1,0:T(8,128)}, bf16[4,112,448]{2,1,0:T(8,128)(2,1)}, bf16[4,112,448]{2,1,0:T(8,128)(2,1)}, bf16[4,112,448]{2,1,0:T(8,128)(2,1)}) custom-call(s32[131]{0:T(256)} %concatenate.9.sched, f32[64]{0:T(128)} %select_reduce_fusion.weights, bf16[16,112,512]{2,1,0:T(8,128)(2,1)} %all-to-all-done.2.t_hbm, ...), custom_call_target="tpu_custom_call" | custom-call | tf_op jit(solution)/shard_map/couple_strips/pallas_call | solution.py:121
  143.7 0.9 collective-permute-start.13
  144.6 3.8 %collective-permute-start.14 = (bf16[4,112,448]{2,1,0:T(8,128)(2,1)}, bf16[4,112,448]{2,1,0:T(8,128)(2,1)S(1)}, u32[]{:S(2)}, u32[]{:S(2)}) collective-permute-start(bf16[4,112,448]{2,1,0:T(8,128)(2,1)} %get-tuple-element.15), channel_id=1, source_target_pairs={{0,2},{1,3},{2,0},{3,1},{4,6},{5,7},{6,4},{7,5},{8,10},{9,11},{10,... | collective-permute-start | bytes 1204232 | tf_op jit(solution)/shard_map/ppermute | solution.py:24
  149.1 3.5 %collective-permute-start.17 = (f32[1,449]{1,0:T(1,128)S(1)}, f32[1,449]{1,0:T(1,128)S(1)}, u32[]{:S(2)}, u32[]{:S(2)}) collective-permute-start(f32[1,449]{1,0:T(1,128)S(1)} %bitcast.55), channel_id=1, source_target_pairs={{0,2},{1,3},{2,0},{3,1},{4,6},{5,7},{6,4},{7,5},{8,10},{9,11},{10,... | collective-permute-start | bytes 5396 | tf_op jit(solution)/shard_map/ppermute | solution.py:24
  152.6 13.6 %collective-permute-done.16 = f32[1,449]{1,0:T(1,128)S(1)} collective-permute-done((f32[1,449]{1,0:T(1,128)S(1)}, f32[1,449]{1,0:T(1,128)S(1)}, u32[]{:S(2)}, u32[]{:S(2)}) %collective-permute-start.16) | collective-permute-done | bytes 1828 | tf_op jit(solution)/shard_map/ppermute | solution.py:24
  166.2 1.0 collective-permute-start.18
  167.2 3.1 %collective-permute-start.1 = (bf16[112,512]{1,0:T(8,128)(2,1)S(1)}, bf16[112,512]{1,0:T(8,128)(2,1)S(1)}, u32[]{:S(2)}, u32[]{:S(2)}) collective-permute-start(bf16[112,512]{1,0:T(8,128)(2,1)S(1)} %get-tuple-element.29), channel_id=1, source_target_pairs={{0,2},{1,3},{2,0},{3,1},{4,6},{5,7},{6,4},{7,5},{8,10},{9,11},{10,... | collective-permute-start | bytes 344072 | tf_op jit(solution)/shard_map/ppermute | solution.py:24
  171.2 3.2 %collective-permute-start = (bf16[112,512]{1,0:T(8,128)(2,1)S(1)}, bf16[112,512]{1,0:T(8,128)(2,1)S(1)}, u32[]{:S(2)}, u32[]{:S(2)}) collective-permute-start(bf16[112,512]{1,0:T(8,128)(2,1)S(1)} %get-tuple-element.28), channel_id=1, source_target_pairs={{0,3},{1,0},{2,1},{3,2},{4,7},{5,4},{6,5},{7,6},{8,11},{9,8},{10,9... | collective-permute-start | bytes 344072 | tf_op jit(solution)/shard_map/ppermute | solution.py:24
  174.5 1.4 convert_add_fusion.1
  175.9 1.0 collective-permute-done.2
  177.2 1.9 gather_fusion.2
  179.2 0.7 gather_fusion.3
  179.8 32.5 %all_to_all.31.t_hbm = bf16[16,112,512]{2,1,0:T(8,128)(2,1)} all-to-all(bf16[16,112,512]{2,1,0:T(8,128)(2,1)S(1)} %gather_fusion.3), channel_id=1, replica_groups=mesh['pairs_0'=4,'pairs_1'=4,'pairs_2'=2,'coup'=4] {'pairs_0','pairs_1'}, dimensions={0} | all-to-all | bytes 3670016 | tf_op jit(solution)/shard_map/all_to_all | solution.py:215
  212.3 3.7 %all-to-all-start.4 = ((bf16[16,112,512]{2,1,0:T(8,128)(2,1)}), bf16[16,112,512]{2,1,0:T(8,128)(2,1)S(1)}, u32[]{:S(2)}, u32[]{:S(2)}) async-start(bf16[16,112,512]{2,1,0:T(8,128)(2,1)} %collective-permute-done.19), calls=%async_computation.4 | async-start | bytes 3670016 | tf_op jit(solution)/shard_map/all_to_all | solution.py:216
  216.1 15.3 %couple_first.3.refs_7_ = f32[4,448,448]{2,1,0:T(8,128)} custom-call(s32[131]{0:T(256)} %concatenate.9.sched, f32[64]{0:T(128)} %select_reduce_fusion.weights, bf16[16,112,512]{2,1,0:T(8,128)(2,1)} %all_to_all.31.t_hbm, bf16[4,448,512]{2,1,0:T(8,128)(2,1)} %pad.21.refs_0_, bf16[2,448,512]{2,1,0:T(8,128)(2,1)} %collective-permute-done.7.refs_1_, ...), custom_call_target="tpu_custom_call" | custom-call | tf_op jit(solution)/shard_map/couple_first/pallas_call | solution.py:121
  231.3 10.9 %all-to-all-done.4.t_hbm = bf16[16,112,512]{2,1,0:T(8,128)(2,1)S(1)} async-done(((bf16[16,112,512]{2,1,0:T(8,128)(2,1)}), bf16[16,112,512]{2,1,0:T(8,128)(2,1)S(1)}, u32[]{:S(2)}, u32[]{:S(2)}) %all-to-all-start.4) | async-done | bytes 1835040 | tf_op jit(solution)/shard_map/all_to_all | solution.py:216
  242.3 1.3 copy-done.6
  243.5 16.2 %couple_pairs.1 = (f32[448,448]{1,0:T(8,128)}, bf16[448,448]{1,0:T(8,128)(2,1)}, bf16[448,448]{1,0:T(8,128)(2,1)}, bf16[448,448]{1,0:T(8,128)(2,1)}) custom-call(s32[131]{0:T(256)} %concatenate.9.sched, f32[64]{0:T(128)} %select_reduce_fusion.weights, bf16[16,112,512]{2,1,0:T(8,128)(2,1)} %copy-done.6, bf16[4,448,512]{2,1,0:T(8,128)(2,1)} %pad.21.refs_0_, ...), custom_call_target="tpu_custom_call" | custom-call | tf_op jit(solution)/shard_map/couple_pairs/pallas_call | solution.py:121
  259.7 0.8 collective-permute-start.20
  260.5 4.4 %collective-permute-start.21 = (bf16[448,448]{1,0:T(8,128)(2,1)}, bf16[448,448]{1,0:T(8,128)(2,1)S(1)}, u32[]{:S(2)}, u32[]{:S(2)}) collective-permute-start(bf16[448,448]{1,0:T(8,128)(2,1)} %get-tuple-element.19), channel_id=1, source_target_pairs={{0,2},{1,3},{2,0},{3,1},{4,6},{5,7},{6,4},{7,5},{8,10},{9,11},{10,... | collective-permute-start | bytes 1204232 | tf_op jit(solution)/shard_map/ppermute | solution.py:24
  264.9 9.2 %collective-permute-done.20 = bf16[448,448]{1,0:T(8,128)(2,1)S(1)} collective-permute-done((bf16[448,448]{1,0:T(8,128)(2,1)}, bf16[448,448]{1,0:T(8,128)(2,1)S(1)}, u32[]{:S(2)}, u32[]{:S(2)}) %collective-permute-start.20) | collective-permute-done | bytes 401440 | tf_op jit(solution)/shard_map/ppermute | solution.py:24
  274.1 7.2 %collective-permute-done.21 = bf16[448,448]{1,0:T(8,128)(2,1)S(1)} collective-permute-done((bf16[448,448]{1,0:T(8,128)(2,1)}, bf16[448,448]{1,0:T(8,128)(2,1)S(1)}, u32[]{:S(2)}, u32[]{:S(2)}) %collective-permute-start.21) | collective-permute-done | bytes 401440 | tf_op jit(solution)/shard_map/ppermute | solution.py:24
  281.4 1.6 fusion.3
  283.0 1.2 copy.39
  (71 shorter events, 3.1 us)
Async XLA Ops:
  0.0 6.7 %copy-start.8 = (s32[3,64]{1,0:T(4,128)S(1)}, s32[3,64]{1,0:T(4,128)}, u32[]{:S(2)}) copy-start(s32[3,64]{1,0:T(4,128)} %param.7) | copy-start | bytes 2308
  0.0 6.7 %copy-start.9 = (s32[128]{0:T(128)S(1)}, s32[128]{0:T(128)}, u32[]{:S(2)}) copy-start(s32[128]{0:T(128)} %param.8) | copy-start | bytes 1540
  1.2 26.1 %copy-start.3 = (bf16[1,448,448]{1,2,0:T(8,128)(2,1)}, bf16[1,448,448]{1,2,0:T(8,128)(2,1)S(1)}, u32[]{:S(2)}) copy-start(bf16[1,448,448]{1,2,0:T(8,128)(2,1)S(1)} %copy.34) | copy-start | bytes 1204228
  3.0 24.3 %collective-permute-start.3 = (bf16[112,512]{1,0:T(8,128)(2,1)S(1)}, bf16[112,512]{1,0:T(8,128)(2,1)S(1)}, u32[]{:S(2)}, u32[]{:S(2)}) collective-permute-start(bf16[112,512]{1,0:T(8,128)(2,1)S(1)} %get-tuple-element.32), channel_id=1, source_target_pairs={{0,3},{1,0},{2,1},{3,2},{4,7},{5,4},{6,5},{7,6},{8,11},{9,8},{10,9... | collective-permute-start | bytes 344072 | tf_op jit(solution)/shard_map/ppermute | solution.py:24
  5.9 21.4 %collective-permute-start.4 = (bf16[112,512]{1,0:T(8,128)(2,1)S(1)}, bf16[112,512]{1,0:T(8,128)(2,1)S(1)}, u32[]{:S(2)}, u32[]{:S(2)}) collective-permute-start(bf16[112,512]{1,0:T(8,128)(2,1)S(1)} %get-tuple-element.33), channel_id=1, source_target_pairs={{0,2},{1,3},{2,0},{3,1},{4,6},{5,7},{6,4},{7,5},{8,10},{9,11},{10,... | collective-permute-start | bytes 344072 | tf_op jit(solution)/shard_map/ppermute | solution.py:24
  11.6 15.6 %all-to-all-start.1 = ((s32[16,2,1]{1,2,0:T(1,128)}), s32[16,2,1]{1,2,0:T(1,128)S(1)}, u32[]{:S(2)}, u32[]{:S(2)}) async-start(s32[16,2,1]{1,2,0:T(1,128)} %copy.37), calls=%async_computation.1 | async-start | bytes 16384 | tf_op jit(solution)/shard_map/all_to_all | solution.py:30
  19.7 7.7 %collective-permute-start.5 = (bf16[112,512]{1,0:T(8,128)(2,1)S(1)}, bf16[112,512]{1,0:T(8,128)(2,1)S(1)}, u32[]{:S(2)}, u32[]{:S(2)}) collective-permute-start(bf16[112,512]{1,0:T(8,128)(2,1)S(1)} %get-tuple-element.34), channel_id=1, source_target_pairs={{0,1},{1,2},{2,3},{3,0},{4,5},{5,6},{6,7},{7,4},{8,9},{9,10},{10,1... | collective-permute-start | bytes 344072 | tf_op jit(solution)/shard_map/ppermute | solution.py:24
  29.4 35.6 %collective-permute-start.6 = (bf16[16,112,512]{2,1,0:T(8,128)(2,1)}, bf16[16,112,512]{2,1,0:T(8,128)(2,1)}, u32[]{:S(2)}, u32[]{:S(2)}) collective-permute-start(bf16[16,112,512]{2,1,0:T(8,128)(2,1)} %gather_fusion), channel_id=1, source_target_pairs={{0,4},{4,0},{1,5},{5,1},{2,6},{6,2},{3,7},{7,3},{8,12},{12,8},{9,1... | collective-permute-start | bytes 5505032 | tf_op jit(solution)/shard_map/ppermute | solution.py:213
  31.3 5.7 %copy-start.5 = (bf16[4,448,448]{2,1,0:T(8,128)(2,1)S(1)}, bf16[4,448,448]{2,1,0:T(8,128)(2,1)}, u32[]{:S(2)}) copy-start(bf16[4,448,448]{2,1,0:T(8,128)(2,1)} %param.13) | copy-start | bytes 4816900
  31.3 33.7 %all-to-all-start.3 = ((bf16[16,112,512]{2,1,0:T(8,128)(2,1)}), bf16[16,112,512]{2,1,0:T(8,128)(2,1)}, u32[]{:S(2)}, u32[]{:S(2)}) async-start(bf16[16,112,512]{2,1,0:T(8,128)(2,1)} %gather_fusion.1), calls=%async_computation.3 | async-start | bytes 3670016 | tf_op jit(solution)/shard_map/all_to_all | solution.py:215
  38.6 34.5 %collective-permute-start.9 = (bf16[2,448,512]{2,1,0:T(8,128)(2,1)}, bf16[2,448,512]{2,1,0:T(8,128)(2,1)S(1)}, u32[]{:S(2)}, u32[]{:S(2)}) collective-permute-start(bf16[2,448,512]{2,1,0:T(8,128)(2,1)} %get-tuple-element.26), channel_id=1, source_target_pairs={{0,1},{1,2},{2,3},{3,0},{4,5},{5,6},{6,7},{7,4},{8,9},{9,10},{10,1... | collective-permute-start | bytes 2752520 | tf_op jit(solution)/shard_map/ppermute | solution.py:24
  38.6 34.5 %collective-permute-start.8 = (bf16[2,448,512]{2,1,0:T(8,128)(2,1)}, bf16[2,448,512]{2,1,0:T(8,128)(2,1)S(1)}, u32[]{:S(2)}, u32[]{:S(2)}) collective-permute-start(bf16[2,448,512]{2,1,0:T(8,128)(2,1)} %get-tuple-element.25), channel_id=1, source_target_pairs={{0,3},{1,0},{2,1},{3,2},{4,7},{5,4},{6,5},{7,6},{8,11},{9,8},{10,9... | collective-permute-start | bytes 2752520 | tf_op jit(solution)/shard_map/ppermute | solution.py:24
  65.0 62.4 %all-to-all-start.2 = ((bf16[16,112,512]{2,1,0:T(8,128)(2,1)}), bf16[16,112,512]{2,1,0:T(8,128)(2,1)}, u32[]{:S(2)}, u32[]{:S(2)}) async-start(bf16[16,112,512]{2,1,0:T(8,128)(2,1)} %collective-permute-done.6), calls=%async_computation.2 | async-start | bytes 3670016 | tf_op jit(solution)/shard_map/all_to_all | solution.py:216
  69.8 24.7 %collective-permute-start.12 = (bf16[2,448,512]{2,1,0:T(8,128)(2,1)}, bf16[2,448,512]{2,1,0:T(8,128)(2,1)S(1)}, u32[]{:S(2)}, u32[]{:S(2)}) collective-permute-start(bf16[2,448,512]{2,1,0:T(8,128)(2,1)} %get-tuple-element.25), channel_id=1, source_target_pairs={{0,1},{1,2},{2,3},{3,0},{4,5},{5,6},{6,7},{7,4},{8,9},{9,10},{10,1... | collective-permute-start | bytes 2752520 | tf_op jit(solution)/shard_map/ppermute | solution.py:24
  69.9 24.6 %collective-permute-start.7 = (bf16[2,448,512]{2,1,0:T(8,128)(2,1)}, bf16[2,448,512]{2,1,0:T(8,128)(2,1)}, u32[]{:S(2)}, u32[]{:S(2)}) collective-permute-start(bf16[2,448,512]{2,1,0:T(8,128)(2,1)} %get-tuple-element.26), channel_id=1, source_target_pairs={{0,3},{1,0},{2,1},{3,2},{4,7},{5,4},{6,5},{7,6},{8,11},{9,8},{10,9... | collective-permute-start | bytes 2752520 | tf_op jit(solution)/shard_map/ppermute | solution.py:24
  73.1 6.2 %copy-start = (bf16[2,448,512]{2,1,0:T(8,128)(2,1)}, bf16[2,448,512]{2,1,0:T(8,128)(2,1)S(1)}, u32[]{:S(2)}) copy-start(bf16[2,448,512]{2,1,0:T(8,128)(2,1)S(1)} %collective-permute-done.9.refs_5_) | copy-start | bytes 2752516
  73.1 39.1 %collective-permute-start.10 = (bf16[2,448,512]{2,1,0:T(8,128)(2,1)S(1)}, bf16[2,448,512]{2,1,0:T(8,128)(2,1)}, u32[]{:S(2)}, u32[]{:S(2)}) collective-permute-start(bf16[2,448,512]{2,1,0:T(8,128)(2,1)S(1)} %collective-permute-done.9.refs_5_), channel_id=1, source_target_pairs={{0,1},{1,2},{2,3},{3,0},{4,5},{5,6},{6,7},{7,4},{8,9},{9,10},{10,1... | collective-permute-start | bytes 2752520 | tf_op jit(solution)/shard_map/ppermute | solution.py:24
  73.1 6.2 %copy-start.1 = (bf16[2,448,512]{2,1,0:T(8,128)(2,1)}, bf16[2,448,512]{2,1,0:T(8,128)(2,1)S(1)}, u32[]{:S(2)}) copy-start(bf16[2,448,512]{2,1,0:T(8,128)(2,1)S(1)} %collective-permute-done.8.refs_2_) | copy-start | bytes 2752516
  73.1 39.0 %collective-permute-start.11 = (bf16[2,448,512]{2,1,0:T(8,128)(2,1)S(1)}, bf16[2,448,512]{2,1,0:T(8,128)(2,1)}, u32[]{:S(2)}, u32[]{:S(2)}) collective-permute-start(bf16[2,448,512]{2,1,0:T(8,128)(2,1)S(1)} %collective-permute-done.8.refs_2_), channel_id=1, source_target_pairs={{0,3},{1,0},{2,1},{3,2},{4,7},{5,4},{6,5},{7,6},{8,11},{9,8},{10,9... | collective-permute-start | bytes 2752520 | tf_op jit(solution)/shard_map/ppermute | solution.py:24
  76.3 3.9 %copy-start.10 = (f32[64]{0:T(128)S(1)}, f32[64]{0:T(128)}, u32[]{:S(2)}) copy-start(f32[64]{0:T(128)} %param.9) | copy-start | bytes 772
  94.5 17.7 %copy-start.2 = (bf16[2,448,512]{2,1,0:T(8,128)(2,1)}, bf16[2,448,512]{2,1,0:T(8,128)(2,1)S(1)}, u32[]{:S(2)}) copy-start(bf16[2,448,512]{2,1,0:T(8,128)(2,1)S(1)} %collective-permute-done.12.refs_6_) | copy-start | bytes 2752516
  127.4 21.0 %copy-start.7 = (f32[1,448]{1,0:T(1,128)S(1)}, f32[1,448]{1,0:T(1,128)}, u32[]{:S(2)}) copy-start(f32[1,448]{1,0:T(1,128)} %param.11) | copy-start | bytes 5380
  127.4 39.8 %copy-start.4 = (bf16[1,448,448]{1,2,0:T(8,128)(2,1)S(1)}, bf16[1,448,448]{1,2,0:T(8,128)(2,1)}, u32[]{:S(2)}) copy-start(bf16[1,448,448]{1,2,0:T(8,128)(2,1)} %copy-done.3) | copy-start | bytes 1204228
  143.7 27.6 %collective-permute-start.13 = (bf16[4,112,448]{2,1,0:T(8,128)(2,1)}, bf16[4,112,448]{2,1,0:T(8,128)(2,1)S(1)}, u32[]{:S(2)}, u32[]{:S(2)}) collective-permute-start(bf16[4,112,448]{2,1,0:T(8,128)(2,1)} %get-tuple-element.14), channel_id=1, source_target_pairs={{0,1},{1,2},{2,3},{3,0},{4,5},{5,6},{6,7},{7,4},{8,9},{9,10},{10,1... | collective-permute-start | bytes 1204232 | tf_op jit(solution)/shard_map/ppermute | solution.py:24
  144.6 29.9 %collective-permute-start.14 = (bf16[4,112,448]{2,1,0:T(8,128)(2,1)}, bf16[4,112,448]{2,1,0:T(8,128)(2,1)S(1)}, u32[]{:S(2)}, u32[]{:S(2)}) collective-permute-start(bf16[4,112,448]{2,1,0:T(8,128)(2,1)} %get-tuple-element.15), channel_id=1, source_target_pairs={{0,2},{1,3},{2,0},{3,1},{4,6},{5,7},{6,4},{7,5},{8,10},{9,11},{10,... | collective-permute-start | bytes 1204232 | tf_op jit(solution)/shard_map/ppermute | solution.py:24
  148.4 26.1 %collective-permute-start.15 = (bf16[4,112,448]{2,1,0:T(8,128)(2,1)}, bf16[4,112,448]{2,1,0:T(8,128)(2,1)S(1)}, u32[]{:S(2)}, u32[]{:S(2)}) collective-permute-start(bf16[4,112,448]{2,1,0:T(8,128)(2,1)} %get-tuple-element.16), channel_id=1, source_target_pairs={{0,3},{1,0},{2,1},{3,2},{4,7},{5,4},{6,5},{7,6},{8,11},{9,8},{10,9... | collective-permute-start | bytes 1204232 | tf_op jit(solution)/shard_map/ppermute | solution.py:24
  148.5 17.7 %collective-permute-start.16 = (f32[1,449]{1,0:T(1,128)S(1)}, f32[1,449]{1,0:T(1,128)S(1)}, u32[]{:S(2)}, u32[]{:S(2)}) collective-permute-start(f32[1,449]{1,0:T(1,128)S(1)} %bitcast.54), channel_id=1, source_target_pairs={{0,3},{1,0},{2,1},{3,2},{4,7},{5,4},{6,5},{7,6},{8,11},{9,8},{10,9... | collective-permute-start | bytes 5396 | tf_op jit(solution)/shard_map/ppermute | solution.py:24
  149.1 18.2 %collective-permute-start.17 = (f32[1,449]{1,0:T(1,128)S(1)}, f32[1,449]{1,0:T(1,128)S(1)}, u32[]{:S(2)}, u32[]{:S(2)}) collective-permute-start(f32[1,449]{1,0:T(1,128)S(1)} %bitcast.55), channel_id=1, source_target_pairs={{0,2},{1,3},{2,0},{3,1},{4,6},{5,7},{6,4},{7,5},{8,10},{9,11},{10,... | collective-permute-start | bytes 5396 | tf_op jit(solution)/shard_map/ppermute | solution.py:24
  166.2 4.8 %collective-permute-start.18 = (f32[1,449]{1,0:T(1,128)S(1)}, f32[1,449]{1,0:T(1,128)S(1)}, u32[]{:S(2)}, u32[]{:S(2)}) collective-permute-start(f32[1,449]{1,0:T(1,128)S(1)} %bitcast.56), channel_id=1, source_target_pairs={{0,1},{1,2},{2,3},{3,0},{4,5},{5,6},{6,7},{7,4},{8,9},{9,10},{10,1... | collective-permute-start | bytes 5396 | tf_op jit(solution)/shard_map/ppermute | solution.py:24
  167.2 8.7 %collective-permute-start.1 = (bf16[112,512]{1,0:T(8,128)(2,1)S(1)}, bf16[112,512]{1,0:T(8,128)(2,1)S(1)}, u32[]{:S(2)}, u32[]{:S(2)}) collective-permute-start(bf16[112,512]{1,0:T(8,128)(2,1)S(1)} %get-tuple-element.29), channel_id=1, source_target_pairs={{0,2},{1,3},{2,0},{3,1},{4,6},{5,7},{6,4},{7,5},{8,10},{9,11},{10,... | collective-permute-start | bytes 344072 | tf_op jit(solution)/shard_map/ppermute | solution.py:24
  170.9 6.0 %collective-permute-start.2 = (bf16[112,512]{1,0:T(8,128)(2,1)S(1)}, bf16[112,512]{1,0:T(8,128)(2,1)S(1)}, u32[]{:S(2)}, u32[]{:S(2)}) collective-permute-start(bf16[112,512]{1,0:T(8,128)(2,1)S(1)} %get-tuple-element.30), channel_id=1, source_target_pairs={{0,1},{1,2},{2,3},{3,0},{4,5},{5,6},{6,7},{7,4},{8,9},{9,10},{10,1... | collective-permute-start | bytes 344072 | tf_op jit(solution)/shard_map/ppermute | solution.py:24
  171.2 5.7 %collective-permute-start = (bf16[112,512]{1,0:T(8,128)(2,1)S(1)}, bf16[112,512]{1,0:T(8,128)(2,1)S(1)}, u32[]{:S(2)}, u32[]{:S(2)}) collective-permute-start(bf16[112,512]{1,0:T(8,128)(2,1)S(1)} %get-tuple-element.28), channel_id=1, source_target_pairs={{0,3},{1,0},{2,1},{3,2},{4,7},{5,4},{6,5},{7,6},{8,11},{9,8},{10,9... | collective-permute-start | bytes 344072 | tf_op jit(solution)/shard_map/ppermute | solution.py:24
  179.2 33.2 %collective-permute-start.19 = (bf16[16,112,512]{2,1,0:T(8,128)(2,1)}, bf16[16,112,512]{2,1,0:T(8,128)(2,1)}, u32[]{:S(2)}, u32[]{:S(2)}) collective-permute-start(bf16[16,112,512]{2,1,0:T(8,128)(2,1)} %gather_fusion.2), channel_id=1, source_target_pairs={{0,4},{4,0},{1,5},{5,1},{2,6},{6,2},{3,7},{7,3},{8,12},{12,8},{9,1... | collective-permute-start | bytes 5505032 | tf_op jit(solution)/shard_map/ppermute | solution.py:213
  212.3 29.9 %all-to-all-start.4 = ((bf16[16,112,512]{2,1,0:T(8,128)(2,1)}), bf16[16,112,512]{2,1,0:T(8,128)(2,1)S(1)}, u32[]{:S(2)}, u32[]{:S(2)}) async-start(bf16[16,112,512]{2,1,0:T(8,128)(2,1)} %collective-permute-done.19), calls=%async_computation.4 | async-start | bytes 3670016 | tf_op jit(solution)/shard_map/all_to_all | solution.py:216
  242.3 1.3 copy-start.6
  259.7 14.4 %collective-permute-start.20 = (bf16[448,448]{1,0:T(8,128)(2,1)}, bf16[448,448]{1,0:T(8,128)(2,1)S(1)}, u32[]{:S(2)}, u32[]{:S(2)}) collective-permute-start(bf16[448,448]{1,0:T(8,128)(2,1)} %get-tuple-element.18), channel_id=1, source_target_pairs={{0,1},{1,2},{2,3},{3,0},{4,5},{5,6},{6,7},{7,4},{8,9},{9,10},{10,1... | collective-permute-start | bytes 1204232 | tf_op jit(solution)/shard_map/ppermute | solution.py:24
  260.5 20.9 %collective-permute-start.21 = (bf16[448,448]{1,0:T(8,128)(2,1)}, bf16[448,448]{1,0:T(8,128)(2,1)S(1)}, u32[]{:S(2)}, u32[]{:S(2)}) collective-permute-start(bf16[448,448]{1,0:T(8,128)(2,1)} %get-tuple-element.19), channel_id=1, source_target_pairs={{0,2},{1,3},{2,0},{3,1},{4,6},{5,7},{6,4},{7,5},{8,10},{9,11},{10,... | collective-permute-start | bytes 1204232 | tf_op jit(solution)/shard_map/ppermute | solution.py:24
  264.9 16.5 %collective-permute-start.22 = (bf16[448,448]{1,0:T(8,128)(2,1)}, bf16[448,448]{1,0:T(8,128)(2,1)S(1)}, u32[]{:S(2)}, u32[]{:S(2)}) collective-permute-start(bf16[448,448]{1,0:T(8,128)(2,1)} %get-tuple-element.20), channel_id=1, source_target_pairs={{0,3},{1,0},{2,1},{3,2},{4,7},{5,4},{6,5},{7,6},{8,11},{9,8},{10,9... | collective-permute-start | bytes 1204232 | tf_op jit(solution)/shard_map/ppermute | solution.py:24

commit v4 on v2

--- a/solution.py
+++ b/solution.py
@@ -25,33 +25,61 @@
 
 
 def exchange_wanted(wanted_here):
-    tiles = wanted_here.reshape(16, 2, 1)
-    tiles = lax.all_to_all(tiles, "pairs_2", 1, 1, tiled=True)
-    tiles = lax.all_to_all(tiles, ("pairs_0", "pairs_1"), 0, 0, tiled=True)
-    return tiles.reshape(32)
+    return lax.all_to_all(wanted_here[:, None, None], PAIRS, 0, 0, tiled=True)[:, 0, 0]
+
+
+def pack(x, lead):
+    whole = x.shape[-1] // 128 * 128
+    tiles = [x[..., t : t + 128] for t in range(0, whole, 128)]
+    tail = x[..., whole:]
+    tiles.append(jnp.concatenate([tail[..., :lead, :], tail[..., -lead:, :]], axis=-1))
+    return jnp.concatenate(tiles, axis=-2)
 
 
 def couple_kernel(
     slices, sched, weights, t_hbm, o_own, o_1, o_2, o_3, o_4, o_5, o_6, kept, out_1, out_2, out_3,
-    acc, t_buf, o_buf, even_0, even_1, odd_0, odd_1, t_sems, o_sems,
+    acc, t_buf, o_buf, t_tail, o_tail, even_0, even_1, odd_0, odd_1, sems,
 ):
-    sources, strip = t_buf.shape[0], t_buf.shape[1]
+    sources, strip, width = t_buf.shape[0], t_buf.shape[1], o_buf.shape[1]
+    full = width // 128
+    o_lead, t_lead = o_tail.shape[1], t_tail.shape[1]
     count = 2 * sources
     offset = pl.multiple_of(sched[2 * count], 16)
     lane = pl.multiple_of(sched[2 * count + 1], 128)
     member = sched[2 * count + 2]
     copies, first = [], 0
-    for i, piece in enumerate((o_own, o_1, o_2, o_3, o_4, o_5, o_6)):
+    for piece in (o_own, o_1, o_2, o_3, o_4, o_5, o_6):
         size = piece.shape[0]
-        copies.append(pltpu.make_async_copy(piece, o_buf.at[pl.ds(first, size)], o_sems.at[i]))
+        into = pl.ds(first, size)
+        for t in range(full):
+            copies.append((piece.at[:, pl.ds(t * width, width), :], o_buf.at[into, :, pl.ds(128 * t, 128)]))
+        copies.append((piece.at[:, pl.ds(full * width, o_lead), :], o_tail.at[into]))
         first += size
-    copies.append(pltpu.make_async_copy(t_hbm, t_buf, t_sems.at[0]))
+    for t in range(full):
+        copies.append((t_hbm.at[:, pl.ds(t * strip, strip), :], t_buf.at[:, :, pl.ds(128 * t, 128)]))
+    copies.append((t_hbm.at[:, pl.ds(full * strip, t_lead), :], t_tail))
+    copies = [pltpu.make_async_copy(src, dst, sems.at[i]) for i, (src, dst) in enumerate(copies)]
     for copy in copies:
         copy.start()
     for ref in (acc, even_0, even_1, odd_0, odd_1):
         ref[...] = jnp.zeros_like(ref)
     for copy in copies:
         copy.wait()
+
+    def unpack(tail, buf, index, lead):
+        both = tail[index]
+        empty = jnp.zeros((lead, 64), both.dtype)
+        rows = buf.shape[1]
+        buf[index, 0:lead, 128 * full :] = jnp.concatenate([both[:, :64], empty], axis=1)
+        buf[index, rows - lead : rows, 128 * full :] = jnp.concatenate([both[:, 64:], empty], axis=1)
+
+    def unpack_o(i, carry):
+        unpack(o_tail, o_buf, i, o_lead)
+        unpack(t_tail, t_buf, 2 * i, t_lead)
+        unpack(t_tail, t_buf, 2 * i + 1, t_lead)
+        return carry
+
+    lax.fori_loop(0, sources // 2, unpack_o, 0)
 
     def right(h, s, ref):
         product = lax.dot_general(
@@ -87,17 +115,25 @@
     for d, out in enumerate((kept, out_1, out_2, out_3)):
         peer = lax.rem(member + d, members)
         if slices:
-            rows = pl.ds(pl.multiple_of(peer * strip, 16), strip)
+            begin = pl.multiple_of(peer * strip, 16)
             for r in range(members):
-                out[r] = acc[lax.rem(peer + r, members), rows, :].astype(out.dtype)
+                row = lax.rem(peer + r, members)
+                for t in range(full):
+                    part = acc[row, pl.ds(begin, strip), 128 * t : 128 * t + 128]
+                    out[r, strip * t : strip * t + strip, :] = part.astype(out.dtype)
+                tail = acc[row, pl.ds(begin, strip), 128 * full :]
+                out[r, strip * full :, :] = jnp.concatenate(
+                    [tail[:t_lead], tail[strip - t_lead :]], axis=1
+                ).astype(out.dtype)
         else:
             out[...] = acc[peer].astype(out.dtype)
 
 
-def couple(sched, weights, strips, pieces, coup, slices):
-    _, strip, lanes = strips.shape
-    width = pieces[0].shape[1]
-    part = (coup, strip, width) if slices else (width, width)
+def couple(sched, weights, strips, pieces, coup, strip, width, slices):
+    sources, packed, _ = strips.shape
+    full = width // 128
+    lanes = 128 * full + 128
+    part = (coup, packed, 128) if slices else (width, width)
     total = sum(piece.shape[0] for piece in pieces)
     whole = pl.BlockSpec(part, lambda i, *_: (0,) * len(part))
     half = pltpu.VMEM((256, width), jnp.bfloat16)
@@ -111,11 +147,12 @@
             out_specs=[whole] * 4,
             scratch_shapes=[
                 pltpu.VMEM((coup, width, width), jnp.float32),
-                pltpu.VMEM(strips.shape, jnp.bfloat16),
+                pltpu.VMEM((sources, strip, lanes), jnp.bfloat16),
                 pltpu.VMEM((total, width, lanes), jnp.bfloat16),
+                pltpu.VMEM((sources, packed - full * strip, 128), jnp.bfloat16),
+                pltpu.VMEM((total, width // 2, 128), jnp.bfloat16),
                 half, half, half, half,
-                pltpu.SemaphoreType.DMA((1,)),
-                pltpu.SemaphoreType.DMA((len(pieces),)),
+                pltpu.SemaphoreType.DMA(((full + 1) * (len(pieces) + 1),)),
             ],
         ),
         compiler_params=pltpu.CompilerParams(vmem_limit_bytes=60 * 2**20),
@@ -139,15 +176,15 @@
     ov_dev, width = intersections.shape[0], integrals.shape[-1]
     count = coupling_list.shape[1]
     strip = width // coup
-    lanes = -width % 128
+    lead = -(-strip // 2 // 16) * 16
 
     half = ov_dev // 2
-    padded = jnp.pad(intersections, ((0, 0), (0, 0), (0, lanes)))
-    low, high = padded[:half], padded[half:]
+    packed = pack(intersections, width // 2)
+    low, high = packed[:half], packed[half:]
     last_low, next_high = shift(low, 1), shift(high, -1)
     last_high, next_low = shift(high, 1), shift(low, -1)
     far_low, far_high = shift(last_low, 1), shift(next_high, -1)
-    pieces = (padded, next_low, next_high, far_low, far_high, last_low, last_high)
+    pieces = (packed, next_low, next_high, far_low, far_high, last_low, last_high)
 
     owner_row = lookup(pair_slot, coupling_list[0]) - group_index * coup
     reader_row = lookup(pair_slot, coupling_list[1])
@@ -170,32 +207,33 @@
     asked = source[None, :] == lax.broadcasted_iota(jnp.int32, (groups, count), 0)
     wanted = exchange_wanted(jnp.max(jnp.where(asked, read_pair[None, :], 0), axis=1))
 
-    flipped = jnp.pad(jnp.transpose(integrals[0]), ((0, 0), (0, lanes)))
-    rows_of = lambda d: lax.dynamic_slice_in_dim(flipped, lax.rem(member + d, coup) * strip, strip)
-    sent = [shift(rows_of(coup - e), coup - e) for e in range(1, coup)]
-    integral_strips = jnp.stack([rows_of(0)] + sent)
+    denominator = orbital_energy[:, :, None] + orbital_energy[:, None, :] + pair_energy[:, None, None]
+    own_integrals = integrals.astype(jnp.float32)
+
+    def to_strips(matrix):
+        tiles = pack(jnp.transpose(matrix).reshape(coup, strip, width), lead)
+        part = lambda d: lax.dynamic_index_in_dim(tiles, lax.rem(member + d, coup), keepdims=False)
+        return jnp.stack([part(0)] + [shift(part(coup - e), coup - e) for e in range(1, coup)])
+
+    rounded = to_strips((-own_integrals / denominator).astype(jnp.bfloat16)[0])
+    integral_strips = to_strips(integrals[0])
     energies = jnp.concatenate([orbital_energy[0], pair_energy])[None]
     energies = jnp.concatenate([energies] + [shift(energies, -e) for e in range(1, coup)])
     orbital, pair = energies[:, :width], energies[:, width]
     own_rows = lax.dynamic_slice_in_dim(orbital, strip_row, strip, axis=1)
-    all_columns = jnp.pad(orbital, ((0, 0), (0, lanes)))
-    strip_denominator = own_rows[:, :, None] + all_columns[:, None, :] + pair[:, None, None]
-    integral_f = integral_strips.astype(jnp.float32)
-    amplitudes = -integral_f / strip_denominator
+    strip_denominator = pack(own_rows[:, :, None] + orbital[:, None, :] + pair[:, None, None], lead)
     wanted = (wanted - member) % coup
 
     for iteration in range(ITERS):
-        rounded = amplitudes.astype(jnp.bfloat16)
         outgoing = rounded.at[wanted].get(mode="promise_in_bounds")
         arrived = lax.all_to_all(outgoing, PAIRS, 0, 0, tiled=True)
         last = iteration == ITERS - 1
-        kept, *parts = couple(sched, weights, arrived, pieces, coup, not last)
+        kept, *parts = couple(sched, weights, arrived, pieces, coup, strip, width, not last)
         coupled = sum_parts(kept, parts)
         if not last:
-            coupled = jnp.pad(coupled, ((0, 0), (0, 0), (0, lanes)))
-            amplitudes = -(integral_f + coupled) / strip_denominator
-    denominator = orbital_energy[:, :, None] + orbital_energy[:, None, :] + pair_energy[:, None, None]
-    return -(integrals.astype(jnp.float32) + jnp.transpose(coupled)[None]) / denominator
+            amplitudes = -(integral_strips.astype(jnp.float32) + coupled) / strip_denominator
+            rounded = amplitudes.astype(jnp.bfloat16)
+    return -(own_integrals + jnp.transpose(coupled)[None]) / denominator
 
 
 def solution(mesh):

time: 273 us -> 252 us (0.923)
  waiting for transfers between devices: 104 us -> 90.5 us
  blocking collectives: 56 us -> 49 us
    ppermute x18 -> x21, waiting for transfers between devices: 96 us -> 84.2 us  [shift(): lax.ppermute(x, 'coup', [(i, (i + step) % peers) for i in range(peers)])]
    all_to_all x1 -> x0, blocking collectives: 3.69 us -> none  [exchange_wanted(): tiles = lax.all_to_all(tiles, 'pairs_2', 1, 1, tiled=True)]
    all_to_all x1, blocking collectives: 52.3 us -> 49 us  [amplitudes_of(): arrived = lax.all_to_all(outgoing, PAIRS, 0, 0, tiled=True)]
    ppermute x18 -> x21, starting transfers between devices: 27.1 us -> 26.7 us  [shift(): lax.ppermute(x, 'coup', [(i, (i + step) % peers) for i in range(peers)])]
  transfers between devices with their start and end apart: 20 -> 23, of which waited for: 11 -> 10; matrix products, arithmetic and copies ran while one was open for 4% -> 3% of each run, Pallas kernels for 0% -> 10%
where the time goes in v4:
time: 252 us
  waiting for transfers between devices  90.5 us (36%)
  Pallas kernels  50.8 us (20%)
  blocking collectives  49 us (19%)
  starting transfers between devices  40.8 us (16%)
  local copies, waits for them, and re-layouts  12.6 us (5%)
  other arithmetic  6.89 us (3%)
    ppermute x21, waiting for transfers between devices, shift(): lax.ppermute(x, 'coup', [(i, (i + step) % peers) for i in range(peers)])  84.2 us
    pallas_call x2, Pallas kernels, couple(): pl.pallas_call(functools.partial(couple_kernel, slices), out_shape=[jax.S...  50.8 us
    all_to_all x1, blocking collectives, amplitudes_of(): arrived = lax.all_to_all(outgoing, PAIRS, 0, 0, tiled=True)  49 us
    ppermute x21, starting transfers between devices, shift(): lax.ppermute(x, 'coup', [(i, (i + step) % peers) for i in range(peers)])  26.7 us
    all_to_all x1, starting transfers between devices, exchange_wanted(): lax.all_to_all(wanted_here[:, None, None], PAIRS, 0, 0, tiled=True)[:, 0, 0]  8.34 us
    all_to_all x1, waiting for transfers between devices, exchange_wanted(): lax.all_to_all(wanted_here[:, None, None], PAIRS, 0, 0, tiled=True)[:, 0, 0]  6.36 us
    all_to_all x1, starting transfers between devices, amplitudes_of(): arrived = lax.all_to_all(outgoing, PAIRS, 0, 0, tiled=True)  5.77 us
    gather x2, local copies, waits for them, and re-layouts, amplitudes_of(): outgoing = rounded.at[wanted].get(mode='promise_in_bounds')  5.39 us
  transfers between devices with their start and end apart: 23, of which 10 were waited for; matrix products, arithmetic and copies ran while one was open for 3% of the time, Pallas kernels for 10%

profile of v4, /device:TPU:0, one launch (start us, length us, event | category | flops | bytes accessed | tf_op | source)
XLA Modules:
  0.0 251.7 jit_solution(14726112039578636713)
XLA Ops:
  0.7 1.2 copy.27
  1.9 1.0 fusion.1
  3.2 2.9 %collective-permute-start.3 = (bf16[400,128]{1,0:T(8,128)(2,1)S(1)}, bf16[400,128]{1,0:T(8,128)(2,1)S(1)}, u32[]{:S(2)}, u32[]{:S(2)}) collective-permute-start(bf16[400,128]{1,0:T(8,128)(2,1)S(1)} %get-tuple-element.54), channel_id=1, source_target_pairs={{0,3},{1,0},{2,1},{3,2},{4,7},{5,4},{6,5},{7,6},{8,11},{9,8},{10,9... | collective-permute-start | bytes 307208 | tf_op jit(solution)/shard_map/ppermute | solution.py:24
  6.1 0.8 collective-permute-start.4
  6.9 0.2 select_reduce_fusion.2
  7.3 0.7 copy.29
  8.0 8.3 %all-to-all-start = ((s32[32,1,1]{2,1,0:T(1,128)}), s32[32,1,1]{2,1,0:T(1,128)S(1)}, u32[]{:S(2)}, u32[]{:S(2)}) async-start(s32[32,1,1]{2,1,0:T(1,128)} %copy.29), calls=%async_computation | async-start | bytes 32768 | tf_op jit(solution)/shard_map/all_to_all | solution.py:28
  16.3 1.0 collective-permute-start.5
  17.3 6.4 %all-to-all-done = s32[32,1,1]{2,1,0:T(1,128)S(1)} async-done(((s32[32,1,1]{2,1,0:T(1,128)}), s32[32,1,1]{2,1,0:T(1,128)S(1)}, u32[]{:S(2)}, u32[]{:S(2)}) %all-to-all-start) | async-done | bytes 160 | tf_op jit(solution)/shard_map/all_to_all | solution.py:28
  23.6 0.7 subtract_reduce_fusion
  24.4 2.7 %gather_fusion = bf16[32,400,128]{2,1,0:T(8,128)(2,1)} fusion(bf16[4,400,128]{2,1,0:T(8,128)(2,1)S(1)} %pad_maximum_fusion, s32[1024]{0:T(1024)S(1)} %pad_clamp_fusion), kind=kCustom, calls=%fused_computation | custom fusion | bytes 6553728 | tf_op jit(solution)/shard_map/gather | solution.py:228
  27.1 5.8 %all-to-all-start.1 = ((bf16[32,400,128]{2,1,0:T(8,128)(2,1)}), bf16[32,400,128]{2,1,0:T(8,128)(2,1)}, u32[]{:S(2)}, u32[]{:S(2)}) async-start(bf16[32,400,128]{2,1,0:T(8,128)(2,1)} %gather_fusion), calls=%async_computation.1 | async-start | bytes 6553600 | tf_op jit(solution)/shard_map/all_to_all | solution.py:229
  33.0 0.3 fusion.10
  33.3 0.2 maximum_maximum_fusion.o_own
  33.5 1.4 fusion.12
  34.9 0.3 collective-permute-start.7
  35.3 1.7 collective-permute-start.11
  37.0 3.2 %collective-permute-start.6 = (bf16[2,1568,128]{2,1,0:T(8,128)(2,1)}, bf16[2,1568,128]{2,1,0:T(8,128)(2,1)}, u32[]{:S(2)}, u32[]{:S(2)}) collective-permute-start(bf16[2,1568,128]{2,1,0:T(8,128)(2,1)} %get-tuple-element.31), channel_id=1, source_target_pairs={{0,3},{1,0},{2,1},{3,2},{4,7},{5,4},{6,5},{7,6},{8,11},{9,8},{10,9... | collective-permute-start | bytes 2408456 | tf_op jit(solution)/shard_map/ppermute | solution.py:24
  40.3 0.3 collective-permute-start.15
  40.6 1.2 copy.28
  42.2 13.7 %collective-permute-done.7.o_2 = bf16[2,1568,128]{2,1,0:T(8,128)(2,1)S(1)} collective-permute-done((bf16[2,1568,128]{2,1,0:T(8,128)(2,1)}, bf16[2,1568,128]{2,1,0:T(8,128)(2,1)S(1)}, u32[]{:S(2)}, u32[]{:S(2)}) %collective-permute-start.7) | collective-permute-done | bytes 802848 | tf_op jit(solution)/shard_map/ppermute | solution.py:24
  55.9 1.6 collective-permute-start.10
  57.4 16.3 %collective-permute-done.8.o_5 = bf16[2,1568,128]{2,1,0:T(8,128)(2,1)} collective-permute-done((bf16[2,1568,128]{2,1,0:T(8,128)(2,1)}, bf16[2,1568,128]{2,1,0:T(8,128)(2,1)}, u32[]{:S(2)}, u32[]{:S(2)}) %collective-permute-start.8) | collective-permute-done | bytes 802848 | tf_op jit(solution)/shard_map/ppermute | solution.py:24
  73.7 0.5 collective-permute-start.9
  74.2 1.9 collective-permute-start.16
  76.2 16.8 %collective-permute-done.16 = f32[1,449]{1,0:T(1,128)S(1)} collective-permute-done((f32[1,449]{1,0:T(1,128)S(1)}, f32[1,449]{1,0:T(1,128)S(1)}, u32[]{:S(2)}, u32[]{:S(2)}) %collective-permute-start.16) | collective-permute-done | bytes 1828 | tf_op jit(solution)/shard_map/ppermute | solution.py:24
  93.1 0.6 select_reduce_fusion.weights
  93.7 0.7 concatenate.33.sched
  94.4 3.5 %collective-permute-done.17 = f32[1,449]{1,0:T(1,128)S(1)} collective-permute-done((f32[1,449]{1,0:T(1,128)S(1)}, f32[1,449]{1,0:T(1,128)S(1)}, u32[]{:S(2)}, u32[]{:S(2)}) %collective-permute-start.17) | collective-permute-done | bytes 1828 | tf_op jit(solution)/shard_map/ppermute | solution.py:24
  97.9 0.2 maximum_reduce_fusion
  98.3 0.9 collective-permute-start.1
  99.3 25.3 %couple_strips.1 = (f32[4,400,128]{2,1,0:T(8,128)}, bf16[4,400,128]{2,1,0:T(8,128)(2,1)}, bf16[4,400,128]{2,1,0:T(8,128)(2,1)}, bf16[4,400,128]{2,1,0:T(8,128)(2,1)}) custom-call(s32[131]{0:T(256)} %concatenate.33.sched, f32[64]{0:T(128)} %select_reduce_fusion.weights, bf16[32,400,128]{2,1,0:T(8,128)(2,1)} %all-to-all-done.1.t_hbm, ...), custom_call_target="tpu_custom_call" | custom-call | tf_op jit(solution)/shard_map/couple_strips/pallas_call | solution.py:140
  124.6 1.3 collective-permute-start.12
  125.9 4.3 %collective-permute-start.13 = (bf16[4,400,128]{2,1,0:T(8,128)(2,1)}, bf16[4,400,128]{2,1,0:T(8,128)(2,1)S(1)}, u32[]{:S(2)}, u32[]{:S(2)}) collective-permute-start(bf16[4,400,128]{2,1,0:T(8,128)(2,1)} %get-tuple-element.15), channel_id=1, source_target_pairs={{0,2},{1,3},{2,0},{3,1},{4,6},{5,7},{6,4},{7,5},{8,10},{9,11},{10,... | collective-permute-start | bytes 1228808 | tf_op jit(solution)/shard_map/ppermute | solution.py:24
  130.3 2.1 collective-permute-start.2
  132.4 9.9 %collective-permute-done.2 = bf16[400,128]{1,0:T(8,128)(2,1)S(1)} collective-permute-done((bf16[400,128]{1,0:T(8,128)(2,1)S(1)}, bf16[400,128]{1,0:T(8,128)(2,1)S(1)}, u32[]{:S(2)}, u32[]{:S(2)}) %collective-permute-start.2) | collective-permute-done | bytes 102432 | tf_op jit(solution)/shard_map/ppermute | solution.py:24
  142.3 3.4 %collective-permute-done.13 = bf16[4,400,128]{2,1,0:T(8,128)(2,1)S(1)} collective-permute-done((bf16[4,400,128]{2,1,0:T(8,128)(2,1)}, bf16[4,400,128]{2,1,0:T(8,128)(2,1)S(1)}, u32[]{:S(2)}, u32[]{:S(2)}) %collective-permute-start.13) | collective-permute-done | bytes 409632 | tf_op jit(solution)/shard_map/ppermute | solution.py:24
  145.7 1.5 fusion.4
  147.2 2.7 %gather_fusion.1 = bf16[32,400,128]{2,1,0:T(8,128)(2,1)} fusion(bf16[4,400,128]{2,1,0:T(8,128)(2,1)S(1)} %fusion.4, s32[1024]{0:T(1024)S(1)} %pad_clamp_fusion), kind=kCustom, calls=%fused_computation.1 | custom fusion | bytes 6553728 | tf_op jit(solution)/shard_map/gather | solution.py:228
  149.9 49.0 %all_to_all.15.t_hbm = bf16[32,400,128]{2,1,0:T(8,128)(2,1)} all-to-all(bf16[32,400,128]{2,1,0:T(8,128)(2,1)} %gather_fusion.1), channel_id=1, replica_groups=mesh['pairs_0'=4,'pairs_1'=4,'pairs_2'=2,'coup'=4] {'pairs_0','pairs_1',..., dimensions={0} | all-to-all | bytes 6553600 | tf_op jit(solution)/shard_map/all_to_all | solution.py:229
  198.9 25.4 %couple_pairs.1 = (f32[448,448]{1,0:T(8,128)}, bf16[448,448]{1,0:T(8,128)(2,1)}, bf16[448,448]{1,0:T(8,128)(2,1)}, bf16[448,448]{1,0:T(8,128)(2,1)}) custom-call(s32[131]{0:T(256)} %concatenate.33.sched, f32[64]{0:T(128)} %select_reduce_fusion.weights, bf16[32,400,128]{2,1,0:T(8,128)(2,1)} %all_to_all.15.t_hbm, bf16[4,1568,128]{2,1,0:T(8,128)(2,1)} %copy-done, ...), custom_call_target="tpu_custom_call" | custom-call | tf_op jit(solution)/shard_map/couple_pairs/pallas_call | solution.py:140
  224.5 3.4 %collective-permute-start.19 = (bf16[448,448]{1,0:T(8,128)(2,1)}, bf16[448,448]{1,0:T(8,128)(2,1)S(1)}, u32[]{:S(2)}, u32[]{:S(2)}) collective-permute-start(bf16[448,448]{1,0:T(8,128)(2,1)} %get-tuple-element.19), channel_id=1, source_target_pairs={{0,2},{1,3},{2,0},{3,1},{4,6},{5,7},{6,4},{7,5},{8,10},{9,11},{10,... | collective-permute-start | bytes 1204232 | tf_op jit(solution)/shard_map/ppermute | solution.py:24
  227.8 0.4 collective-permute-start.20
  228.2 10.9 %collective-permute-done.18 = bf16[448,448]{1,0:T(8,128)(2,1)S(1)} collective-permute-done((bf16[448,448]{1,0:T(8,128)(2,1)}, bf16[448,448]{1,0:T(8,128)(2,1)S(1)}, u32[]{:S(2)}, u32[]{:S(2)}) %collective-permute-start.18) | collective-permute-done | bytes 401440 | tf_op jit(solution)/shard_map/ppermute | solution.py:24
  239.1 9.2 %collective-permute-done.19 = bf16[448,448]{1,0:T(8,128)(2,1)S(1)} collective-permute-done((bf16[448,448]{1,0:T(8,128)(2,1)}, bf16[448,448]{1,0:T(8,128)(2,1)S(1)}, u32[]{:S(2)}, u32[]{:S(2)}) %collective-permute-start.19) | collective-permute-done | bytes 401440 | tf_op jit(solution)/shard_map/ppermute | solution.py:24
  248.4 0.5 collective-permute-done.20
  248.9 1.6 fusion.3
  250.5 1.2 copy.30
  (56 shorter events, 1.6 us)
Async XLA Ops:
  0.0 6.9 %copy-start.4 = (s32[3,64]{1,0:T(4,128)S(1)}, s32[3,64]{1,0:T(4,128)}, u32[]{:S(2)}) copy-start(s32[3,64]{1,0:T(4,128)} %param.7) | copy-start | bytes 2308
  0.0 6.9 %copy-start.5 = (s32[128]{0:T(128)S(1)}, s32[128]{0:T(128)}, u32[]{:S(2)}) copy-start(s32[128]{0:T(128)} %param.8) | copy-start | bytes 1540
  3.2 21.1 %collective-permute-start.3 = (bf16[400,128]{1,0:T(8,128)(2,1)S(1)}, bf16[400,128]{1,0:T(8,128)(2,1)S(1)}, u32[]{:S(2)}, u32[]{:S(2)}) collective-permute-start(bf16[400,128]{1,0:T(8,128)(2,1)S(1)} %get-tuple-element.54), channel_id=1, source_target_pairs={{0,3},{1,0},{2,1},{3,2},{4,7},{5,4},{6,5},{7,6},{8,11},{9,8},{10,9... | collective-permute-start | bytes 307208 | tf_op jit(solution)/shard_map/ppermute | solution.py:24
  6.1 18.2 %collective-permute-start.4 = (bf16[400,128]{1,0:T(8,128)(2,1)S(1)}, bf16[400,128]{1,0:T(8,128)(2,1)S(1)}, u32[]{:S(2)}, u32[]{:S(2)}) collective-permute-start(bf16[400,128]{1,0:T(8,128)(2,1)S(1)} %get-tuple-element.53), channel_id=1, source_target_pairs={{0,2},{1,3},{2,0},{3,1},{4,6},{5,7},{6,4},{7,5},{8,10},{9,11},{10,... | collective-permute-start | bytes 307208 | tf_op jit(solution)/shard_map/ppermute | solution.py:24
  8.0 15.7 %all-to-all-start = ((s32[32,1,1]{2,1,0:T(1,128)}), s32[32,1,1]{2,1,0:T(1,128)S(1)}, u32[]{:S(2)}, u32[]{:S(2)}) async-start(s32[32,1,1]{2,1,0:T(1,128)} %copy.29), calls=%async_computation | async-start | bytes 32768 | tf_op jit(solution)/shard_map/all_to_all | solution.py:28
  16.3 8.0 %collective-permute-start.5 = (bf16[400,128]{1,0:T(8,128)(2,1)S(1)}, bf16[400,128]{1,0:T(8,128)(2,1)S(1)}, u32[]{:S(2)}, u32[]{:S(2)}) collective-permute-start(bf16[400,128]{1,0:T(8,128)(2,1)S(1)} %get-tuple-element.52), channel_id=1, source_target_pairs={{0,1},{1,2},{2,3},{3,0},{4,5},{5,6},{6,7},{7,4},{8,9},{9,10},{10,1... | collective-permute-start | bytes 307208 | tf_op jit(solution)/shard_map/ppermute | solution.py:24
  27.1 5.8 %copy-start.2 = (bf16[4,448,448]{2,1,0:T(8,128)(2,1)S(1)}, bf16[4,448,448]{2,1,0:T(8,128)(2,1)}, u32[]{:S(2)}) copy-start(bf16[4,448,448]{2,1,0:T(8,128)(2,1)} %param.13) | copy-start | bytes 4816900
  27.1 72.2 %all-to-all-start.1 = ((bf16[32,400,128]{2,1,0:T(8,128)(2,1)}), bf16[32,400,128]{2,1,0:T(8,128)(2,1)}, u32[]{:S(2)}, u32[]{:S(2)}) async-start(bf16[32,400,128]{2,1,0:T(8,128)(2,1)} %gather_fusion), calls=%async_computation.1 | async-start | bytes 6553600 | tf_op jit(solution)/shard_map/all_to_all | solution.py:229
  33.3 6.9 %copy-start.3 = (f32[1,448]{1,0:T(1,128)S(1)}, f32[1,448]{1,0:T(1,128)}, u32[]{:S(2)}) copy-start(f32[1,448]{1,0:T(1,128)} %param.11) | copy-start | bytes 5380
  33.5 40.7 %copy-start = (bf16[4,1568,128]{2,1,0:T(8,128)(2,1)}, bf16[4,1568,128]{2,1,0:T(8,128)(2,1)S(1)}, u32[]{:S(2)}) copy-start(bf16[4,1568,128]{2,1,0:T(8,128)(2,1)S(1)} %maximum_maximum_fusion.o_own) | copy-start | bytes 4816900
  33.5 59.6 %copy-start.6 = (f32[64]{0:T(128)S(1)}, f32[64]{0:T(128)}, u32[]{:S(2)}) copy-start(f32[64]{0:T(128)} %param.9) | copy-start | bytes 772
  34.9 21.0 %collective-permute-start.7 = (bf16[2,1568,128]{2,1,0:T(8,128)(2,1)}, bf16[2,1568,128]{2,1,0:T(8,128)(2,1)S(1)}, u32[]{:S(2)}, u32[]{:S(2)}) collective-permute-start(bf16[2,1568,128]{2,1,0:T(8,128)(2,1)} %get-tuple-element.30), channel_id=1, source_target_pairs={{0,3},{1,0},{2,1},{3,2},{4,7},{5,4},{6,5},{7,6},{8,11},{9,8},{10,9... | collective-permute-start | bytes 2408456 | tf_op jit(solution)/shard_map/ppermute | solution.py:24
  35.3 63.1 %collective-permute-start.11 = (bf16[2,1568,128]{2,1,0:T(8,128)(2,1)}, bf16[2,1568,128]{2,1,0:T(8,128)(2,1)}, u32[]{:S(2)}, u32[]{:S(2)}) collective-permute-start(bf16[2,1568,128]{2,1,0:T(8,128)(2,1)} %get-tuple-element.30), channel_id=1, source_target_pairs={{0,1},{1,2},{2,3},{3,0},{4,5},{5,6},{6,7},{7,4},{8,9},{9,10},{10,1... | collective-permute-start | bytes 2408456 | tf_op jit(solution)/shard_map/ppermute | solution.py:24
  36.9 36.8 %collective-permute-start.8 = (bf16[2,1568,128]{2,1,0:T(8,128)(2,1)}, bf16[2,1568,128]{2,1,0:T(8,128)(2,1)}, u32[]{:S(2)}, u32[]{:S(2)}) collective-permute-start(bf16[2,1568,128]{2,1,0:T(8,128)(2,1)} %get-tuple-element.31), channel_id=1, source_target_pairs={{0,1},{1,2},{2,3},{3,0},{4,5},{5,6},{6,7},{7,4},{8,9},{9,10},{10,1... | collective-permute-start | bytes 2408456 | tf_op jit(solution)/shard_map/ppermute | solution.py:24
  37.0 62.3 %collective-permute-start.6 = (bf16[2,1568,128]{2,1,0:T(8,128)(2,1)}, bf16[2,1568,128]{2,1,0:T(8,128)(2,1)}, u32[]{:S(2)}, u32[]{:S(2)}) collective-permute-start(bf16[2,1568,128]{2,1,0:T(8,128)(2,1)} %get-tuple-element.31), channel_id=1, source_target_pairs={{0,3},{1,0},{2,1},{3,2},{4,7},{5,4},{6,5},{7,6},{8,11},{9,8},{10,9... | collective-permute-start | bytes 2408456 | tf_op jit(solution)/shard_map/ppermute | solution.py:24
  40.3 34.0 %collective-permute-start.15 = (f32[1,449]{1,0:T(1,128)S(1)}, f32[1,449]{1,0:T(1,128)S(1)}, u32[]{:S(2)}, u32[]{:S(2)}) collective-permute-start(f32[1,449]{1,0:T(1,128)S(1)} %bitcast.67), channel_id=1, source_target_pairs={{0,3},{1,0},{2,1},{3,2},{4,7},{5,4},{6,5},{7,6},{8,11},{9,8},{10,9... | collective-permute-start | bytes 5396 | tf_op jit(solution)/shard_map/ppermute | solution.py:24
  55.9 43.4 %copy-start.1 = (bf16[2,1568,128]{2,1,0:T(8,128)(2,1)}, bf16[2,1568,128]{2,1,0:T(8,128)(2,1)S(1)}, u32[]{:S(2)}) copy-start(bf16[2,1568,128]{2,1,0:T(8,128)(2,1)S(1)} %collective-permute-done.7.o_2) | copy-start | bytes 2408452
  55.9 43.4 %collective-permute-start.10 = (bf16[2,1568,128]{2,1,0:T(8,128)(2,1)S(1)}, bf16[2,1568,128]{2,1,0:T(8,128)(2,1)}, u32[]{:S(2)}, u32[]{:S(2)}) collective-permute-start(bf16[2,1568,128]{2,1,0:T(8,128)(2,1)S(1)} %collective-permute-done.7.o_2), channel_id=1, source_target_pairs={{0,3},{1,0},{2,1},{3,2},{4,7},{5,4},{6,5},{7,6},{8,11},{9,8},{10,9... | collective-permute-start | bytes 2408456 | tf_op jit(solution)/shard_map/ppermute | solution.py:24
  73.7 25.6 %collective-permute-start.9 = (bf16[2,1568,128]{2,1,0:T(8,128)(2,1)}, bf16[2,1568,128]{2,1,0:T(8,128)(2,1)}, u32[]{:S(2)}, u32[]{:S(2)}) collective-permute-start(bf16[2,1568,128]{2,1,0:T(8,128)(2,1)} %collective-permute-done.8.o_5), channel_id=1, source_target_pairs={{0,1},{1,2},{2,3},{3,0},{4,5},{5,6},{6,7},{7,4},{8,9},{9,10},{10,1... | collective-permute-start | bytes 2408456 | tf_op jit(solution)/shard_map/ppermute | solution.py:24
  74.2 18.8 %collective-permute-start.16 = (f32[1,449]{1,0:T(1,128)S(1)}, f32[1,449]{1,0:T(1,128)S(1)}, u32[]{:S(2)}, u32[]{:S(2)}) collective-permute-start(f32[1,449]{1,0:T(1,128)S(1)} %bitcast.68), channel_id=1, source_target_pairs={{0,2},{1,3},{2,0},{3,1},{4,6},{5,7},{6,4},{7,5},{8,10},{9,11},{10,... | collective-permute-start | bytes 5396 | tf_op jit(solution)/shard_map/ppermute | solution.py:24
  93.1 4.8 %collective-permute-start.17 = (f32[1,449]{1,0:T(1,128)S(1)}, f32[1,449]{1,0:T(1,128)S(1)}, u32[]{:S(2)}, u32[]{:S(2)}) collective-permute-start(f32[1,449]{1,0:T(1,128)S(1)} %bitcast.69), channel_id=1, source_target_pairs={{0,1},{1,2},{2,3},{3,0},{4,5},{5,6},{6,7},{7,4},{8,9},{9,10},{10,1... | collective-permute-start | bytes 5396 | tf_op jit(solution)/shard_map/ppermute | solution.py:24
  97.9 32.4 %collective-permute-start = (bf16[400,128]{1,0:T(8,128)(2,1)S(1)}, bf16[400,128]{1,0:T(8,128)(2,1)S(1)}, u32[]{:S(2)}, u32[]{:S(2)}) collective-permute-start(bf16[400,128]{1,0:T(8,128)(2,1)S(1)} %get-tuple-element.50), channel_id=1, source_target_pairs={{0,3},{1,0},{2,1},{3,2},{4,7},{5,4},{6,5},{7,6},{8,11},{9,8},{10,9... | collective-permute-start | bytes 307208 | tf_op jit(solution)/shard_map/ppermute | solution.py:24
  98.3 34.1 %collective-permute-start.1 = (bf16[400,128]{1,0:T(8,128)(2,1)S(1)}, bf16[400,128]{1,0:T(8,128)(2,1)S(1)}, u32[]{:S(2)}, u32[]{:S(2)}) collective-permute-start(bf16[400,128]{1,0:T(8,128)(2,1)S(1)} %get-tuple-element.49), channel_id=1, source_target_pairs={{0,2},{1,3},{2,0},{3,1},{4,6},{5,7},{6,4},{7,5},{8,10},{9,11},{10,... | collective-permute-start | bytes 307208 | tf_op jit(solution)/shard_map/ppermute | solution.py:24
  124.6 17.7 %collective-permute-start.12 = (bf16[4,400,128]{2,1,0:T(8,128)(2,1)}, bf16[4,400,128]{2,1,0:T(8,128)(2,1)S(1)}, u32[]{:S(2)}, u32[]{:S(2)}) collective-permute-start(bf16[4,400,128]{2,1,0:T(8,128)(2,1)} %get-tuple-element.14), channel_id=1, source_target_pairs={{0,1},{1,2},{2,3},{3,0},{4,5},{5,6},{6,7},{7,4},{8,9},{9,10},{10,1... | collective-permute-start | bytes 1228808 | tf_op jit(solution)/shard_map/ppermute | solution.py:24
  125.9 19.8 %collective-permute-start.13 = (bf16[4,400,128]{2,1,0:T(8,128)(2,1)}, bf16[4,400,128]{2,1,0:T(8,128)(2,1)S(1)}, u32[]{:S(2)}, u32[]{:S(2)}) collective-permute-start(bf16[4,400,128]{2,1,0:T(8,128)(2,1)} %get-tuple-element.15), channel_id=1, source_target_pairs={{0,2},{1,3},{2,0},{3,1},{4,6},{5,7},{6,4},{7,5},{8,10},{9,11},{10,... | collective-permute-start | bytes 1228808 | tf_op jit(solution)/shard_map/ppermute | solution.py:24
  130.2 15.4 %collective-permute-start.14 = (bf16[4,400,128]{2,1,0:T(8,128)(2,1)}, bf16[4,400,128]{2,1,0:T(8,128)(2,1)S(1)}, u32[]{:S(2)}, u32[]{:S(2)}) collective-permute-start(bf16[4,400,128]{2,1,0:T(8,128)(2,1)} %get-tuple-element.16), channel_id=1, source_target_pairs={{0,3},{1,0},{2,1},{3,2},{4,7},{5,4},{6,5},{7,6},{8,11},{9,8},{10,9... | collective-permute-start | bytes 1228808 | tf_op jit(solution)/shard_map/ppermute | solution.py:24
  130.3 12.0 %collective-permute-start.2 = (bf16[400,128]{1,0:T(8,128)(2,1)S(1)}, bf16[400,128]{1,0:T(8,128)(2,1)S(1)}, u32[]{:S(2)}, u32[]{:S(2)}) collective-permute-start(bf16[400,128]{1,0:T(8,128)(2,1)S(1)} %get-tuple-element.48), channel_id=1, source_target_pairs={{0,1},{1,2},{2,3},{3,0},{4,5},{5,6},{6,7},{7,4},{8,9},{9,10},{10,1... | collective-permute-start | bytes 307208 | tf_op jit(solution)/shard_map/ppermute | solution.py:24
  224.4 14.7 %collective-permute-start.18 = (bf16[448,448]{1,0:T(8,128)(2,1)}, bf16[448,448]{1,0:T(8,128)(2,1)S(1)}, u32[]{:S(2)}, u32[]{:S(2)}) collective-permute-start(bf16[448,448]{1,0:T(8,128)(2,1)} %get-tuple-element.18), channel_id=1, source_target_pairs={{0,1},{1,2},{2,3},{3,0},{4,5},{5,6},{6,7},{7,4},{8,9},{9,10},{10,1... | collective-permute-start | bytes 1204232 | tf_op jit(solution)/shard_map/ppermute | solution.py:24
  224.5 23.9 %collective-permute-start.19 = (bf16[448,448]{1,0:T(8,128)(2,1)}, bf16[448,448]{1,0:T(8,128)(2,1)S(1)}, u32[]{:S(2)}, u32[]{:S(2)}) collective-permute-start(bf16[448,448]{1,0:T(8,128)(2,1)} %get-tuple-element.19), channel_id=1, source_target_pairs={{0,2},{1,3},{2,0},{3,1},{4,6},{5,7},{6,4},{7,5},{8,10},{9,11},{10,... | collective-permute-start | bytes 1204232 | tf_op jit(solution)/shard_map/ppermute | solution.py:24
  227.8 21.0 %collective-permute-start.20 = (bf16[448,448]{1,0:T(8,128)(2,1)}, bf16[448,448]{1,0:T(8,128)(2,1)S(1)}, u32[]{:S(2)}, u32[]{:S(2)}) collective-permute-start(bf16[448,448]{1,0:T(8,128)(2,1)} %get-tuple-element.20), channel_id=1, source_target_pairs={{0,3},{1,0},{2,1},{3,2},{4,7},{5,4},{6,5},{7,6},{8,11},{9,8},{10,9... | collective-permute-start | bytes 1204232 | tf_op jit(solution)/shard_map/ppermute | solution.py:24

commit v5 on v4

--- a/solution.py
+++ b/solution.py
@@ -36,17 +36,17 @@
     return jnp.concatenate(tiles, axis=-2)
 
 
-def couple_kernel(
-    slices, sched, weights, t_hbm, o_own, o_1, o_2, o_3, o_4, o_5, o_6, kept, out_1, out_2, out_3,
-    acc, t_buf, o_buf, t_tail, o_tail, even_0, even_1, odd_0, odd_1, sems,
-):
+def couple_kernel(distances, slices, unroll, sched, weights, t_hbm, o_own, o_1, o_2, o_3, o_4, o_5, o_6, *refs):
+    outs, refs = refs[: len(distances)], refs[len(distances) :]
+    acc, t_buf, o_buf, t_tail, o_tail, even_0, even_1, odd_0, odd_1, sems = refs
     sources, strip, width = t_buf.shape[0], t_buf.shape[1], o_buf.shape[1]
     full = width // 128
     o_lead, t_lead = o_tail.shape[1], t_tail.shape[1]
     count = 2 * sources
-    offset = pl.multiple_of(sched[2 * count], 16)
-    lane = pl.multiple_of(sched[2 * count + 1], 128)
-    member = sched[2 * count + 2]
+    offset = pl.multiple_of(sched[3 * count], 16)
+    lane = pl.multiple_of(sched[3 * count + 1], 128)
+    member = sched[3 * count + 2]
+    begin, turns = sched[3 * count + 3], sched[3 * count + 4]
     copies, first = [], 0
     for piece in (o_own, o_1, o_2, o_3, o_4, o_5, o_6):
         size = piece.shape[0]
@@ -81,47 +81,48 @@
 
     lax.fori_loop(0, sources // 2, unpack_o, 0)
 
-    def right(h, s, ref):
+    def right(k, ref):
+        k = jnp.minimum(k, count - 1)
         product = lax.dot_general(
-            t_buf[h], o_buf[sched[2 * h + s]], (((1,), (1,)), ((), ())), preferred_element_type=jnp.float32
+            t_buf[sched[2 * count + k]], o_buf[sched[k]], (((1,), (1,)), ((), ())),
+            preferred_element_type=jnp.float32,
         )
         ref[pl.ds(offset, strip), :] = product.astype(jnp.bfloat16)
 
-    def left(h, s, ref):
-        k = 2 * h + s
+    def left(k, ref):
         product = jnp.dot(
             o_buf[sched[k], :, pl.ds(lane, 256)], ref[...], preferred_element_type=jnp.float32
         )
         acc[sched[count + k]] += weights[k] * product
 
-    right(0, 0, even_0)
-    right(0, 1, even_1)
-
-    def step(i, carry):
-        h = 2 * i
-        right(h + 1, 0, odd_0)
-        left(h, 0, even_0)
-        right(h + 1, 1, odd_1)
-        left(h, 1, even_1)
-        after = jnp.minimum(h + 2, sources - 1)
-        right(after, 0, even_0)
-        left(h + 1, 0, odd_0)
-        right(after, 1, even_1)
-        left(h + 1, 1, odd_1)
+    right(begin, even_0)
+    right(begin + 1, even_1)
+
+    def turn(i, carry):
+        for u in range(unroll):
+            k = begin + 4 * (unroll * i + u)
+            right(k + 2, odd_0)
+            left(k, even_0)
+            right(k + 3, odd_1)
+            left(k + 1, even_1)
+            right(k + 4, even_0)
+            left(k + 2, odd_0)
+            right(k + 5, even_1)
+            left(k + 3, odd_1)
         return carry
 
-    lax.fori_loop(0, sources // 2, step, 0)
+    lax.fori_loop(0, turns, turn, 0)
     members = acc.shape[0]
-    for d, out in enumerate((kept, out_1, out_2, out_3)):
+    for d, out in zip(distances, outs):
         peer = lax.rem(member + d, members)
         if slices:
-            begin = pl.multiple_of(peer * strip, 16)
+            rows = pl.ds(pl.multiple_of(peer * strip, 16), strip)
             for r in range(members):
                 row = lax.rem(peer + r, members)
                 for t in range(full):
-                    part = acc[row, pl.ds(begin, strip), 128 * t : 128 * t + 128]
+                    part = acc[row, rows, 128 * t : 128 * t + 128]
                     out[r, strip * t : strip * t + strip, :] = part.astype(out.dtype)
-                tail = acc[row, pl.ds(begin, strip), 128 * full :]
+                tail = acc[row, rows, 128 * full :]
                 out[r, strip * full :, :] = jnp.concatenate(
                     [tail[:t_lead], tail[strip - t_lead :]], axis=1
                 ).astype(out.dtype)
@@ -129,7 +130,7 @@
             out[...] = acc[peer].astype(out.dtype)
 
 
-def couple(sched, weights, strips, pieces, coup, strip, width, slices):
+def couple(sched, weights, strips, pieces, coup, strip, width, distances, slices, unroll):
     sources, packed, _ = strips.shape
     full = width // 128
     lanes = 128 * full + 128
@@ -138,13 +139,13 @@
     whole = pl.BlockSpec(part, lambda i, *_: (0,) * len(part))
     half = pltpu.VMEM((256, width), jnp.bfloat16)
     return pl.pallas_call(
-        functools.partial(couple_kernel, slices),
-        out_shape=[jax.ShapeDtypeStruct(part, jnp.float32)] + [jax.ShapeDtypeStruct(part, jnp.bfloat16)] * 3,
+        functools.partial(couple_kernel, distances, slices, unroll),
+        out_shape=[jax.ShapeDtypeStruct(part, jnp.bfloat16 if d else jnp.float32) for d in distances],
         grid_spec=pltpu.PrefetchScalarGridSpec(
             num_scalar_prefetch=2,
             grid=(1,),
             in_specs=[pl.BlockSpec(memory_space=pl.ANY)] * (1 + len(pieces)),
-            out_specs=[whole] * 4,
+            out_specs=[whole] * len(distances),
             scratch_shapes=[
                 pltpu.VMEM((coup, width, width), jnp.float32),
                 pltpu.VMEM((sources, strip, lanes), jnp.bfloat16),
@@ -156,14 +157,7 @@
             ],
         ),
         compiler_params=pltpu.CompilerParams(vmem_limit_bytes=60 * 2**20),
-        name="couple_strips" if slices else "couple_pairs",
     )(sched, weights, strips, *pieces)
-
-
-def sum_parts(kept, parts):
-    for d, part in enumerate(parts):
-        kept = kept + shift(part, d + 1).astype(jnp.float32)
-    return kept
 
 
 def amplitudes_of(
@@ -197,13 +191,29 @@
     )
     slot = 2 * source + twin
     chosen = slot[None, :] == position[:, None]
-    pick = lambda v: jnp.sum(jnp.where(chosen, v[None, :], jnp.zeros((), v.dtype)), axis=1)
+    pick = lambda chosen, v: jnp.sum(jnp.where(chosen, v[None, :], jnp.zeros((), v.dtype)), axis=1)
     strip_row = member * strip
     lane_tile = jnp.minimum(strip_row // 128, 2) * 128
-    sched = jnp.concatenate(
-        [pick(local_o), pick(owner_row), jnp.stack([strip_row - lane_tile, lane_tile, member])]
-    ).astype(jnp.int32)
-    weights = pick(coupling_weight)
+    place = [strip_row - lane_tile, lane_tile, member]
+
+    def schedule(chosen, *bounds):
+        columns = [pick(chosen, v) for v in (local_o, owner_row, source)]
+        return jnp.concatenate([*columns, jnp.stack([*place, *bounds])]).astype(jnp.int32)
+
+    by_source = schedule(chosen, jnp.int32(0), jnp.int32(count // 16))
+    weights = pick(chosen, coupling_weight)
+    distance = (owner_row - member) % coup
+    outer = (distance == 1) | (distance == 2)
+    before = position[None, :] < position[:, None]
+    ahead = jnp.sum(jnp.where(outer[None, :] & (before | ~outer[:, None]), 1, 0), axis=1)
+    behind = jnp.sum(jnp.where(~outer[None, :] & before, 1, 0), axis=1)
+    chosen = jnp.where(outer, ahead, ahead + behind)[None, :] == position[:, None]
+    outer_count = jnp.sum(jnp.where(outer, 1, 0))
+    outer_turns, inner_begin = (outer_count + 3) // 4, outer_count // 4 * 4
+    by_row_outer = schedule(chosen, jnp.int32(0), outer_turns)
+    by_row_inner = schedule(chosen, inner_begin, (count - inner_begin) // 4)
+    weights_outer = pick(chosen, jnp.where(outer, coupling_weight, 0.0))
+    weights_inner = pick(chosen, jnp.where(outer, 0.0, coupling_weight))
     asked = source[None, :] == lax.broadcasted_iota(jnp.int32, (groups, count), 0)
     wanted = exchange_wanted(jnp.max(jnp.where(asked, read_pair[None, :], 0), axis=1))
 
@@ -224,15 +234,31 @@
     strip_denominator = pack(own_rows[:, :, None] + orbital[:, None, :] + pair[:, None, None], lead)
     wanted = (wanted - member) % coup
 
-    for iteration in range(ITERS):
+    def exchange(rounded):
         outgoing = rounded.at[wanted].get(mode="promise_in_bounds")
         arrived = lax.all_to_all(outgoing, PAIRS, 0, 0, tiled=True)
-        last = iteration == ITERS - 1
-        kept, *parts = couple(sched, weights, arrived, pieces, coup, strip, width, not last)
-        coupled = sum_parts(kept, parts)
-        if not last:
-            amplitudes = -(integral_strips.astype(jnp.float32) + coupled) / strip_denominator
-            rounded = amplitudes.astype(jnp.bfloat16)
+        return pltpu.with_memory_space_constraint(arrived, pltpu.HBM)
+
+    for _ in range(ITERS - 1):
+        arrived = exchange(rounded)
+        kept, *parts = couple(by_source, weights, arrived, pieces, coup, strip, width, (0, 1, 2, 3), True, 4)
+        for d, part in enumerate(parts):
+            kept = kept + shift(part, d + 1).astype(jnp.float32)
+        amplitudes = -(integral_strips.astype(jnp.float32) + kept) / strip_denominator
+        rounded = amplitudes.astype(jnp.bfloat16)
+
+    arrived = exchange(rounded)
+    part_2, part_1 = couple(
+        by_row_outer, weights_outer, arrived, pieces, coup, strip, width, (2, 1), False, 1
+    )
+    part_2, part_1 = shift(part_2, 2), shift(part_1, 1)
+    part_3, kept = couple(
+        by_row_inner, weights_inner, arrived, pieces, coup, strip, width, (3, 0), False, 1
+    )
+    part_3 = shift(part_3, 3)
+    coupled = kept
+    for part in (part_1, part_2, part_3):
+        coupled = coupled + part.astype(jnp.float32)
     return -(own_integrals + jnp.transpose(coupled)[None]) / denominator
 
 

time: 252 us -> 257 us (1.020)
  blocking collectives: 49 us -> 0 us
  waiting for transfers between devices: 90.5 us -> 117 us
  starting transfers between devices: 40.8 us -> 48 us
  local copies, waits for them, and re-layouts: 12.6 us -> 19.5 us
  Pallas kernels: 50.8 us -> 57.5 us
  other arithmetic: 6.89 us -> 10.3 us
  between operations: 1.05 us -> 4.31 us
    all_to_all x1 -> x0, blocking collectives: 49 us -> none  [amplitudes_of(): arrived = lax.all_to_all(outgoing, PAIRS, 0, 0, tiled=True)]
    all_to_all x1 -> x2, waiting for transfers between devices: 0.01 us -> 36.3 us  [exchange(): arrived = lax.all_to_all(outgoing, PAIRS, 0, 0, tiled=True)]
    ppermute x21, waiting for transfers between devices: 84.2 us -> 74 us  [shift(): lax.ppermute(x, 'coup', [(i, (i + step) % peers) for i in range(peers)])]
    all_to_all x1 -> x2, starting transfers between devices: 5.77 us -> 13.3 us  [exchange(): arrived = lax.all_to_all(outgoing, PAIRS, 0, 0, tiled=True)]
    pallas_call x2 -> x3, Pallas kernels: 50.8 us -> 57.5 us  [couple(): pl.pallas_call(functools.partial(couple_kernel, distances, slices, unroll...]
  transfers between devices with their start and end apart: 23 -> 24, of which waited for: 10 -> 10; matrix products, arithmetic and copies ran while one was open for 3% -> 6% of each run, Pallas kernels for 10% -> 15%
where the time goes in v5:
time: 257 us; the launch traced here: 256 us
  waiting for transfers between devices  117 us (46%)
  Pallas kernels  57.5 us (22%)
  starting transfers between devices  48 us (19%)
  local copies, waits for them, and re-layouts  19.5 us (8%)
  other arithmetic  10.3 us (4%)
  between operations  4.31 us (2%)
    ppermute x21, waiting for transfers between devices, shift(): lax.ppermute(x, 'coup', [(i, (i + step) % peers) for i in range(peers)])  74 us
    pallas_call x3, Pallas kernels, couple(): pl.pallas_call(functools.partial(couple_kernel, distances, slices, unroll...  57.5 us
    all_to_all x2, waiting for transfers between devices, exchange(): arrived = lax.all_to_all(outgoing, PAIRS, 0, 0, tiled=True)  36.3 us
    ppermute x21, starting transfers between devices, shift(): lax.ppermute(x, 'coup', [(i, (i + step) % peers) for i in range(peers)])  26.4 us
    all_to_all x2, starting transfers between devices, exchange(): arrived = lax.all_to_all(outgoing, PAIRS, 0, 0, tiled=True)  13.3 us
    all_to_all x1, starting transfers between devices, exchange_wanted(): lax.all_to_all(wanted_here[:, None, None], PAIRS, 0, 0, tiled=True)[:, 0, 0]  8.33 us
    all_to_all x1, waiting for transfers between devices, exchange_wanted(): lax.all_to_all(wanted_here[:, None, None], PAIRS, 0, 0, tiled=True)[:, 0, 0]  6.36 us
    gather x2, local copies, waits for them, and re-layouts, exchange(): outgoing = rounded.at[wanted].get(mode='promise_in_bounds')  5.33 us
  transfers between devices with their start and end apart: 24, of which 10 were waited for; matrix products, arithmetic and copies ran while one was open for 6% of the time, Pallas kernels for 15%

profile of v5, /device:TPU:0, one launch (start us, length us, event | category | flops | bytes accessed | tf_op | source)
XLA Modules:
  0.0 256.2 jit_solution(17305331515022501641)
XLA Ops:
  0.7 1.2 copy.27
  1.9 1.0 fusion.1
  3.2 2.9 %collective-permute-start.3 = (bf16[400,128]{1,0:T(8,128)(2,1)S(1)}, bf16[400,128]{1,0:T(8,128)(2,1)S(1)}, u32[]{:S(2)}, u32[]{:S(2)}) collective-permute-start(bf16[400,128]{1,0:T(8,128)(2,1)S(1)} %get-tuple-element.65), channel_id=1, source_target_pairs={{0,3},{1,0},{2,1},{3,2},{4,7},{5,4},{6,5},{7,6},{8,11},{9,8},{10,9... | collective-permute-start | bytes 307208 | tf_op jit(solution)/shard_map/ppermute | solution.py:24
  6.1 0.8 collective-permute-start.4
  7.9 0.7 and_select_fusion.1
  8.7 0.7 copy.29
  9.4 8.3 %all-to-all-start = ((s32[32,1,1]{2,1,0:T(1,128)}), s32[32,1,1]{2,1,0:T(1,128)S(1)}, u32[]{:S(2)}, u32[]{:S(2)}) async-start(s32[32,1,1]{2,1,0:T(1,128)} %copy.29), calls=%async_computation | async-start | bytes 32768 | tf_op jit(solution)/shard_map/all_to_all | solution.py:28
  17.8 1.0 collective-permute-start.5
  18.7 6.4 %all-to-all-done = s32[32,1,1]{2,1,0:T(1,128)S(1)} async-done(((s32[32,1,1]{2,1,0:T(1,128)}), s32[32,1,1]{2,1,0:T(1,128)S(1)}, u32[]{:S(2)}, u32[]{:S(2)}) %all-to-all-start) | async-done | bytes 160 | tf_op jit(solution)/shard_map/all_to_all | solution.py:28
  25.1 0.7 subtract_reduce_fusion
  25.9 2.7 %gather_fusion = bf16[32,400,128]{2,1,0:T(8,128)(2,1)} fusion(bf16[4,400,128]{2,1,0:T(8,128)(2,1)S(1)} %pad_maximum_fusion, s32[1024]{0:T(1024)S(1)} %pad_clamp_fusion), kind=kCustom, calls=%fused_computation | custom fusion | bytes 6553728 | tf_op jit(solution)/shard_map/gather | solution.py:238
  28.6 5.8 %all-to-all-start.1 = ((bf16[32,400,128]{2,1,0:T(8,128)(2,1)}), bf16[32,400,128]{2,1,0:T(8,128)(2,1)}, u32[]{:S(2)}, u32[]{:S(2)}) async-start(bf16[32,400,128]{2,1,0:T(8,128)(2,1)} %gather_fusion), calls=%async_computation.1 | async-start | bytes 6553600 | tf_op jit(solution)/shard_map/all_to_all | solution.py:239
  35.0 1.4 fusion.16
  36.7 1.7 collective-permute-start.11
  38.4 3.2 %collective-permute-start.6 = (bf16[2,1568,128]{2,1,0:T(8,128)(2,1)}, bf16[2,1568,128]{2,1,0:T(8,128)(2,1)}, u32[]{:S(2)}, u32[]{:S(2)}) collective-permute-start(bf16[2,1568,128]{2,1,0:T(8,128)(2,1)} %get-tuple-element.42), channel_id=1, source_target_pairs={{0,3},{1,0},{2,1},{3,2},{4,7},{5,4},{6,5},{7,6},{8,11},{9,8},{10,9... | collective-permute-start | bytes 2408456 | tf_op jit(solution)/shard_map/ppermute | solution.py:24
  42.0 2.0 copy.28
  44.2 0.9 fusion.20
  45.1 1.0 fusion.19
  46.3 11.0 %collective-permute-done.7.o_2 = bf16[2,1568,128]{2,1,0:T(8,128)(2,1)S(1)} collective-permute-done((bf16[2,1568,128]{2,1,0:T(8,128)(2,1)}, bf16[2,1568,128]{2,1,0:T(8,128)(2,1)S(1)}, u32[]{:S(2)}, u32[]{:S(2)}) %collective-permute-start.7) | collective-permute-done | bytes 802848 | tf_op jit(solution)/shard_map/ppermute | solution.py:24
  57.3 1.6 collective-permute-start.10
  58.9 16.3 %collective-permute-done.8.o_5 = bf16[2,1568,128]{2,1,0:T(8,128)(2,1)} collective-permute-done((bf16[2,1568,128]{2,1,0:T(8,128)(2,1)}, bf16[2,1568,128]{2,1,0:T(8,128)(2,1)}, u32[]{:S(2)}, u32[]{:S(2)}) %collective-permute-start.8) | collective-permute-done | bytes 802848 | tf_op jit(solution)/shard_map/ppermute | solution.py:24
  75.6 0.8 select_reduce_fusion.2
  76.4 0.7 constant_dynamic-slice_fusion.2
  77.1 1.8 collective-permute-start.16
  78.9 1.3 select_reduce_fusion.1.weights
  80.2 14.3 %collective-permute-done.16 = f32[1,449]{1,0:T(1,128)S(1)} collective-permute-done((f32[1,449]{1,0:T(1,128)S(1)}, f32[1,449]{1,0:T(1,128)S(1)}, u32[]{:S(2)}, u32[]{:S(2)}) %collective-permute-start.16) | collective-permute-done | bytes 1828 | tf_op jit(solution)/shard_map/ppermute | solution.py:24
  94.5 1.3 concatenate.42.sched
  95.8 3.5 %collective-permute-done.17 = f32[1,449]{1,0:T(1,128)S(1)} collective-permute-done((f32[1,449]{1,0:T(1,128)S(1)}, f32[1,449]{1,0:T(1,128)S(1)}, u32[]{:S(2)}, u32[]{:S(2)}) %collective-permute-start.17) | collective-permute-done | bytes 1828 | tf_op jit(solution)/shard_map/ppermute | solution.py:24
  99.8 0.9 collective-permute-start.1
  100.8 23.5 %shard_map.76 = (f32[4,400,128]{2,1,0:T(8,128)}, bf16[4,400,128]{2,1,0:T(8,128)(2,1)}, bf16[4,400,128]{2,1,0:T(8,128)(2,1)}, bf16[4,400,128]{2,1,0:T(8,128)(2,1)}) custom-call(s32[197]{0:T(256)} %concatenate.42.sched, f32[64]{0:T(128)} %select_reduce_fusion.1.weights, bf16[32,400,128]{2,1,0:T(8,128)(2,1)} %all-to-all-done.1.t_hbm, ...), custom_call_target="tpu_custom_call" | custom-call | tf_op jit(solution)/shard_map/pallas_call | solution.py:141
  124.3 2.0 collective-permute-start.12
  126.3 3.7 %collective-permute-start.13 = (bf16[4,400,128]{2,1,0:T(8,128)(2,1)}, bf16[4,400,128]{2,1,0:T(8,128)(2,1)S(1)}, u32[]{:S(2)}, u32[]{:S(2)}) collective-permute-start(bf16[4,400,128]{2,1,0:T(8,128)(2,1)} %get-tuple-element.15), channel_id=1, source_target_pairs={{0,2},{1,3},{2,0},{3,1},{4,6},{5,7},{6,4},{7,5},{8,10},{9,11},{10,... | collective-permute-start | bytes 1228808 | tf_op jit(solution)/shard_map/ppermute | solution.py:24
  130.0 2.1 collective-permute-start.2
  132.2 10.6 %collective-permute-done.2 = bf16[400,128]{1,0:T(8,128)(2,1)S(1)} collective-permute-done((bf16[400,128]{1,0:T(8,128)(2,1)S(1)}, bf16[400,128]{1,0:T(8,128)(2,1)S(1)}, u32[]{:S(2)}, u32[]{:S(2)}) %collective-permute-start.2) | collective-permute-done | bytes 102432 | tf_op jit(solution)/shard_map/ppermute | solution.py:24
  142.7 2.7 %collective-permute-done.13 = bf16[4,400,128]{2,1,0:T(8,128)(2,1)S(1)} collective-permute-done((bf16[4,400,128]{2,1,0:T(8,128)(2,1)}, bf16[4,400,128]{2,1,0:T(8,128)(2,1)S(1)}, u32[]{:S(2)}, u32[]{:S(2)}) %collective-permute-start.13) | collective-permute-done | bytes 409632 | tf_op jit(solution)/shard_map/ppermute | solution.py:24
  145.4 1.5 fusion.4
  146.9 2.7 %gather_fusion.1 = bf16[32,400,128]{2,1,0:T(8,128)(2,1)} fusion(bf16[4,400,128]{2,1,0:T(8,128)(2,1)S(1)} %fusion.4, s32[1024]{0:T(1024)S(1)} %pad_clamp_fusion), kind=kCustom, calls=%fused_computation.1 | custom fusion | bytes 6553728 | tf_op jit(solution)/shard_map/gather | solution.py:238
  149.6 7.5 %all-to-all-start.2 = ((bf16[32,400,128]{2,1,0:T(8,128)(2,1)}), bf16[32,400,128]{2,1,0:T(8,128)(2,1)S(1)}, u32[]{:S(2)}, u32[]{:S(2)}) async-start(bf16[32,400,128]{2,1,0:T(8,128)(2,1)} %gather_fusion.1), calls=%async_computation.2 | async-start | bytes 6553600 | tf_op jit(solution)/shard_map/all_to_all | solution.py:239
  160.3 0.7 concatenate.51.sched
  162.3 36.3 %all-to-all-done.2.t_hbm = bf16[32,400,128]{2,1,0:T(8,128)(2,1)S(1)} async-done(((bf16[32,400,128]{2,1,0:T(8,128)(2,1)}), bf16[32,400,128]{2,1,0:T(8,128)(2,1)S(1)}, u32[]{:S(2)}, u32[]{:S(2)}) %all-to-all-start.2) | async-done | bytes 3276832 | tf_op jit(solution)/shard_map/all_to_all | solution.py:239
  198.6 1.7 copy-done.1
  200.3 19.5 %shard_map.78 = (bf16[448,448]{1,0:T(8,128)(2,1)}, bf16[448,448]{1,0:T(8,128)(2,1)}) custom-call(s32[197]{0:T(256)} %concatenate.51.sched, f32[64]{0:T(128)} %get-tuple-element.21.weights, bf16[32,400,128]{2,1,0:T(8,128)(2,1)} %copy-done.1, bf16[4,1568,128]{2,1,0:T(8,128)(2,1)} %copy-done, bf16[2,1568,128]{2,1,0:T(8,128)(2,1)} %collective-permute-done.6.o_1, ...), custom_call_target="tpu_custom_call" | custom-call | tf_op jit(solution)/shard_map/pallas_call | solution.py:141
  219.9 3.3 %collective-permute-start.19 = (bf16[448,448]{1,0:T(8,128)(2,1)}, bf16[448,448]{1,0:T(8,128)(2,1)S(1)}, u32[]{:S(2)}, u32[]{:S(2)}) collective-permute-start(bf16[448,448]{1,0:T(8,128)(2,1)} %get-tuple-element.19), channel_id=1, source_target_pairs={{0,2},{1,3},{2,0},{3,1},{4,6},{5,7},{6,4},{7,5},{8,10},{9,11},{10,... | collective-permute-start | bytes 1204232 | tf_op jit(solution)/shard_map/ppermute | solution.py:24
  223.2 14.4 %shard_map.77 = (bf16[448,448]{1,0:T(8,128)(2,1)}, f32[448,448]{1,0:T(8,128)}) custom-call(s32[197]{0:T(256)} %concatenate.39.sched, f32[64]{0:T(128)} %get-tuple-element.22.weights, bf16[32,400,128]{2,1,0:T(8,128)(2,1)} %copy-done.1, bf16[4,1568,128]{2,1,0:T(8,128)(2,1)} %copy-done, bf16[2,1568,128]{2,1,0:T(8,128)(2,1)} %collective-permute-done.6.o_1, ...), custom_call_target="tpu_custom_call" | custom-call | tf_op jit(solution)/shard_map/pallas_call | solution.py:141
  237.7 4.0 %collective-permute-done.19 = bf16[448,448]{1,0:T(8,128)(2,1)S(1)} collective-permute-done((bf16[448,448]{1,0:T(8,128)(2,1)}, bf16[448,448]{1,0:T(8,128)(2,1)S(1)}, u32[]{:S(2)}, u32[]{:S(2)}) %collective-permute-start.19) | collective-permute-done | bytes 401440 | tf_op jit(solution)/shard_map/ppermute | solution.py:24
  241.8 11.6 %collective-permute-done.20 = bf16[448,448]{1,0:T(8,128)(2,1)S(1)} collective-permute-done((bf16[448,448]{1,0:T(8,128)(2,1)}, bf16[448,448]{1,0:T(8,128)(2,1)S(1)}, u32[]{:S(2)}, u32[]{:S(2)}) %collective-permute-start.20) | collective-permute-done | bytes 401440 | tf_op jit(solution)/shard_map/ppermute | solution.py:24
  253.4 1.6 fusion.3
  254.9 1.2 copy.30
  (77 shorter events, 5.6 us)
Async XLA Ops:
  0.0 6.9 %copy-start.9 = (s32[3,64]{1,0:T(4,128)S(1)}, s32[3,64]{1,0:T(4,128)}, u32[]{:S(2)}) copy-start(s32[3,64]{1,0:T(4,128)} %param.7) | copy-start | bytes 2308
  0.0 7.0 %copy-start.10 = (s32[128]{0:T(128)S(1)}, s32[128]{0:T(128)}, u32[]{:S(2)}) copy-start(s32[128]{0:T(128)} %param.8) | copy-start | bytes 1540
  0.0 7.1 %copy-start.11 = (f32[64]{0:T(128)S(1)}, f32[64]{0:T(128)}, u32[]{:S(2)}) copy-start(f32[64]{0:T(128)} %param.9) | copy-start | bytes 772
  1.9 23.9 %copy-start.4 = (bf16[1,448,448]{1,2,0:T(8,128)(2,1)}, bf16[1,448,448]{1,2,0:T(8,128)(2,1)S(1)}, u32[]{:S(2)}) copy-start(bf16[1,448,448]{1,2,0:T(8,128)(2,1)S(1)} %copy.27) | copy-start | bytes 1204228
  3.2 22.6 %collective-permute-start.3 = (bf16[400,128]{1,0:T(8,128)(2,1)S(1)}, bf16[400,128]{1,0:T(8,128)(2,1)S(1)}, u32[]{:S(2)}, u32[]{:S(2)}) collective-permute-start(bf16[400,128]{1,0:T(8,128)(2,1)S(1)} %get-tuple-element.65), channel_id=1, source_target_pairs={{0,3},{1,0},{2,1},{3,2},{4,7},{5,4},{6,5},{7,6},{8,11},{9,8},{10,9... | collective-permute-start | bytes 307208 | tf_op jit(solution)/shard_map/ppermute | solution.py:24
  6.1 19.6 %collective-permute-start.4 = (bf16[400,128]{1,0:T(8,128)(2,1)S(1)}, bf16[400,128]{1,0:T(8,128)(2,1)S(1)}, u32[]{:S(2)}, u32[]{:S(2)}) collective-permute-start(bf16[400,128]{1,0:T(8,128)(2,1)S(1)} %get-tuple-element.64), channel_id=1, source_target_pairs={{0,2},{1,3},{2,0},{3,1},{4,6},{5,7},{6,4},{7,5},{8,10},{9,11},{10,... | collective-permute-start | bytes 307208 | tf_op jit(solution)/shard_map/ppermute | solution.py:24
  9.4 15.7 %all-to-all-start = ((s32[32,1,1]{2,1,0:T(1,128)}), s32[32,1,1]{2,1,0:T(1,128)S(1)}, u32[]{:S(2)}, u32[]{:S(2)}) async-start(s32[32,1,1]{2,1,0:T(1,128)} %copy.29), calls=%async_computation | async-start | bytes 32768 | tf_op jit(solution)/shard_map/all_to_all | solution.py:28
  17.8 8.0 %collective-permute-start.5 = (bf16[400,128]{1,0:T(8,128)(2,1)S(1)}, bf16[400,128]{1,0:T(8,128)(2,1)S(1)}, u32[]{:S(2)}, u32[]{:S(2)}) collective-permute-start(bf16[400,128]{1,0:T(8,128)(2,1)S(1)} %get-tuple-element.63), channel_id=1, source_target_pairs={{0,1},{1,2},{2,3},{3,0},{4,5},{5,6},{6,7},{7,4},{8,9},{9,10},{10,1... | collective-permute-start | bytes 307208 | tf_op jit(solution)/shard_map/ppermute | solution.py:24
  28.6 5.8 %copy-start.6 = (bf16[4,448,448]{2,1,0:T(8,128)(2,1)S(1)}, bf16[4,448,448]{2,1,0:T(8,128)(2,1)}, u32[]{:S(2)}) copy-start(bf16[4,448,448]{2,1,0:T(8,128)(2,1)} %param.13) | copy-start | bytes 4816900
  28.6 72.2 %all-to-all-start.1 = ((bf16[32,400,128]{2,1,0:T(8,128)(2,1)}), bf16[32,400,128]{2,1,0:T(8,128)(2,1)}, u32[]{:S(2)}, u32[]{:S(2)}) async-start(bf16[32,400,128]{2,1,0:T(8,128)(2,1)} %gather_fusion), calls=%async_computation.1 | async-start | bytes 6553600 | tf_op jit(solution)/shard_map/all_to_all | solution.py:239
  34.8 6.9 %copy-start.7 = (f32[1,448]{1,0:T(1,128)S(1)}, f32[1,448]{1,0:T(1,128)}, u32[]{:S(2)}) copy-start(f32[1,448]{1,0:T(1,128)} %param.11) | copy-start | bytes 5380
  35.0 42.1 %copy-start = (bf16[4,1568,128]{2,1,0:T(8,128)(2,1)}, bf16[4,1568,128]{2,1,0:T(8,128)(2,1)S(1)}, u32[]{:S(2)}) copy-start(bf16[4,1568,128]{2,1,0:T(8,128)(2,1)S(1)} %maximum_maximum_fusion.o_own) | copy-start | bytes 4816900
  36.3 21.0 %collective-permute-start.7 = (bf16[2,1568,128]{2,1,0:T(8,128)(2,1)}, bf16[2,1568,128]{2,1,0:T(8,128)(2,1)S(1)}, u32[]{:S(2)}, u32[]{:S(2)}) collective-permute-start(bf16[2,1568,128]{2,1,0:T(8,128)(2,1)} %get-tuple-element.41), channel_id=1, source_target_pairs={{0,3},{1,0},{2,1},{3,2},{4,7},{5,4},{6,5},{7,6},{8,11},{9,8},{10,9... | collective-permute-start | bytes 2408456 | tf_op jit(solution)/shard_map/ppermute | solution.py:24
  36.7 63.1 %collective-permute-start.11 = (bf16[2,1568,128]{2,1,0:T(8,128)(2,1)}, bf16[2,1568,128]{2,1,0:T(8,128)(2,1)S(1)}, u32[]{:S(2)}, u32[]{:S(2)}) collective-permute-start(bf16[2,1568,128]{2,1,0:T(8,128)(2,1)} %get-tuple-element.41), channel_id=1, source_target_pairs={{0,1},{1,2},{2,3},{3,0},{4,5},{5,6},{6,7},{7,4},{8,9},{9,10},{10,1... | collective-permute-start | bytes 2408456 | tf_op jit(solution)/shard_map/ppermute | solution.py:24
  38.4 36.8 %collective-permute-start.8 = (bf16[2,1568,128]{2,1,0:T(8,128)(2,1)}, bf16[2,1568,128]{2,1,0:T(8,128)(2,1)}, u32[]{:S(2)}, u32[]{:S(2)}) collective-permute-start(bf16[2,1568,128]{2,1,0:T(8,128)(2,1)} %get-tuple-element.42), channel_id=1, source_target_pairs={{0,1},{1,2},{2,3},{3,0},{4,5},{5,6},{6,7},{7,4},{8,9},{9,10},{10,1... | collective-permute-start | bytes 2408456 | tf_op jit(solution)/shard_map/ppermute | solution.py:24
  38.4 62.3 %collective-permute-start.6 = (bf16[2,1568,128]{2,1,0:T(8,128)(2,1)}, bf16[2,1568,128]{2,1,0:T(8,128)(2,1)}, u32[]{:S(2)}, u32[]{:S(2)}) collective-permute-start(bf16[2,1568,128]{2,1,0:T(8,128)(2,1)} %get-tuple-element.42), channel_id=1, source_target_pairs={{0,3},{1,0},{2,1},{3,2},{4,7},{5,4},{6,5},{7,6},{8,11},{9,8},{10,9... | collective-permute-start | bytes 2408456 | tf_op jit(solution)/shard_map/ppermute | solution.py:24
  41.7 35.4 %collective-permute-start.15 = (f32[1,449]{1,0:T(1,128)S(1)}, f32[1,449]{1,0:T(1,128)S(1)}, u32[]{:S(2)}, u32[]{:S(2)}) collective-permute-start(f32[1,449]{1,0:T(1,128)S(1)} %bitcast.70), channel_id=1, source_target_pairs={{0,3},{1,0},{2,1},{3,2},{4,7},{5,4},{6,5},{7,6},{8,11},{9,8},{10,9... | collective-permute-start | bytes 5396 | tf_op jit(solution)/shard_map/ppermute | solution.py:24
  57.3 43.4 %copy-start.2 = (bf16[2,1568,128]{2,1,0:T(8,128)(2,1)}, bf16[2,1568,128]{2,1,0:T(8,128)(2,1)S(1)}, u32[]{:S(2)}) copy-start(bf16[2,1568,128]{2,1,0:T(8,128)(2,1)S(1)} %collective-permute-done.7.o_2) | copy-start | bytes 2408452
  57.3 43.4 %collective-permute-start.10 = (bf16[2,1568,128]{2,1,0:T(8,128)(2,1)S(1)}, bf16[2,1568,128]{2,1,0:T(8,128)(2,1)}, u32[]{:S(2)}, u32[]{:S(2)}) collective-permute-start(bf16[2,1568,128]{2,1,0:T(8,128)(2,1)S(1)} %collective-permute-done.7.o_2), channel_id=1, source_target_pairs={{0,3},{1,0},{2,1},{3,2},{4,7},{5,4},{6,5},{7,6},{8,11},{9,8},{10,9... | collective-permute-start | bytes 2408456 | tf_op jit(solution)/shard_map/ppermute | solution.py:24
  75.1 25.6 %collective-permute-start.9 = (bf16[2,1568,128]{2,1,0:T(8,128)(2,1)}, bf16[2,1568,128]{2,1,0:T(8,128)(2,1)}, u32[]{:S(2)}, u32[]{:S(2)}) collective-permute-start(bf16[2,1568,128]{2,1,0:T(8,128)(2,1)} %collective-permute-done.8.o_5), channel_id=1, source_target_pairs={{0,1},{1,2},{2,3},{3,0},{4,5},{5,6},{6,7},{7,4},{8,9},{9,10},{10,1... | collective-permute-start | bytes 2408456 | tf_op jit(solution)/shard_map/ppermute | solution.py:24
  77.1 17.4 %collective-permute-start.16 = (f32[1,449]{1,0:T(1,128)S(1)}, f32[1,449]{1,0:T(1,128)S(1)}, u32[]{:S(2)}, u32[]{:S(2)}) collective-permute-start(f32[1,449]{1,0:T(1,128)S(1)} %bitcast.71), channel_id=1, source_target_pairs={{0,2},{1,3},{2,0},{3,1},{4,6},{5,7},{6,4},{7,5},{8,10},{9,11},{10,... | collective-permute-start | bytes 5396 | tf_op jit(solution)/shard_map/ppermute | solution.py:24
  94.5 4.8 %collective-permute-start.17 = (f32[1,449]{1,0:T(1,128)S(1)}, f32[1,449]{1,0:T(1,128)S(1)}, u32[]{:S(2)}, u32[]{:S(2)}) collective-permute-start(f32[1,449]{1,0:T(1,128)S(1)} %bitcast.72), channel_id=1, source_target_pairs={{0,1},{1,2},{2,3},{3,0},{4,5},{5,6},{6,7},{7,4},{8,9},{9,10},{10,1... | collective-permute-start | bytes 5396 | tf_op jit(solution)/shard_map/ppermute | solution.py:24
  99.3 30.7 %collective-permute-start = (bf16[400,128]{1,0:T(8,128)(2,1)}, bf16[400,128]{1,0:T(8,128)(2,1)S(1)}, u32[]{:S(2)}, u32[]{:S(2)}) collective-permute-start(bf16[400,128]{1,0:T(8,128)(2,1)} %get-tuple-element.61), channel_id=1, source_target_pairs={{0,3},{1,0},{2,1},{3,2},{4,7},{5,4},{6,5},{7,6},{8,11},{9,8},{10,9... | collective-permute-start | bytes 307208 | tf_op jit(solution)/shard_map/ppermute | solution.py:24
  99.8 1.0 copy-start.3
  99.8 32.4 %collective-permute-start.1 = (bf16[400,128]{1,0:T(8,128)(2,1)S(1)}, bf16[400,128]{1,0:T(8,128)(2,1)S(1)}, u32[]{:S(2)}, u32[]{:S(2)}) collective-permute-start(bf16[400,128]{1,0:T(8,128)(2,1)S(1)} %get-tuple-element.60), channel_id=1, source_target_pairs={{0,2},{1,3},{2,0},{3,1},{4,6},{5,7},{6,4},{7,5},{8,10},{9,11},{10,... | collective-permute-start | bytes 307208 | tf_op jit(solution)/shard_map/ppermute | solution.py:24
  124.3 18.5 %collective-permute-start.12 = (bf16[4,400,128]{2,1,0:T(8,128)(2,1)}, bf16[4,400,128]{2,1,0:T(8,128)(2,1)S(1)}, u32[]{:S(2)}, u32[]{:S(2)}) collective-permute-start(bf16[4,400,128]{2,1,0:T(8,128)(2,1)} %get-tuple-element.14), channel_id=1, source_target_pairs={{0,1},{1,2},{2,3},{3,0},{4,5},{5,6},{6,7},{7,4},{8,9},{9,10},{10,1... | collective-permute-start | bytes 1228808 | tf_op jit(solution)/shard_map/ppermute | solution.py:24
  126.3 19.1 %collective-permute-start.13 = (bf16[4,400,128]{2,1,0:T(8,128)(2,1)}, bf16[4,400,128]{2,1,0:T(8,128)(2,1)S(1)}, u32[]{:S(2)}, u32[]{:S(2)}) collective-permute-start(bf16[4,400,128]{2,1,0:T(8,128)(2,1)} %get-tuple-element.15), channel_id=1, source_target_pairs={{0,2},{1,3},{2,0},{3,1},{4,6},{5,7},{6,4},{7,5},{8,10},{9,11},{10,... | collective-permute-start | bytes 1228808 | tf_op jit(solution)/shard_map/ppermute | solution.py:24
  130.0 15.4 %collective-permute-start.14 = (bf16[4,400,128]{2,1,0:T(8,128)(2,1)}, bf16[4,400,128]{2,1,0:T(8,128)(2,1)S(1)}, u32[]{:S(2)}, u32[]{:S(2)}) collective-permute-start(bf16[4,400,128]{2,1,0:T(8,128)(2,1)} %get-tuple-element.16), channel_id=1, source_target_pairs={{0,3},{1,0},{2,1},{3,2},{4,7},{5,4},{6,5},{7,6},{8,11},{9,8},{10,9... | collective-permute-start | bytes 1228808 | tf_op jit(solution)/shard_map/ppermute | solution.py:24
  130.0 12.7 %collective-permute-start.2 = (bf16[400,128]{1,0:T(8,128)(2,1)S(1)}, bf16[400,128]{1,0:T(8,128)(2,1)S(1)}, u32[]{:S(2)}, u32[]{:S(2)}) collective-permute-start(bf16[400,128]{1,0:T(8,128)(2,1)S(1)} %get-tuple-element.59), channel_id=1, source_target_pairs={{0,1},{1,2},{2,3},{3,0},{4,5},{5,6},{6,7},{7,4},{8,9},{9,10},{10,1... | collective-permute-start | bytes 307208 | tf_op jit(solution)/shard_map/ppermute | solution.py:24
  149.6 12.0 %copy-start.12 = (f32[64]{0:T(128)S(1)}, f32[64]{0:T(128)}, u32[]{:S(2)}) copy-start(f32[64]{0:T(128)} %param.9) | copy-start | bytes 772
  149.6 12.0 %copy-start.8 = (f32[64]{0:T(128)S(1)}, f32[64]{0:T(128)}, u32[]{:S(2)}) copy-start(f32[64]{0:T(128)} %get-tuple-element.33) | copy-start | bytes 772
  149.6 49.0 %all-to-all-start.2 = ((bf16[32,400,128]{2,1,0:T(8,128)(2,1)}), bf16[32,400,128]{2,1,0:T(8,128)(2,1)S(1)}, u32[]{:S(2)}, u32[]{:S(2)}) async-start(bf16[32,400,128]{2,1,0:T(8,128)(2,1)} %gather_fusion.1), calls=%async_computation.2 | async-start | bytes 6553600 | tf_op jit(solution)/shard_map/all_to_all | solution.py:239
  198.6 1.7 copy-start.1
  219.8 17.9 %collective-permute-start.18 = (bf16[448,448]{1,0:T(8,128)(2,1)}, bf16[448,448]{1,0:T(8,128)(2,1)S(1)}, u32[]{:S(2)}, u32[]{:S(2)}) collective-permute-start(bf16[448,448]{1,0:T(8,128)(2,1)} %get-tuple-element.18), channel_id=1, source_target_pairs={{0,1},{1,2},{2,3},{3,0},{4,5},{5,6},{6,7},{7,4},{8,9},{9,10},{10,1... | collective-permute-start | bytes 1204232 | tf_op jit(solution)/shard_map/ppermute | solution.py:24
  219.9 21.9 %collective-permute-start.19 = (bf16[448,448]{1,0:T(8,128)(2,1)}, bf16[448,448]{1,0:T(8,128)(2,1)S(1)}, u32[]{:S(2)}, u32[]{:S(2)}) collective-permute-start(bf16[448,448]{1,0:T(8,128)(2,1)} %get-tuple-element.19), channel_id=1, source_target_pairs={{0,2},{1,3},{2,0},{3,1},{4,6},{5,7},{6,4},{7,5},{8,10},{9,11},{10,... | collective-permute-start | bytes 1204232 | tf_op jit(solution)/shard_map/ppermute | solution.py:24
  223.2 30.1 %copy-start.5 = (bf16[1,448,448]{1,2,0:T(8,128)(2,1)S(1)}, bf16[1,448,448]{1,2,0:T(8,128)(2,1)}, u32[]{:S(2)}) copy-start(bf16[1,448,448]{1,2,0:T(8,128)(2,1)} %copy-done.4) | copy-start | bytes 1204228
  237.6 15.7 %collective-permute-start.20 = (bf16[448,448]{1,0:T(8,128)(2,1)}, bf16[448,448]{1,0:T(8,128)(2,1)S(1)}, u32[]{:S(2)}, u32[]{:S(2)}) collective-permute-start(bf16[448,448]{1,0:T(8,128)(2,1)} %get-tuple-element.20), channel_id=1, source_target_pairs={{0,3},{1,0},{2,1},{3,2},{4,7},{5,4},{6,5},{7,6},{8,11},{9,8},{10,9... | collective-permute-start | bytes 1204232 | tf_op jit(solution)/shard_map/ppermute | solution.py:24

commit v6 on v4

--- a/solution.py
+++ b/solution.py
@@ -36,54 +36,64 @@
     return jnp.concatenate(tiles, axis=-2)
 
 
-def couple_kernel(
-    slices, sched, weights, t_hbm, o_own, o_1, o_2, o_3, o_4, o_5, o_6, kept, out_1, out_2, out_3,
-    acc, t_buf, o_buf, t_tail, o_tail, even_0, even_1, odd_0, odd_1, sems,
-):
-    sources, strip, width = t_buf.shape[0], t_buf.shape[1], o_buf.shape[1]
+def couple_kernel(slices, unroll, sched, weights, t_ref, *refs):
+    if slices:
+        pieces, outs, o_buf, refs = refs[:7], refs[7:11], refs[11], refs[12:]
+        acc, t_tail, even_0, even_1, odd_0, odd_1, o_tail, sems = refs
+    else:
+        o_buf, outs, refs = refs[0], refs[1:5], refs[5:]
+        acc, t_tail, even_0, even_1, odd_0, odd_1 = refs
+    sources, strip, width = t_tail.shape[0], t_tail.shape[1], o_buf.shape[1]
     full = width // 128
-    o_lead, t_lead = o_tail.shape[1], t_tail.shape[1]
+    t_lead = t_ref.shape[1] - full * strip
     count = 2 * sources
     offset = pl.multiple_of(sched[2 * count], 16)
     lane = pl.multiple_of(sched[2 * count + 1], 128)
     member = sched[2 * count + 2]
     copies, first = [], 0
-    for piece in (o_own, o_1, o_2, o_3, o_4, o_5, o_6):
-        size = piece.shape[0]
-        into = pl.ds(first, size)
-        for t in range(full):
-            copies.append((piece.at[:, pl.ds(t * width, width), :], o_buf.at[into, :, pl.ds(128 * t, 128)]))
-        copies.append((piece.at[:, pl.ds(full * width, o_lead), :], o_tail.at[into]))
-        first += size
-    for t in range(full):
-        copies.append((t_hbm.at[:, pl.ds(t * strip, strip), :], t_buf.at[:, :, pl.ds(128 * t, 128)]))
-    copies.append((t_hbm.at[:, pl.ds(full * strip, t_lead), :], t_tail))
-    copies = [pltpu.make_async_copy(src, dst, sems.at[i]) for i, (src, dst) in enumerate(copies)]
-    for copy in copies:
-        copy.start()
+    if slices:
+        o_lead = o_tail.shape[1]
+        for piece in pieces:
+            size = piece.shape[0]
+            into = pl.ds(first, size)
+            for t in range(full):
+                copies.append((piece.at[:, pl.ds(t * width, width), :], o_buf.at[into, :, pl.ds(128 * t, 128)]))
+            copies.append((piece.at[:, pl.ds(full * width, o_lead), :], o_tail.at[into]))
+            first += size
+        copies = [pltpu.make_async_copy(src, dst, sems.at[i]) for i, (src, dst) in enumerate(copies)]
+        for copy in copies:
+            copy.start()
     for ref in (acc, even_0, even_1, odd_0, odd_1):
         ref[...] = jnp.zeros_like(ref)
+
+    def halves(both):
+        empty = jnp.zeros((both.shape[0], 64), both.dtype)
+        return jnp.concatenate([both[:, :64], empty], axis=1), jnp.concatenate([both[:, 64:], empty], axis=1)
+
+    def unpack_t(h, carry):
+        low, high = halves(t_ref[h, full * strip :, :])
+        t_tail[h, 0:t_lead, :] = low
+        t_tail[h, strip - t_lead :, :] = high
+        return carry
+
+    lax.fori_loop(0, sources, unpack_t, 0)
     for copy in copies:
         copy.wait()
-
-    def unpack(tail, buf, index, lead):
-        both = tail[index]
-        empty = jnp.zeros((lead, 64), both.dtype)
-        rows = buf.shape[1]
-        buf[index, 0:lead, 128 * full :] = jnp.concatenate([both[:, :64], empty], axis=1)
-        buf[index, rows - lead : rows, 128 * full :] = jnp.concatenate([both[:, 64:], empty], axis=1)
-
-    def unpack_o(i, carry):
-        unpack(o_tail, o_buf, i, o_lead)
-        unpack(t_tail, t_buf, 2 * i, t_lead)
-        unpack(t_tail, t_buf, 2 * i + 1, t_lead)
-        return carry
-
-    lax.fori_loop(0, sources // 2, unpack_o, 0)
+    if slices:
+
+        def unpack_o(i, carry):
+            low, high = halves(o_tail[i])
+            o_buf[i, 0:o_lead, 128 * full :] = low
+            o_buf[i, width - o_lead :, 128 * full :] = high
+            return carry
+
+        lax.fori_loop(0, first, unpack_o, 0)
 
     def right(h, s, ref):
+        tiles = [t_ref[h, strip * t : strip * t + strip, :] for t in range(full)] + [t_tail[h]]
         product = lax.dot_general(
-            t_buf[h], o_buf[sched[2 * h + s]], (((1,), (1,)), ((), ())), preferred_element_type=jnp.float32
+            jnp.concatenate(tiles, axis=1), o_buf[sched[2 * h + s]], (((1,), (1,)), ((), ())),
+            preferred_element_type=jnp.float32,
         )
         ref[pl.ds(offset, strip), :] = product.astype(jnp.bfloat16)
 
@@ -97,22 +107,23 @@
     right(0, 0, even_0)
     right(0, 1, even_1)
 
-    def step(i, carry):
-        h = 2 * i
-        right(h + 1, 0, odd_0)
-        left(h, 0, even_0)
-        right(h + 1, 1, odd_1)
-        left(h, 1, even_1)
-        after = jnp.minimum(h + 2, sources - 1)
-        right(after, 0, even_0)
-        left(h + 1, 0, odd_0)
-        right(after, 1, even_1)
-        left(h + 1, 1, odd_1)
+    def turn(i, carry):
+        for u in range(unroll):
+            h = 2 * (unroll * i + u)
+            right(h + 1, 0, odd_0)
+            left(h, 0, even_0)
+            right(h + 1, 1, odd_1)
+            left(h, 1, even_1)
+            after = jnp.minimum(h + 2, sources - 1)
+            right(after, 0, even_0)
+            left(h + 1, 0, odd_0)
+            right(after, 1, even_1)
+            left(h + 1, 1, odd_1)
         return carry
 
-    lax.fori_loop(0, sources // 2, step, 0)
+    lax.fori_loop(0, sources // (2 * unroll), turn, 0)
     members = acc.shape[0]
-    for d, out in enumerate((kept, out_1, out_2, out_3)):
+    for d, out in enumerate(outs):
         peer = lax.rem(member + d, members)
         if slices:
             begin = pl.multiple_of(peer * strip, 16)
@@ -129,35 +140,40 @@
             out[...] = acc[peer].astype(out.dtype)
 
 
-def couple(sched, weights, strips, pieces, coup, strip, width, slices):
+def couple(sched, weights, strips, held, coup, strip, width, slices):
     sources, packed, _ = strips.shape
     full = width // 128
-    lanes = 128 * full + 128
+    total = sum(piece.shape[0] for piece in held)
     part = (coup, packed, 128) if slices else (width, width)
-    total = sum(piece.shape[0] for piece in pieces)
+    table = (total, width, 128 * full + 128)
+    resident = pl.BlockSpec(memory_space=pltpu.VMEM)
     whole = pl.BlockSpec(part, lambda i, *_: (0,) * len(part))
     half = pltpu.VMEM((256, width), jnp.bfloat16)
+    scratch = [
+        pltpu.VMEM((coup, width, width), jnp.float32),
+        pltpu.VMEM((sources, strip, 128), jnp.bfloat16),
+        half, half, half, half,
+    ]
+    shapes = [jax.ShapeDtypeStruct(part, jnp.float32)] + [jax.ShapeDtypeStruct(part, jnp.bfloat16)] * 3
+    if slices:
+        scratch += [
+            pltpu.VMEM((total, width // 2, 128), jnp.bfloat16),
+            pltpu.SemaphoreType.DMA(((full + 1) * len(held),)),
+        ]
+        shapes.append(pltpu.VMEM(table, jnp.bfloat16))
     return pl.pallas_call(
-        functools.partial(couple_kernel, slices),
-        out_shape=[jax.ShapeDtypeStruct(part, jnp.float32)] + [jax.ShapeDtypeStruct(part, jnp.bfloat16)] * 3,
+        functools.partial(couple_kernel, slices, 4),
+        out_shape=shapes,
         grid_spec=pltpu.PrefetchScalarGridSpec(
             num_scalar_prefetch=2,
             grid=(1,),
-            in_specs=[pl.BlockSpec(memory_space=pl.ANY)] * (1 + len(pieces)),
-            out_specs=[whole] * 4,
-            scratch_shapes=[
-                pltpu.VMEM((coup, width, width), jnp.float32),
-                pltpu.VMEM((sources, strip, lanes), jnp.bfloat16),
-                pltpu.VMEM((total, width, lanes), jnp.bfloat16),
-                pltpu.VMEM((sources, packed - full * strip, 128), jnp.bfloat16),
-                pltpu.VMEM((total, width // 2, 128), jnp.bfloat16),
-                half, half, half, half,
-                pltpu.SemaphoreType.DMA(((full + 1) * (len(pieces) + 1),)),
-            ],
+            in_specs=[resident] + ([pl.BlockSpec(memory_space=pl.ANY)] * len(held) if slices else [resident]),
+            out_specs=[whole] * 4 + ([resident] if slices else []),
+            scratch_shapes=scratch,
         ),
-        compiler_params=pltpu.CompilerParams(vmem_limit_bytes=60 * 2**20),
+        compiler_params=pltpu.CompilerParams(vmem_limit_bytes=32 * 2**20),
         name="couple_strips" if slices else "couple_pairs",
-    )(sched, weights, strips, *pieces)
+    )(sched, weights, strips, *held)
 
 
 def sum_parts(kept, parts):
@@ -227,8 +243,13 @@
     for iteration in range(ITERS):
         outgoing = rounded.at[wanted].get(mode="promise_in_bounds")
         arrived = lax.all_to_all(outgoing, PAIRS, 0, 0, tiled=True)
+        arrived = pltpu.with_memory_space_constraint(arrived, pltpu.VMEM)
         last = iteration == ITERS - 1
-        kept, *parts = couple(sched, weights, arrived, pieces, coup, strip, width, not last)
+        if iteration == 0:
+            kept, *parts, table = couple(sched, weights, arrived, pieces, coup, strip, width, True)
+        else:
+            table = pltpu.with_memory_space_constraint(table, pltpu.VMEM)
+            kept, *parts = couple(sched, weights, arrived, (table,), coup, strip, width, False)
         coupled = sum_parts(kept, parts)
         if not last:
             amplitudes = -(integral_strips.astype(jnp.float32) + coupled) / strip_denominator

time: 252 us -> 249 us (0.988)
  local copies, waits for them, and re-layouts: 12.6 us -> 22 us
  Pallas kernels: 50.8 us -> 42.5 us
  waiting for transfers between devices: 90.5 us -> 85.9 us
    pallas_call x2, Pallas kernels: 50.8 us -> 42.5 us  [couple(): pl.pallas_call(functools.partial(couple_kernel, slices, 4), out_shape=sha...]
    unnamed x15 -> x19, local copies, waits for them, and re-layouts: 1.24 us -> 7.25 us
    ppermute x21, waiting for transfers between devices: 84.2 us -> 79.5 us  [shift(): lax.ppermute(x, 'coup', [(i, (i + step) % peers) for i in range(peers)])]
  transfers between devices with their start and end apart: 23 -> 23, of which waited for: 10 -> 10; matrix products, arithmetic and copies ran while one was open for 3% -> 5% of each run, Pallas kernels for 10% -> 9%
where the time goes in v6:
time: 249 us; the launch traced here: 248 us
  waiting for transfers between devices  85.9 us (34%)
  blocking collectives  48.9 us (20%)
  Pallas kernels  42.5 us (17%)
  starting transfers between devices  40.9 us (16%)
  local copies, waits for them, and re-layouts  22 us (9%)
  other arithmetic  7.07 us (3%)
    ppermute x21, waiting for transfers between devices, shift(): lax.ppermute(x, 'coup', [(i, (i + step) % peers) for i in range(peers)])  79.5 us
    all_to_all x1, blocking collectives, amplitudes_of(): arrived = lax.all_to_all(outgoing, PAIRS, 0, 0, tiled=True)  48.9 us
    pallas_call x2, Pallas kernels, couple(): pl.pallas_call(functools.partial(couple_kernel, slices, 4), out_shape=sha...  42.5 us
    ppermute x21, starting transfers between devices, shift(): lax.ppermute(x, 'coup', [(i, (i + step) % peers) for i in range(peers)])  26.9 us
    all_to_all x1, starting transfers between devices, exchange_wanted(): lax.all_to_all(wanted_here[:, None, None], PAIRS, 0, 0, tiled=True)[:, 0, 0]  8.33 us
    unnamed x19, local copies, waits for them, and re-layouts  7.25 us
    all_to_all x1, waiting for transfers between devices, exchange_wanted(): lax.all_to_all(wanted_here[:, None, None], PAIRS, 0, 0, tiled=True)[:, 0, 0]  6.36 us
    all_to_all x1, starting transfers between devices, amplitudes_of(): arrived = lax.all_to_all(outgoing, PAIRS, 0, 0, tiled=True)  5.76 us
  transfers between devices with their start and end apart: 23, of which 10 were waited for; matrix products, arithmetic and copies ran while one was open for 5% of the time, Pallas kernels for 9%

profile of v6, /device:TPU:0, one launch (start us, length us, event | category | flops | bytes accessed | tf_op | source)
XLA Modules:
  0.0 248.4 jit_solution(10996330346403894819)
XLA Ops:
  0.7 1.2 copy.27
  1.9 1.0 fusion.1
  3.2 2.9 %collective-permute-start.3 = (bf16[400,128]{1,0:T(8,128)(2,1)S(1)}, bf16[400,128]{1,0:T(8,128)(2,1)S(1)}, u32[]{:S(2)}, u32[]{:S(2)}) collective-permute-start(bf16[400,128]{1,0:T(8,128)(2,1)S(1)} %get-tuple-element.56), channel_id=1, source_target_pairs={{0,3},{1,0},{2,1},{3,2},{4,7},{5,4},{6,5},{7,6},{8,11},{9,8},{10,9... | collective-permute-start | bytes 307208 | tf_op jit(solution)/shard_map/ppermute | solution.py:24
  6.1 0.8 collective-permute-start.4
  7.3 0.7 copy.29
  8.0 8.3 %all-to-all-start = ((s32[32,1,1]{2,1,0:T(1,128)}), s32[32,1,1]{2,1,0:T(1,128)S(1)}, u32[]{:S(2)}, u32[]{:S(2)}) async-start(s32[32,1,1]{2,1,0:T(1,128)} %copy.29), calls=%async_computation | async-start | bytes 32768 | tf_op jit(solution)/shard_map/all_to_all | solution.py:28
  16.3 1.0 collective-permute-start.5
  17.3 6.4 %all-to-all-done = s32[32,1,1]{2,1,0:T(1,128)S(1)} async-done(((s32[32,1,1]{2,1,0:T(1,128)}), s32[32,1,1]{2,1,0:T(1,128)S(1)}, u32[]{:S(2)}, u32[]{:S(2)}) %all-to-all-start) | async-done | bytes 160 | tf_op jit(solution)/shard_map/all_to_all | solution.py:28
  23.6 0.7 subtract_reduce_fusion
  24.4 2.7 %gather_fusion = bf16[32,400,128]{2,1,0:T(8,128)(2,1)} fusion(bf16[4,400,128]{2,1,0:T(8,128)(2,1)S(1)} %pad_maximum_fusion, s32[1024]{0:T(1024)S(1)} %pad_clamp_fusion), kind=kCustom, calls=%fused_computation | custom fusion | bytes 6553728 | tf_op jit(solution)/shard_map/gather | solution.py:244
  27.1 5.8 %all-to-all-start.1 = ((bf16[32,400,128]{2,1,0:T(8,128)(2,1)}), bf16[32,400,128]{2,1,0:T(8,128)(2,1)}, u32[]{:S(2)}, u32[]{:S(2)}) async-start(bf16[32,400,128]{2,1,0:T(8,128)(2,1)} %gather_fusion), calls=%async_computation.1 | async-start | bytes 6553600 | tf_op jit(solution)/shard_map/all_to_all | solution.py:245
  33.5 1.3 fusion.12
  35.1 1.7 collective-permute-start.11
  36.9 3.2 %collective-permute-start.6 = (bf16[2,1568,128]{2,1,0:T(8,128)(2,1)}, bf16[2,1568,128]{2,1,0:T(8,128)(2,1)}, u32[]{:S(2)}, u32[]{:S(2)}) collective-permute-start(bf16[2,1568,128]{2,1,0:T(8,128)(2,1)} %get-tuple-element.33), channel_id=1, source_target_pairs={{0,3},{1,0},{2,1},{3,2},{4,7},{5,4},{6,5},{7,6},{8,11},{9,8},{10,9... | collective-permute-start | bytes 2408456 | tf_op jit(solution)/shard_map/ppermute | solution.py:24
  40.5 2.0 copy.28
  42.6 0.9 fusion.16
  43.6 1.0 fusion.15
  44.7 11.0 %collective-permute-done.7.refs_2_ = bf16[2,1568,128]{2,1,0:T(8,128)(2,1)S(1)} collective-permute-done((bf16[2,1568,128]{2,1,0:T(8,128)(2,1)}, bf16[2,1568,128]{2,1,0:T(8,128)(2,1)S(1)}, u32[]{:S(2)}, u32[]{:S(2)}) %collective-permute-start.7) | collective-permute-done | bytes 802848 | tf_op jit(solution)/shard_map/ppermute | solution.py:24
  55.8 1.6 collective-permute-start.10
  57.3 16.3 %collective-permute-done.8.refs_5_ = bf16[2,1568,128]{2,1,0:T(8,128)(2,1)} collective-permute-done((bf16[2,1568,128]{2,1,0:T(8,128)(2,1)}, bf16[2,1568,128]{2,1,0:T(8,128)(2,1)}, u32[]{:S(2)}, u32[]{:S(2)}) %collective-permute-start.8) | collective-permute-done | bytes 802848 | tf_op jit(solution)/shard_map/ppermute | solution.py:24
  73.6 0.5 collective-permute-start.9
  74.1 0.7 constant_dynamic-slice_fusion.2
  74.7 1.8 collective-permute-start.16
  76.6 0.6 select_reduce_fusion.1
  77.2 15.8 %collective-permute-done.16 = f32[1,449]{1,0:T(1,128)S(1)} collective-permute-done((f32[1,449]{1,0:T(1,128)S(1)}, f32[1,449]{1,0:T(1,128)S(1)}, u32[]{:S(2)}, u32[]{:S(2)}) %collective-permute-start.16) | collective-permute-done | bytes 1828 | tf_op jit(solution)/shard_map/ppermute | solution.py:24
  93.0 0.8 select_reduce_fusion.weights
  93.8 0.7 concatenate.33.sched
  94.5 3.3 %collective-permute-done.17 = f32[1,449]{1,0:T(1,128)S(1)} collective-permute-done((f32[1,449]{1,0:T(1,128)S(1)}, f32[1,449]{1,0:T(1,128)S(1)}, u32[]{:S(2)}, u32[]{:S(2)}) %collective-permute-start.17) | collective-permute-done | bytes 1828 | tf_op jit(solution)/shard_map/ppermute | solution.py:24
  98.1 1.1 add_add_fusion
  99.1 0.9 collective-permute-start.1
  100.0 23.5 %couple_strips.1 = (f32[4,400,128]{2,1,0:T(8,128)S(1)}, bf16[4,400,128]{2,1,0:T(8,128)(2,1)S(1)}, bf16[4,400,128]{2,1,0:T(8,128)(2,1)S(1)}, bf16[4,400,128]{2,1,0:T(8,128)(2,1)S(1)}, bf16[16,448,512]{2,1,0:T(8,128)(2,1)S(1)}) custom-call(s32[131]{0:T(256)S(1)} %concatenate.33.sched, f32[64]{0:T(128)S(1)} %select_reduce_fusion.weights, ...), custom_call_target="tpu_custom_call" | custom-call | tf_op jit(solution)/shard_map/couple_strips/pallas_call | solution.py:164
  123.5 2.9 %copy-done = bf16[16,448,512]{2,1,0:T(8,128)(2,1)} copy-done((bf16[16,448,512]{2,1,0:T(8,128)(2,1)}, bf16[16,448,512]{2,1,0:T(8,128)(2,1)S(1)}, u32[]{:S(2)}) %copy-start) | copy-done | bytes 7340056
  126.5 1.2 collective-permute-start.12
  127.6 4.4 %collective-permute-start.13 = (bf16[4,400,128]{2,1,0:T(8,128)(2,1)S(1)}, bf16[4,400,128]{2,1,0:T(8,128)(2,1)S(1)}, u32[]{:S(2)}, u32[]{:S(2)}) collective-permute-start(bf16[4,400,128]{2,1,0:T(8,128)(2,1)S(1)} %get-tuple-element.16), channel_id=1, source_target_pairs={{0,2},{1,3},{2,0},{3,1},{4,6},{5,7},{6,4},{7,5},{8,10},{9,11},{10,... | collective-permute-start | bytes 1228808 | tf_op jit(solution)/shard_map/ppermute | solution.py:24
  132.1 2.1 collective-permute-start.2
  134.2 9.6 %collective-permute-done.2 = bf16[400,128]{1,0:T(8,128)(2,1)S(1)} collective-permute-done((bf16[400,128]{1,0:T(8,128)(2,1)S(1)}, bf16[400,128]{1,0:T(8,128)(2,1)S(1)}, u32[]{:S(2)}, u32[]{:S(2)}) %collective-permute-start.2) | collective-permute-done | bytes 102432 | tf_op jit(solution)/shard_map/ppermute | solution.py:24
  143.8 3.5 %collective-permute-done.13 = bf16[4,400,128]{2,1,0:T(8,128)(2,1)S(1)} collective-permute-done((bf16[4,400,128]{2,1,0:T(8,128)(2,1)S(1)}, bf16[4,400,128]{2,1,0:T(8,128)(2,1)S(1)}, u32[]{:S(2)}, u32[]{:S(2)}) %collective-permute-start.13) | collective-permute-done | bytes 409632 | tf_op jit(solution)/shard_map/ppermute | solution.py:24
  147.3 1.3 fusion.4
  148.6 2.8 %gather_fusion.1 = bf16[32,400,128]{2,1,0:T(8,128)(2,1)} fusion(bf16[4,400,128]{2,1,0:T(8,128)(2,1)S(1)} %fusion.4, s32[1024]{0:T(1024)S(1)} %pad_clamp_fusion), kind=kCustom, calls=%fused_computation.1 | custom fusion | bytes 6553728 | tf_op jit(solution)/shard_map/gather | solution.py:244
  151.3 48.9 %all_to_all.15.t_ref = bf16[32,400,128]{2,1,0:T(8,128)(2,1)S(1)} all-to-all(bf16[32,400,128]{2,1,0:T(8,128)(2,1)} %gather_fusion.1), channel_id=1, replica_groups=mesh['pairs_0'=4,'pairs_1'=4,'pairs_2'=2,'coup'=4] {'pairs_0','pairs_1',..., dimensions={0} | all-to-all | bytes 6553600 | tf_op jit(solution)/shard_map/all_to_all | solution.py:245
  200.3 3.1 %copy-done.1 = bf16[16,448,512]{2,1,0:T(8,128)(2,1)S(1)} copy-done((bf16[16,448,512]{2,1,0:T(8,128)(2,1)S(1)}, bf16[16,448,512]{2,1,0:T(8,128)(2,1)}, u32[]{:S(2)}) %copy-start.1) | copy-done | bytes 7340056
  203.4 19.1 %couple_pairs.1 = (f32[448,448]{1,0:T(8,128)S(1)}, bf16[448,448]{1,0:T(8,128)(2,1)S(1)}, bf16[448,448]{1,0:T(8,128)(2,1)S(1)}, bf16[448,448]{1,0:T(8,128)(2,1)S(1)}) custom-call(s32[131]{0:T(256)S(1)} %concatenate.33.sched, f32[64]{0:T(128)S(1)} %select_reduce_fusion.weights, bf16[32,400,128]{2,1,0:T(8,128)(2,1)S(1)} %all_to_all.15.t_ref, ...), custom_call_target="tpu_custom_call" | custom-call | tf_op jit(solution)/shard_map/couple_pairs/pallas_call | solution.py:164
  222.5 3.3 %collective-permute-start.19 = (bf16[448,448]{1,0:T(8,128)(2,1)S(1)}, bf16[448,448]{1,0:T(8,128)(2,1)S(1)}, u32[]{:S(2)}, u32[]{:S(2)}) collective-permute-start(bf16[448,448]{1,0:T(8,128)(2,1)S(1)} %get-tuple-element.21), channel_id=1, source_target_pairs={{0,2},{1,3},{2,0},{3,1},{4,6},{5,7},{6,4},{7,5},{8,10},{9,11},{10,... | collective-permute-start | bytes 1204232 | tf_op jit(solution)/shard_map/ppermute | solution.py:24
  225.8 0.8 collective-permute-start.20
  226.6 10.4 %collective-permute-done.18 = bf16[448,448]{1,0:T(8,128)(2,1)S(1)} collective-permute-done((bf16[448,448]{1,0:T(8,128)(2,1)S(1)}, bf16[448,448]{1,0:T(8,128)(2,1)S(1)}, u32[]{:S(2)}, u32[]{:S(2)}) %collective-permute-start.18) | collective-permute-done | bytes 401440 | tf_op jit(solution)/shard_map/ppermute | solution.py:24
  237.0 9.2 %collective-permute-done.19 = bf16[448,448]{1,0:T(8,128)(2,1)S(1)} collective-permute-done((bf16[448,448]{1,0:T(8,128)(2,1)S(1)}, bf16[448,448]{1,0:T(8,128)(2,1)S(1)}, u32[]{:S(2)}, u32[]{:S(2)}) %collective-permute-start.19) | collective-permute-done | bytes 401440 | tf_op jit(solution)/shard_map/ppermute | solution.py:24
  246.2 0.5 collective-permute-done.20
  247.1 1.2 copy.30
  (60 shorter events, 3.3 us)
Async XLA Ops:
  0.0 6.9 %copy-start.7 = (s32[3,64]{1,0:T(4,128)S(1)}, s32[3,64]{1,0:T(4,128)}, u32[]{:S(2)}) copy-start(s32[3,64]{1,0:T(4,128)} %param.7) | copy-start | bytes 2308
  0.0 6.9 %copy-start.8 = (s32[128]{0:T(128)S(1)}, s32[128]{0:T(128)}, u32[]{:S(2)}) copy-start(s32[128]{0:T(128)} %param.8) | copy-start | bytes 1540
  1.9 22.5 %copy-start.2 = (bf16[1,448,448]{1,2,0:T(8,128)(2,1)}, bf16[1,448,448]{1,2,0:T(8,128)(2,1)S(1)}, u32[]{:S(2)}) copy-start(bf16[1,448,448]{1,2,0:T(8,128)(2,1)S(1)} %copy.27) | copy-start | bytes 1204228
  3.2 21.1 %collective-permute-start.3 = (bf16[400,128]{1,0:T(8,128)(2,1)S(1)}, bf16[400,128]{1,0:T(8,128)(2,1)S(1)}, u32[]{:S(2)}, u32[]{:S(2)}) collective-permute-start(bf16[400,128]{1,0:T(8,128)(2,1)S(1)} %get-tuple-element.56), channel_id=1, source_target_pairs={{0,3},{1,0},{2,1},{3,2},{4,7},{5,4},{6,5},{7,6},{8,11},{9,8},{10,9... | collective-permute-start | bytes 307208 | tf_op jit(solution)/shard_map/ppermute | solution.py:24
  6.1 18.2 %collective-permute-start.4 = (bf16[400,128]{1,0:T(8,128)(2,1)S(1)}, bf16[400,128]{1,0:T(8,128)(2,1)S(1)}, u32[]{:S(2)}, u32[]{:S(2)}) collective-permute-start(bf16[400,128]{1,0:T(8,128)(2,1)S(1)} %get-tuple-element.55), channel_id=1, source_target_pairs={{0,2},{1,3},{2,0},{3,1},{4,6},{5,7},{6,4},{7,5},{8,10},{9,11},{10,... | collective-permute-start | bytes 307208 | tf_op jit(solution)/shard_map/ppermute | solution.py:24
  8.0 15.7 %all-to-all-start = ((s32[32,1,1]{2,1,0:T(1,128)}), s32[32,1,1]{2,1,0:T(1,128)S(1)}, u32[]{:S(2)}, u32[]{:S(2)}) async-start(s32[32,1,1]{2,1,0:T(1,128)} %copy.29), calls=%async_computation | async-start | bytes 32768 | tf_op jit(solution)/shard_map/all_to_all | solution.py:28
  16.3 8.0 %collective-permute-start.5 = (bf16[400,128]{1,0:T(8,128)(2,1)S(1)}, bf16[400,128]{1,0:T(8,128)(2,1)S(1)}, u32[]{:S(2)}, u32[]{:S(2)}) collective-permute-start(bf16[400,128]{1,0:T(8,128)(2,1)S(1)} %get-tuple-element.54), channel_id=1, source_target_pairs={{0,1},{1,2},{2,3},{3,0},{4,5},{5,6},{6,7},{7,4},{8,9},{9,10},{10,1... | collective-permute-start | bytes 307208 | tf_op jit(solution)/shard_map/ppermute | solution.py:24
  27.1 5.8 %copy-start.5 = (bf16[4,448,448]{2,1,0:T(8,128)(2,1)S(1)}, bf16[4,448,448]{2,1,0:T(8,128)(2,1)}, u32[]{:S(2)}) copy-start(bf16[4,448,448]{2,1,0:T(8,128)(2,1)} %param.13) | copy-start | bytes 4816900
  27.1 72.9 %all-to-all-start.1 = ((bf16[32,400,128]{2,1,0:T(8,128)(2,1)}), bf16[32,400,128]{2,1,0:T(8,128)(2,1)}, u32[]{:S(2)}, u32[]{:S(2)}) async-start(bf16[32,400,128]{2,1,0:T(8,128)(2,1)} %gather_fusion), calls=%async_computation.1 | async-start | bytes 6553600 | tf_op jit(solution)/shard_map/all_to_all | solution.py:245
  33.3 6.7 %copy-start.6 = (f32[1,448]{1,0:T(1,128)S(1)}, f32[1,448]{1,0:T(1,128)}, u32[]{:S(2)}) copy-start(f32[1,448]{1,0:T(1,128)} %param.11) | copy-start | bytes 5380
  34.8 21.0 %collective-permute-start.7 = (bf16[2,1568,128]{2,1,0:T(8,128)(2,1)}, bf16[2,1568,128]{2,1,0:T(8,128)(2,1)S(1)}, u32[]{:S(2)}, u32[]{:S(2)}) collective-permute-start(bf16[2,1568,128]{2,1,0:T(8,128)(2,1)} %get-tuple-element.32), channel_id=1, source_target_pairs={{0,3},{1,0},{2,1},{3,2},{4,7},{5,4},{6,5},{7,6},{8,11},{9,8},{10,9... | collective-permute-start | bytes 2408456 | tf_op jit(solution)/shard_map/ppermute | solution.py:24
  35.1 64.0 %collective-permute-start.11 = (bf16[2,1568,128]{2,1,0:T(8,128)(2,1)}, bf16[2,1568,128]{2,1,0:T(8,128)(2,1)S(1)}, u32[]{:S(2)}, u32[]{:S(2)}) collective-permute-start(bf16[2,1568,128]{2,1,0:T(8,128)(2,1)} %get-tuple-element.32), channel_id=1, source_target_pairs={{0,1},{1,2},{2,3},{3,0},{4,5},{5,6},{6,7},{7,4},{8,9},{9,10},{10,1... | collective-permute-start | bytes 2408456 | tf_op jit(solution)/shard_map/ppermute | solution.py:24
  36.8 36.8 %collective-permute-start.8 = (bf16[2,1568,128]{2,1,0:T(8,128)(2,1)}, bf16[2,1568,128]{2,1,0:T(8,128)(2,1)}, u32[]{:S(2)}, u32[]{:S(2)}) collective-permute-start(bf16[2,1568,128]{2,1,0:T(8,128)(2,1)} %get-tuple-element.33), channel_id=1, source_target_pairs={{0,1},{1,2},{2,3},{3,0},{4,5},{5,6},{6,7},{7,4},{8,9},{9,10},{10,1... | collective-permute-start | bytes 2408456 | tf_op jit(solution)/shard_map/ppermute | solution.py:24
  36.9 63.1 %collective-permute-start.6 = (bf16[2,1568,128]{2,1,0:T(8,128)(2,1)}, bf16[2,1568,128]{2,1,0:T(8,128)(2,1)}, u32[]{:S(2)}, u32[]{:S(2)}) collective-permute-start(bf16[2,1568,128]{2,1,0:T(8,128)(2,1)} %get-tuple-element.33), channel_id=1, source_target_pairs={{0,3},{1,0},{2,1},{3,2},{4,7},{5,4},{6,5},{7,6},{8,11},{9,8},{10,9... | collective-permute-start | bytes 2408456 | tf_op jit(solution)/shard_map/ppermute | solution.py:24
  40.1 34.6 %collective-permute-start.15 = (f32[1,449]{1,0:T(1,128)S(1)}, f32[1,449]{1,0:T(1,128)S(1)}, u32[]{:S(2)}, u32[]{:S(2)}) collective-permute-start(f32[1,449]{1,0:T(1,128)S(1)} %bitcast.65), channel_id=1, source_target_pairs={{0,3},{1,0},{2,1},{3,2},{4,7},{5,4},{6,5},{7,6},{8,11},{9,8},{10,9... | collective-permute-start | bytes 5396 | tf_op jit(solution)/shard_map/ppermute | solution.py:24
  55.8 44.2 %collective-permute-start.10 = (bf16[2,1568,128]{2,1,0:T(8,128)(2,1)S(1)}, bf16[2,1568,128]{2,1,0:T(8,128)(2,1)}, u32[]{:S(2)}, u32[]{:S(2)}) collective-permute-start(bf16[2,1568,128]{2,1,0:T(8,128)(2,1)S(1)} %collective-permute-done.7.refs_2_), channel_id=1, source_target_pairs={{0,3},{1,0},{2,1},{3,2},{4,7},{5,4},{6,5},{7,6},{8,11},{9,8},{10,9... | collective-permute-start | bytes 2408456 | tf_op jit(solution)/shard_map/ppermute | solution.py:24
  73.6 26.4 %collective-permute-start.9 = (bf16[2,1568,128]{2,1,0:T(8,128)(2,1)}, bf16[2,1568,128]{2,1,0:T(8,128)(2,1)}, u32[]{:S(2)}, u32[]{:S(2)}) collective-permute-start(bf16[2,1568,128]{2,1,0:T(8,128)(2,1)} %collective-permute-done.8.refs_5_), channel_id=1, source_target_pairs={{0,1},{1,2},{2,3},{3,0},{4,5},{5,6},{6,7},{7,4},{8,9},{9,10},{10,1... | collective-permute-start | bytes 2408456 | tf_op jit(solution)/shard_map/ppermute | solution.py:24
  74.7 18.2 %collective-permute-start.16 = (f32[1,449]{1,0:T(1,128)S(1)}, f32[1,449]{1,0:T(1,128)S(1)}, u32[]{:S(2)}, u32[]{:S(2)}) collective-permute-start(f32[1,449]{1,0:T(1,128)S(1)} %bitcast.66), channel_id=1, source_target_pairs={{0,2},{1,3},{2,0},{3,1},{4,6},{5,7},{6,4},{7,5},{8,10},{9,11},{10,... | collective-permute-start | bytes 5396 | tf_op jit(solution)/shard_map/ppermute | solution.py:24
  93.0 4.8 %collective-permute-start.17 = (f32[1,449]{1,0:T(1,128)S(1)}, f32[1,449]{1,0:T(1,128)S(1)}, u32[]{:S(2)}, u32[]{:S(2)}) collective-permute-start(f32[1,449]{1,0:T(1,128)S(1)} %bitcast.67), channel_id=1, source_target_pairs={{0,1},{1,2},{2,3},{3,0},{4,5},{5,6},{6,7},{7,4},{8,9},{9,10},{10,1... | collective-permute-start | bytes 5396 | tf_op jit(solution)/shard_map/ppermute | solution.py:24
  97.8 34.3 %collective-permute-start = (bf16[400,128]{1,0:T(8,128)(2,1)}, bf16[400,128]{1,0:T(8,128)(2,1)}, u32[]{:S(2)}, u32[]{:S(2)}) collective-permute-start(bf16[400,128]{1,0:T(8,128)(2,1)} %get-tuple-element.52), channel_id=1, source_target_pairs={{0,3},{1,0},{2,1},{3,2},{4,7},{5,4},{6,5},{7,6},{8,11},{9,8},{10,9... | collective-permute-start | bytes 307208 | tf_op jit(solution)/shard_map/ppermute | solution.py:24
  99.1 35.1 %collective-permute-start.1 = (bf16[400,128]{1,0:T(8,128)(2,1)S(1)}, bf16[400,128]{1,0:T(8,128)(2,1)}, u32[]{:S(2)}, u32[]{:S(2)}) collective-permute-start(bf16[400,128]{1,0:T(8,128)(2,1)S(1)} %get-tuple-element.51), channel_id=1, source_target_pairs={{0,2},{1,3},{2,0},{3,1},{4,6},{5,7},{6,4},{7,5},{8,10},{9,11},{10,... | collective-permute-start | bytes 307208 | tf_op jit(solution)/shard_map/ppermute | solution.py:24
  100.0 32.0 %copy-start.4 = (f32[4,112,448]{2,1,0:T(8,128)S(1)}, f32[4,112,448]{2,1,0:T(8,128)}, u32[]{:S(2)}) copy-start(f32[4,112,448]{2,1,0:T(8,128)} %add_add_fusion) | copy-start | bytes 2408452
  123.5 2.9 %copy-start = (bf16[16,448,512]{2,1,0:T(8,128)(2,1)}, bf16[16,448,512]{2,1,0:T(8,128)(2,1)S(1)}, u32[]{:S(2)}) copy-start(bf16[16,448,512]{2,1,0:T(8,128)(2,1)S(1)} %get-tuple-element.18.refs_0_) | copy-start | bytes 22020100
  126.5 17.4 %collective-permute-start.12 = (bf16[4,400,128]{2,1,0:T(8,128)(2,1)S(1)}, bf16[4,400,128]{2,1,0:T(8,128)(2,1)S(1)}, u32[]{:S(2)}, u32[]{:S(2)}) collective-permute-start(bf16[4,400,128]{2,1,0:T(8,128)(2,1)S(1)} %get-tuple-element.15), channel_id=1, source_target_pairs={{0,1},{1,2},{2,3},{3,0},{4,5},{5,6},{6,7},{7,4},{8,9},{9,10},{10,1... | collective-permute-start | bytes 1228808 | tf_op jit(solution)/shard_map/ppermute | solution.py:24
  127.6 19.7 %collective-permute-start.13 = (bf16[4,400,128]{2,1,0:T(8,128)(2,1)S(1)}, bf16[4,400,128]{2,1,0:T(8,128)(2,1)S(1)}, u32[]{:S(2)}, u32[]{:S(2)}) collective-permute-start(bf16[4,400,128]{2,1,0:T(8,128)(2,1)S(1)} %get-tuple-element.16), channel_id=1, source_target_pairs={{0,2},{1,3},{2,0},{3,1},{4,6},{5,7},{6,4},{7,5},{8,10},{9,11},{10,... | collective-permute-start | bytes 1228808 | tf_op jit(solution)/shard_map/ppermute | solution.py:24
  132.0 15.3 %collective-permute-start.14 = (bf16[4,400,128]{2,1,0:T(8,128)(2,1)S(1)}, bf16[4,400,128]{2,1,0:T(8,128)(2,1)S(1)}, u32[]{:S(2)}, u32[]{:S(2)}) collective-permute-start(bf16[4,400,128]{2,1,0:T(8,128)(2,1)S(1)} %get-tuple-element.17), channel_id=1, source_target_pairs={{0,3},{1,0},{2,1},{3,2},{4,7},{5,4},{6,5},{7,6},{8,11},{9,8},{10,9... | collective-permute-start | bytes 1228808 | tf_op jit(solution)/shard_map/ppermute | solution.py:24
  132.1 11.7 %collective-permute-start.2 = (bf16[400,128]{1,0:T(8,128)(2,1)S(1)}, bf16[400,128]{1,0:T(8,128)(2,1)S(1)}, u32[]{:S(2)}, u32[]{:S(2)}) collective-permute-start(bf16[400,128]{1,0:T(8,128)(2,1)S(1)} %get-tuple-element.50), channel_id=1, source_target_pairs={{0,1},{1,2},{2,3},{3,0},{4,5},{5,6},{6,7},{7,4},{8,9},{9,10},{10,1... | collective-permute-start | bytes 307208 | tf_op jit(solution)/shard_map/ppermute | solution.py:24
  200.3 3.1 %copy-start.1 = (bf16[16,448,512]{2,1,0:T(8,128)(2,1)S(1)}, bf16[16,448,512]{2,1,0:T(8,128)(2,1)}, u32[]{:S(2)}) copy-start(bf16[16,448,512]{2,1,0:T(8,128)(2,1)} %copy-done) | copy-start | bytes 22020100
  203.4 43.3 %copy-start.3 = (bf16[1,448,448]{1,2,0:T(8,128)(2,1)S(1)}, bf16[1,448,448]{1,2,0:T(8,128)(2,1)}, u32[]{:S(2)}) copy-start(bf16[1,448,448]{1,2,0:T(8,128)(2,1)} %copy-done.2) | copy-start | bytes 1204228
  222.4 14.6 %collective-permute-start.18 = (bf16[448,448]{1,0:T(8,128)(2,1)S(1)}, bf16[448,448]{1,0:T(8,128)(2,1)S(1)}, u32[]{:S(2)}, u32[]{:S(2)}) collective-permute-start(bf16[448,448]{1,0:T(8,128)(2,1)S(1)} %get-tuple-element.20), channel_id=1, source_target_pairs={{0,1},{1,2},{2,3},{3,0},{4,5},{5,6},{6,7},{7,4},{8,9},{9,10},{10,1... | collective-permute-start | bytes 1204232 | tf_op jit(solution)/shard_map/ppermute | solution.py:24
  222.5 23.7 %collective-permute-start.19 = (bf16[448,448]{1,0:T(8,128)(2,1)S(1)}, bf16[448,448]{1,0:T(8,128)(2,1)S(1)}, u32[]{:S(2)}, u32[]{:S(2)}) collective-permute-start(bf16[448,448]{1,0:T(8,128)(2,1)S(1)} %get-tuple-element.21), channel_id=1, source_target_pairs={{0,2},{1,3},{2,0},{3,1},{4,6},{5,7},{6,4},{7,5},{8,10},{9,11},{10,... | collective-permute-start | bytes 1204232 | tf_op jit(solution)/shard_map/ppermute | solution.py:24
  225.8 20.9 %collective-permute-start.20 = (bf16[448,448]{1,0:T(8,128)(2,1)S(1)}, bf16[448,448]{1,0:T(8,128)(2,1)S(1)}, u32[]{:S(2)}, u32[]{:S(2)}) collective-permute-start(bf16[448,448]{1,0:T(8,128)(2,1)S(1)} %get-tuple-element.22), channel_id=1, source_target_pairs={{0,3},{1,0},{2,1},{3,2},{4,7},{5,4},{6,5},{7,6},{8,11},{9,8},{10,9... | collective-permute-start | bytes 1204232 | tf_op jit(solution)/shard_map/ppermute | solution.py:24
